TPU v7x, 32 devices: a whole 2x2x4 slice. The times are simulated.
32 devices in a mesh: space: 8 (over y, x, core), dp: 4 (over z).
Axes of the slice: x: 2, y: 2, z: 4, core: 2. Of those that a mesh axis runs over, the one named last changes fastest.
Arguments:
- features: bfloat16 [8, 48, 72, 2048], P('dp', 'space'), may hold values from -6 to 6
- pointwise: bfloat16 [2, 2048, 256], P(None, 'dp'), may hold values from -0.125 to 0.125
- depthwise: bfloat16 [2, 9, 2048], P(None, None, 'dp'), may hold values from -2 to 2
- cotangent: bfloat16 [8, 48, 72, 512], P('dp', 'space'), may hold values from -6 to 6
Outputs:
- branches_out: bfloat16 [8, 48, 72, 512], P('dp', 'space')
- feature_grad: bfloat16 [8, 48, 72, 2048], P('dp', 'space')
- pointwise_grad: float32 [2, 2048, 256], P(None, 'dp')
- depthwise_grad: float32 [2, 9, 2048], P(None, None, 'dp')
All inputs are finite; a program needn't handle non-finite values.
Results may differ from a plain program's by a relative error of at most 0.014.
Values may be sent and summed in bfloat16 or wider, within the bound.
No kernel may reach another device: no remote copies, remote signals or barrier semaphores. Data moves between devices by JAX's collectives and lax.ppermute only.
A program may use at most 64 MiB of HBM per device.

v0:
```python
import jax
import jax.numpy as jnp
from jax import lax
from jax.sharding import PartitionSpec as P

C = 2048
CO = 256
RATE_A = 12
RATE_B = 24


def shifted(value, axis, steps):
    count = lax.axis_size(axis)
    first, last = (max(0, -steps), min(count, count - steps))
    return lax.ppermute(value, axis, [(source, source + steps) for source in range(first, last)])


def column_tap(field, rate, side):
    width = field.shape[2]
    padded = jnp.pad(field, ((0, 0), (0, 0), (rate, rate), (0, 0)))
    start = rate + side * rate
    return padded[:, :, start : start + width, :]


def row_taps(field, offset):
    return shifted(field, "space", offset)


def cot_taps(field, offset):
    return shifted(field, "space", offset)


def transposed(left, weight):
    return lax.dot_general(
        left, weight, (((1,), (1,)), ((), ())), preferred_element_type=jnp.float32
    )


def body(features, pointwise, depthwise, cotangent):
    img_count = features.shape[0]
    rows_dev = features.shape[1]
    width = features.shape[2]
    w_full, k_full = (
        lax.all_gather(pointwise, "dp", axis=1, tiled=True),
        lax.all_gather(depthwise, "dp", axis=2, tiled=True),
    )
    outputs = []
    grad_total = jnp.zeros(features.shape, jnp.float32)
    w_parts = []
    k_parts = []
    for branch, rate in enumerate((RATE_A, RATE_B)):
        offset = rate // rows_dev
        rows_near = {-1: row_taps(features, offset), 0: features, 1: row_taps(features, -offset)}
        dsum = jnp.zeros(features.shape, jnp.float32)
        for up in (-1, 0, 1):
            for side in (-1, 0, 1):
                tap = (up + 1) * 3 + (side + 1)
                dsum = dsum + column_tap(rows_near[up], rate, side).astype(jnp.float32) * k_full[
                    branch, tap
                ].astype(jnp.float32)
        dconv = dsum.astype(jnp.bfloat16)
        flat = dconv.reshape(-1, C)
        weight = w_full[branch]
        pre = jnp.dot(flat, weight, preferred_element_type=jnp.float32)
        sig = jax.nn.sigmoid(pre)
        outputs.append((pre * sig).reshape(img_count, rows_dev, width, CO).astype(jnp.bfloat16))
        cot_part = (
            cotangent[..., branch * CO : (branch + 1) * CO].reshape(-1, CO).astype(jnp.float32)
        )
        gpre = (cot_part * sig * (1.0 + pre * (1.0 - sig))).astype(jnp.bfloat16)
        gdconv = transposed(gpre, weight).astype(jnp.bfloat16).reshape(features.shape)
        w_parts.append(
            lax.dot_general(
                flat, gpre, (((0,), (0,)), ((), ())), preferred_element_type=jnp.float32
            )
        )
        gd_wide = gdconv.astype(jnp.float32)
        tap_rows = []
        for up in (-1, 0, 1):
            for side in (-1, 0, 1):
                source = column_tap(rows_near[up], rate, side).astype(jnp.float32)
                tap_rows.append(jnp.sum(source * gd_wide, axis=(0, 1, 2)))
        k_parts.append(jnp.stack(tap_rows))
        gpre_rows = gpre.reshape(img_count, rows_dev, width, CO)
        grad_near = {0: gdconv}
        for up, shift_by in ((1, offset), (-1, -offset)):
            received = cot_taps(gpre_rows, shift_by)
            grad_near[up] = (
                transposed(received.reshape(-1, CO), weight)
                .astype(jnp.bfloat16)
                .reshape(features.shape)
            )
        for up in (-1, 0, 1):
            for side in (-1, 0, 1):
                tap = (up + 1) * 3 + (side + 1)
                grad_total = grad_total + column_tap(grad_near[up], rate, -side).astype(
                    jnp.float32
                ) * k_full[branch, tap].astype(jnp.float32)
    part_w = jnp.stack(w_parts)
    part_k = jnp.stack(k_parts)
    shard_w, shard_k = (
        lax.psum_scatter(part_w.astype(jnp.bfloat16), "dp", scatter_dimension=1, tiled=True).astype(
            jnp.float32
        ),
        lax.psum_scatter(part_k.astype(jnp.bfloat16), "dp", scatter_dimension=2, tiled=True).astype(
            jnp.float32
        ),
    )
    sum_w, sum_k = lax.psum((shard_w, shard_k), "space")
    cells = lax.axis_size("dp") * img_count * lax.axis_size("space") * rows_dev * width
    factor = 1.0 / jnp.sqrt(jnp.float32(cells))
    branches_out = jnp.concatenate(outputs, axis=-1)
    return (branches_out, grad_total.astype(jnp.bfloat16), sum_w * factor, sum_k * factor)


def solution(mesh):
    return jax.shard_map(
        body,
        mesh=mesh,
        in_specs=(
            P("dp", "space", None, None),
            P(None, "dp", None),
            P(None, None, "dp"),
            P("dp", "space", None, None),
        ),
        out_specs=(
            P("dp", "space", None, None),
            P("dp", "space", None, None),
            P(None, "dp", None),
            P(None, None, "dp"),
        ),
        check_vma=False,
    )
```

profile of v0, /device:TPU:1, one launch (start us, length us, event | category | flops | bytes accessed | tf_op | source)
XLA Modules:
  0.0 381.0 jit_solution(16122468251867462227)
XLA Ops:
  7.2 0.0 all-gather.2.cloned.1.call-start
  7.2 4.2 %collective-permute-start = (bf16[2,6,72,2048]{3,2,1,0:T(8,128)(2,1)}, bf16[2,6,72,2048]{3,2,1,0:T(8,128)(2,1)S(1)}, u32[]{:S(2)}, u32[]{:S(2)}) collective-permute-start(bf16[2,6,72,2048]{3,2,1,0:T(8,128)(2,1)} %param.4), channel_id=1, source_target_pairs={{0,8},{4,12},{8,16},{12,20},{16,24},{20,28},{1,9},{5,13},{9,17},{1... | collective-permute-start | bytes 10616840 | tf_op jit(solution)/shard_map/ppermute | solution.py:15
  11.4 1.3 collective-permute-start.1
  12.7 0.0 all-gather.2.cloned.1.call-update
  12.7 0.0 reduce-scatter.5.cloned.1.call-start
  12.8 6.5 %collective-permute-start.2 = (bf16[2,6,72,2048]{3,2,1,0:T(8,128)(2,1)}, bf16[2,6,72,2048]{3,2,1,0:T(8,128)(2,1)}, u32[]{:S(2)}, u32[]{:S(2)}) collective-permute-start(bf16[2,6,72,2048]{3,2,1,0:T(8,128)(2,1)} %param.4), channel_id=1, source_target_pairs={{0,16},{4,20},{8,24},{12,28},{1,17},{5,21},{9,25},{13,29},{2,18},{... | collective-permute-start | bytes 10616840 | tf_op jit(solution)/shard_map/ppermute | solution.py:15
  19.3 1.3 collective-permute-start.3
  20.6 10.7 %all_gather.6 = bf16[2,9,2048]{2,0,1:T(2,128)(2,1)S(1)} all-gather(bf16[2,9,512]{2,0,1:T(2,128)(2,1)} %param.6), channel_id=1, replica_groups=mesh['space'=8,'dp'=4] {'dp'}, dimensions={2}, use_global_device_ids=true | all-gather | bytes 92160 | tf_op jit(solution)/shard_map/all_gather | solution.py:45
  31.3 2.1 fusion.59
  33.4 0.7 slice_convert_fusion.17
  34.2 52.5 %collective-permute-done = bf16[2,6,72,2048]{3,2,1,0:T(8,128)(2,1)S(1)} collective-permute-done((bf16[2,6,72,2048]{3,2,1,0:T(8,128)(2,1)}, bf16[2,6,72,2048]{3,2,1,0:T(8,128)(2,1)S(1)}, u32[]{:S(2)}, u32[]{:S(2)}) %collective-permute-start) | collective-permute-done | bytes 3538976 | tf_op jit(solution)/shard_map/ppermute | solution.py:15
  86.7 77.8 %collective-permute-done.1 = bf16[2,6,72,2048]{3,2,1,0:T(8,128)(2,1)} collective-permute-done((bf16[2,6,72,2048]{3,2,1,0:T(8,128)(2,1)}, bf16[2,6,72,2048]{3,2,1,0:T(8,128)(2,1)}, u32[]{:S(2)}, u32[]{:S(2)}) %collective-permute-start.1) | collective-permute-done | bytes 3538976 | tf_op jit(solution)/shard_map/ppermute | solution.py:15
  164.6 13.7 %fusion.8 = bf16[2,6,72,2048]{3,2,1,0:T(8,128)(2,1)} fusion(bf16[2,6,72,2048]{3,2,1,0:T(8,128)(2,1)S(1)} %collective-permute-done, bf16[2,6,72,2048]{3,2,1,0:T(8,128)(2,1)} %collective-permute-done.1, bf16[2,6,72,2048]{3,2,1,0:T(8,128)(2,1)} %param.4, f32[2048]{0:T(1024)S(1)} %bitcast.110, f32[2048]{0:T(1024)S(1)} %bitcast.112, f32[2048]{0:T(1024)S(1)} %bitcast.114, ...), kind=kLoop, calls=%fused_computation.46 | loop fusion | flops 47775744 | bytes 14229504 | tf_op jit(solution)/shard_map/convert_element_type | solution.py:61
  178.2 0.0 all-gather.2.cloned.1.call-done
  178.3 4.8 %fusion.56 = (bf16[864,256]{1,0:T(8,128)(2,1)}, bf16[864,256]{1,0:T(8,128)(2,1)}) fusion(bf16[2,6,72,256]{3,2,1,0:T(8,128)(2,1)} %get-tuple-element.45, bf16[864,2048]{1,0:T(8,128)(2,1)} %bitcast.82, bf16[2,2048,256]{2,1,0:T(8,128)(2,1)} %all-gather.2.cloned.1.call-done), kind=kOutput, calls=%fused_computation.132 | convolution fusion | flops 908623872 | bytes 5914624 | tf_op jit(solution)/shard_map/dot_general | solution.py:64
  183.1 1.6 collective-permute-start.4
  184.7 4.8 %collective-permute-start.5 = (bf16[2,6,72,256]{3,2,1,0:T(8,128)(2,1)}, bf16[2,6,72,256]{3,2,1,0:T(8,128)(2,1)}, u32[]{:S(2)}, u32[]{:S(2)}) collective-permute-start(bf16[2,6,72,256]{3,2,1,0:T(8,128)(2,1)} %bitcast.25), channel_id=1, source_target_pairs={{0,8},{4,12},{8,16},{12,20},{16,24},{20,28},{1,9},{5,13},{9,17},{1... | collective-permute-start | bytes 1327112 | tf_op jit(solution)/shard_map/ppermute | solution.py:15
  189.4 3.3 fusion.51
  192.9 0.0 copy-start.8
  192.9 9.9 %fusion.17 = bf16[2,6,72,2048]{3,2,1,0:T(8,128)(2,1)S(1)} fusion(bf16[2,6,72,2048]{3,2,1,0:T(8,128)(2,1)} %collective-permute-done.2, bf16[2,6,72,2048]{3,2,1,0:T(8,128)(2,1)} %collective-permute-done.3, bf16[2,6,72,2048]{3,2,1,0:T(8,128)(2,1)S(1)} %copy-done.2, f32[2048]{0:T(1024)S(1)} %bitcast.92, f32[2048]{0:T(1024)S(1)} %bitcast.94, ...), kind=kLoop, calls=%fused_computation.55 | loop fusion | flops 47775744 | bytes 14229504 | tf_op jit(solution)/shard_map/convert_element_type | solution.py:61
  202.8 2.2 fusion.54
  205.0 3.3 fusion.52
  208.4 1.3 collective-permute-start.6
  209.7 5.5 %collective-permute-start.7 = (bf16[2,6,72,256]{3,2,1,0:T(8,128)(2,1)}, bf16[2,6,72,256]{3,2,1,0:T(8,128)(2,1)}, u32[]{:S(2)}, u32[]{:S(2)}) collective-permute-start(bf16[2,6,72,256]{3,2,1,0:T(8,128)(2,1)} %bitcast.32), channel_id=1, source_target_pairs={{0,16},{4,20},{8,24},{12,28},{1,17},{5,21},{9,25},{13,29},{2,18},{... | collective-permute-start | bytes 1327112 | tf_op jit(solution)/shard_map/ppermute | solution.py:15
  215.1 2.1 convolution_convert_fusion.4
  217.3 2.3 convolution_convert_fusion.1
  219.6 19.3 %fusion.40 = (bf16[2048]{0:T(1024)(128)(2,1)S(1)}, bf16[2048]{0:T(1024)(128)(2,1)S(1)}, bf16[2048]{0:T(1024)(128)(2,1)S(1)}, bf16[2048]{0:T(1024)(128)(2,1)S(1)}...) fusion(bf16[2,6,72,2048]{3,2,1,0:T(8,128)(2,1)S(1)} %bitcast.74, ...), kind=kLoop, calls=%fused_computation.78 | loop fusion | flops 97284096 | bytes 24846336 | tf_op jit(solution)/shard_map/reduce_sum | solution.py:82
  238.9 0.6 stack.107
  239.5 0.6 stack.108
  240.1 0.6 stack.109
  240.7 0.6 stack.110
  241.3 0.6 stack.111
  241.9 0.6 stack.112
  242.5 0.6 stack.113
  243.1 0.6 stack.114
  243.7 0.6 stack.115
  244.3 0.6 stack.118
  244.9 0.6 stack.119
  245.5 0.6 stack.120
  246.1 0.6 stack.121
  246.7 0.6 stack.122
  247.4 0.6 stack.123
  247.9 0.6 stack.124
  248.5 0.6 stack.125
  249.1 0.6 stack.126
  249.8 2.8 stack.116
  252.6 2.9 stack.127
  255.4 1.5 pad_maximum_fusion.2
  257.0 0.0 reduce-scatter.5.cloned.1.call-update
  257.0 0.3 reduce-scatter.3.cloned.1.call-start
  257.3 3.1 pad_maximum_fusion
  260.3 0.0 reduce-scatter.3.cloned.1.call-update
  260.4 2.1 pad_maximum_fusion.1
  262.5 14.4 %reduce-scatter.5.cloned.1.call-done = bf16[2,9,512]{2,1,0:T(8,128)(2,1)} async-done(((bf16[2,9,2048]{2,1,0:T(8,128)(2,1)}), bf16[2,9,512]{2,1,0:T(8,128)(2,1)}) %reduce-scatter.5.cloned.1.call-update) | async-done | bytes 18448 | tf_op jit(solution)/shard_map/reduce_scatter | solution.py:105
  276.9 2.6 convolution_convert_fusion.5
  279.6 2.1 convolution_convert_fusion.3
  281.7 2.1 convolution_convert_fusion.2
  283.9 0.0 copy-start.10
  284.0 2.3 convolution_convert_fusion
  286.5 18.1 %fusion.50 = bf16[2,6,72,2048]{3,2,1,0:T(8,128)(2,1)} fusion(bf16[2,6,72,2048]{3,2,1,0:T(8,128)(2,1)S(1)} %bitcast.81, bf16[2,6,72,2048]{3,2,1,0:T(8,128)(2,1)S(1)} %bitcast.77, bf16[2,6,72,2048]{3,2,1,0:T(8,128)(2,1)S(1)} %bitcast.80, bf16[2,6,72,2048]{3,2,1,0:T(8,128)(2,1)S(1)} %bitcast.79, bf16[2,6,72,2048]{3,2,1,0:T(8,128)(2,1)S(1)} %bitcast.75, ...), kind=kLoop, calls=%fused_computation.88 | loop fusion | flops 95551488 | bytes 24920064 | tf_op jit(solution)/shard_map/convert_element_type | solution.py:113
  304.6 18.4 %reduce-scatter.3.cloned.1.call-done = bf16[2,512,256]{2,1,0:T(8,128)(2,1)} async-done(((bf16[2,2048,256]{2,1,0:T(8,128)(2,1)}), bf16[2,512,256]{2,1,0:T(8,128)(2,1)}) %reduce-scatter.3.cloned.1.call-update) | async-done | bytes 524304 | tf_op jit(solution)/shard_map/reduce_scatter | solution.py:102
  323.0 49.8 %all-reduce.14 = (f32[2,512,256]{2,1,0:T(8,128)S(1)}, f32[2,9,512]{2,1,0:T(8,128)S(1)}) all-reduce(bf16[2,512,256]{2,1,0:T(8,128)(2,1)} %reduce-scatter.3.cloned.1.call-done, bf16[2,9,512]{2,1,0:T(8,128)(2,1)} %reduce-scatter.5.cloned.1.call-done), channel_id=1, replica_groups=mesh['space'=8,'dp'=4] {'space'}, use_global_device_ids=true, to_apply=%region_1.2 | all-reduce | flops 271360 | bytes 1628160 | tf_op jit(solution)/shard_map/psum | solution.py:109
  372.8 1.1 broadcast_multiply_fusion
  373.8 0.6 copy.8
  (87 shorter events, 0.2 us)
Async XLA Ops:
  7.2 171.1 %all-gather.2.cloned.1.call-start = ((), (), s32[]{:S(2)}) async-start(), calls=%async_computation.2 | async-start | bytes 2621440 | tf_op jit(solution)/shard_map/all_gather | solution.py:44
  7.2 79.5 %collective-permute-start = (bf16[2,6,72,2048]{3,2,1,0:T(8,128)(2,1)}, bf16[2,6,72,2048]{3,2,1,0:T(8,128)(2,1)S(1)}, u32[]{:S(2)}, u32[]{:S(2)}) collective-permute-start(bf16[2,6,72,2048]{3,2,1,0:T(8,128)(2,1)} %param.4), channel_id=1, source_target_pairs={{0,8},{4,12},{8,16},{12,20},{16,24},{20,28},{1,9},{5,13},{9,17},{1... | collective-permute-start | bytes 10616840 | tf_op jit(solution)/shard_map/ppermute | solution.py:15
  11.4 153.1 %collective-permute-start.1 = (bf16[2,6,72,2048]{3,2,1,0:T(8,128)(2,1)}, bf16[2,6,72,2048]{3,2,1,0:T(8,128)(2,1)}, u32[]{:S(2)}, u32[]{:S(2)}) collective-permute-start(bf16[2,6,72,2048]{3,2,1,0:T(8,128)(2,1)} %param.4), channel_id=1, source_target_pairs={{8,0},{12,4},{16,8},{20,12},{24,16},{28,20},{9,1},{13,5},{17,9},{2... | collective-permute-start | bytes 10616840 | tf_op jit(solution)/shard_map/ppermute | solution.py:15
  12.7 264.2 %reduce-scatter.5.cloned.1.call-start = ((), (), s32[]{:S(2)}) async-start(), calls=%async_computation.4 | async-start | bytes 163840 | tf_op jit(solution)/shard_map/reduce_scatter | solution.py:105
  12.8 180.0 %collective-permute-start.2 = (bf16[2,6,72,2048]{3,2,1,0:T(8,128)(2,1)}, bf16[2,6,72,2048]{3,2,1,0:T(8,128)(2,1)}, u32[]{:S(2)}, u32[]{:S(2)}) collective-permute-start(bf16[2,6,72,2048]{3,2,1,0:T(8,128)(2,1)} %param.4), channel_id=1, source_target_pairs={{0,16},{4,20},{8,24},{12,28},{1,17},{5,21},{9,25},{13,29},{2,18},{... | collective-permute-start | bytes 10616840 | tf_op jit(solution)/shard_map/ppermute | solution.py:15
  19.3 173.5 %collective-permute-start.3 = (bf16[2,6,72,2048]{3,2,1,0:T(8,128)(2,1)}, bf16[2,6,72,2048]{3,2,1,0:T(8,128)(2,1)}, u32[]{:S(2)}, u32[]{:S(2)}) collective-permute-start(bf16[2,6,72,2048]{3,2,1,0:T(8,128)(2,1)} %param.4), channel_id=1, source_target_pairs={{16,0},{20,4},{24,8},{28,12},{17,1},{21,5},{25,9},{29,13},{18,2},{... | collective-permute-start | bytes 10616840 | tf_op jit(solution)/shard_map/ppermute | solution.py:15
  34.1 130.4 %copy-start.25 = (f32[1,1,2048]{2,0,1:T(1,128)}, f32[1,1,2048]{2,0,1:T(1,128)S(1)}, u32[]{:S(2)}) copy-start(f32[1,1,2048]{2,0,1:T(1,128)S(1)} %get-tuple-element.59) | copy-start | bytes 24580
  34.1 130.4 %copy-start.27 = (f32[1,1,2048]{2,0,1:T(1,128)}, f32[1,1,2048]{2,0,1:T(1,128)S(1)}, u32[]{:S(2)}) copy-start(f32[1,1,2048]{2,0,1:T(1,128)S(1)} %get-tuple-element.60) | copy-start | bytes 24580
  34.1 130.3 %copy-start.29 = (f32[1,1,2048]{2,0,1:T(1,128)}, f32[1,1,2048]{2,0,1:T(1,128)S(1)}, u32[]{:S(2)}) copy-start(f32[1,1,2048]{2,0,1:T(1,128)S(1)} %get-tuple-element.61) | copy-start | bytes 24580
  34.2 130.3 %copy-start.31 = (f32[1,1,2048]{2,0,1:T(1,128)}, f32[1,1,2048]{2,0,1:T(1,128)S(1)}, u32[]{:S(2)}) copy-start(f32[1,1,2048]{2,0,1:T(1,128)S(1)} %get-tuple-element.62) | copy-start | bytes 24580
  34.2 130.3 %copy-start.33 = (f32[1,1,2048]{2,0,1:T(1,128)}, f32[1,1,2048]{2,0,1:T(1,128)S(1)}, u32[]{:S(2)}) copy-start(f32[1,1,2048]{2,0,1:T(1,128)S(1)} %get-tuple-element.63) | copy-start | bytes 24580
  34.2 130.3 %copy-start.35 = (f32[1,1,2048]{2,0,1:T(1,128)}, f32[1,1,2048]{2,0,1:T(1,128)S(1)}, u32[]{:S(2)}) copy-start(f32[1,1,2048]{2,0,1:T(1,128)S(1)} %get-tuple-element.64) | copy-start | bytes 24580
  34.2 130.3 %copy-start.37 = (f32[1,1,2048]{2,0,1:T(1,128)}, f32[1,1,2048]{2,0,1:T(1,128)S(1)}, u32[]{:S(2)}) copy-start(f32[1,1,2048]{2,0,1:T(1,128)S(1)} %get-tuple-element.65) | copy-start | bytes 24580
  34.2 130.3 %copy-start.39 = (f32[1,1,2048]{2,0,1:T(1,128)}, f32[1,1,2048]{2,0,1:T(1,128)S(1)}, u32[]{:S(2)}) copy-start(f32[1,1,2048]{2,0,1:T(1,128)S(1)} %get-tuple-element.66) | copy-start | bytes 24580
  86.7 91.6 %copy-start.5 = (bf16[2,6,72,2048]{3,2,1,0:T(8,128)(2,1)}, bf16[2,6,72,2048]{3,2,1,0:T(8,128)(2,1)S(1)}, u32[]{:S(2)}) copy-start(bf16[2,6,72,2048]{3,2,1,0:T(8,128)(2,1)S(1)} %collective-permute-done) | copy-start | bytes 10616836
  178.3 11.2 %copy-start.7 = (bf16[2,6,72,2048]{3,2,1,0:T(8,128)(2,1)S(1)}, bf16[2,6,72,2048]{3,2,1,0:T(8,128)(2,1)}, u32[]{:S(2)}) copy-start(bf16[2,6,72,2048]{3,2,1,0:T(8,128)(2,1)} %fusion.8) | copy-start | bytes 10616836
  183.0 9.7 %copy-start.2 = (bf16[2,6,72,2048]{3,2,1,0:T(8,128)(2,1)S(1)}, bf16[2,6,72,2048]{3,2,1,0:T(8,128)(2,1)}, u32[]{:S(2)}) copy-start(bf16[2,6,72,2048]{3,2,1,0:T(8,128)(2,1)} %param.4) | copy-start | bytes 10616836
  183.0 9.7 %copy-start.9 = (f32[1,1,2048]{2,0,1:T(1,128)S(1)}, f32[1,1,2048]{2,0,1:T(1,128)}, u32[]{:S(2)}) copy-start(f32[1,1,2048]{2,0,1:T(1,128)} %get-tuple-element.51) | copy-start | bytes 24580
  183.1 9.7 %copy-start.11 = (f32[1,1,2048]{2,0,1:T(1,128)S(1)}, f32[1,1,2048]{2,0,1:T(1,128)}, u32[]{:S(2)}) copy-start(f32[1,1,2048]{2,0,1:T(1,128)} %get-tuple-element.52) | copy-start | bytes 24580
  183.1 9.7 %copy-start.13 = (f32[1,1,2048]{2,0,1:T(1,128)S(1)}, f32[1,1,2048]{2,0,1:T(1,128)}, u32[]{:S(2)}) copy-start(f32[1,1,2048]{2,0,1:T(1,128)} %get-tuple-element.53) | copy-start | bytes 24580
  183.1 9.7 %copy-start.15 = (f32[1,1,2048]{2,0,1:T(1,128)S(1)}, f32[1,1,2048]{2,0,1:T(1,128)}, u32[]{:S(2)}) copy-start(f32[1,1,2048]{2,0,1:T(1,128)} %get-tuple-element.54) | copy-start | bytes 24580
  183.1 9.7 %copy-start.17 = (f32[1,1,2048]{2,0,1:T(1,128)S(1)}, f32[1,1,2048]{2,0,1:T(1,128)}, u32[]{:S(2)}) copy-start(f32[1,1,2048]{2,0,1:T(1,128)} %get-tuple-element.55) | copy-start | bytes 24580
  183.1 9.7 %copy-start.19 = (f32[1,1,2048]{2,0,1:T(1,128)S(1)}, f32[1,1,2048]{2,0,1:T(1,128)}, u32[]{:S(2)}) copy-start(f32[1,1,2048]{2,0,1:T(1,128)} %get-tuple-element.56) | copy-start | bytes 24580
  183.1 9.7 %copy-start.21 = (f32[1,1,2048]{2,0,1:T(1,128)S(1)}, f32[1,1,2048]{2,0,1:T(1,128)}, u32[]{:S(2)}) copy-start(f32[1,1,2048]{2,0,1:T(1,128)} %get-tuple-element.57) | copy-start | bytes 24580
  183.1 9.7 %copy-start.23 = (f32[1,1,2048]{2,0,1:T(1,128)S(1)}, f32[1,1,2048]{2,0,1:T(1,128)}, u32[]{:S(2)}) copy-start(f32[1,1,2048]{2,0,1:T(1,128)} %get-tuple-element.58) | copy-start | bytes 24580
  183.1 93.8 %collective-permute-start.4 = (bf16[2,6,72,256]{3,2,1,0:T(8,128)(2,1)}, bf16[2,6,72,256]{3,2,1,0:T(8,128)(2,1)}, u32[]{:S(2)}, u32[]{:S(2)}) collective-permute-start(bf16[2,6,72,256]{3,2,1,0:T(8,128)(2,1)} %bitcast.25), channel_id=1, source_target_pairs={{8,0},{12,4},{16,8},{20,12},{24,16},{28,20},{9,1},{13,5},{17,9},{2... | collective-permute-start | bytes 1327112 | tf_op jit(solution)/shard_map/ppermute | solution.py:15
  184.7 94.9 %collective-permute-start.5 = (bf16[2,6,72,256]{3,2,1,0:T(8,128)(2,1)}, bf16[2,6,72,256]{3,2,1,0:T(8,128)(2,1)}, u32[]{:S(2)}, u32[]{:S(2)}) collective-permute-start(bf16[2,6,72,256]{3,2,1,0:T(8,128)(2,1)} %bitcast.25), channel_id=1, source_target_pairs={{0,8},{4,12},{8,16},{12,20},{16,24},{20,28},{1,9},{5,13},{9,17},{1... | collective-permute-start | bytes 1327112 | tf_op jit(solution)/shard_map/ppermute | solution.py:15
  192.9 9.9 %copy-start.3 = (bf16[2,2048,256]{2,1,0:T(8,128)(2,1)S(1)}, bf16[2,2048,256]{2,1,0:T(8,128)(2,1)}, u32[]{:S(2)}) copy-start(bf16[2,2048,256]{2,1,0:T(8,128)(2,1)} %all-gather.2.cloned.1.call-done) | copy-start | bytes 6291460
  192.9 9.9 %copy-start.8 = (bf16[2,6,72,256]{3,2,1,0:T(8,128)(2,1)S(1)}, bf16[2,6,72,256]{3,2,1,0:T(8,128)(2,1)}, u32[]{:S(2)}) copy-start(bf16[2,6,72,256]{3,2,1,0:T(8,128)(2,1)} %get-tuple-element.46) | copy-start | bytes 1327108
  208.4 73.3 %collective-permute-start.6 = (bf16[2,6,72,256]{3,2,1,0:T(8,128)(2,1)}, bf16[2,6,72,256]{3,2,1,0:T(8,128)(2,1)}, u32[]{:S(2)}, u32[]{:S(2)}) collective-permute-start(bf16[2,6,72,256]{3,2,1,0:T(8,128)(2,1)} %bitcast.32), channel_id=1, source_target_pairs={{16,0},{20,4},{24,8},{28,12},{17,1},{21,5},{25,9},{29,13},{18,2},{... | collective-permute-start | bytes 1327112 | tf_op jit(solution)/shard_map/ppermute | solution.py:15
  209.7 74.2 %collective-permute-start.7 = (bf16[2,6,72,256]{3,2,1,0:T(8,128)(2,1)}, bf16[2,6,72,256]{3,2,1,0:T(8,128)(2,1)}, u32[]{:S(2)}, u32[]{:S(2)}) collective-permute-start(bf16[2,6,72,256]{3,2,1,0:T(8,128)(2,1)} %bitcast.32), channel_id=1, source_target_pairs={{0,16},{4,20},{8,24},{12,28},{1,17},{5,21},{9,25},{13,29},{2,18},{... | collective-permute-start | bytes 1327112 | tf_op jit(solution)/shard_map/ppermute | solution.py:15
  217.3 2.3 copy-start.6
  219.6 19.3 %copy-start = (bf16[864,2048]{1,0:T(8,128)(2,1)}, bf16[864,2048]{1,0:T(8,128)(2,1)S(1)}, u32[]{:S(2)}) copy-start(bf16[864,2048]{1,0:T(8,128)(2,1)S(1)} %convolution_convert_fusion.1) | copy-start | bytes 10616836
  257.0 66.0 %reduce-scatter.3.cloned.1.call-start = ((), (), s32[]{:S(2)}) async-start(), calls=%async_computation.3 | async-start | bytes 2621440 | tf_op jit(solution)/shard_map/reduce_scatter | solution.py:102
  276.9 2.6 copy-start.4
  283.8 2.5 copy-start.1
  283.9 2.5 copy-start.10
  283.9 2.5 copy-start.12
  283.9 2.5 copy-start.14
  283.9 2.5 copy-start.16
  283.9 2.5 copy-start.18
  283.9 2.5 copy-start.20
  283.9 2.5 copy-start.22
  283.9 2.5 copy-start.24
  283.9 2.5 copy-start.26
  284.0 2.5 copy-start.28
  284.0 2.5 copy-start.30
  284.0 2.5 copy-start.32
  284.0 2.5 copy-start.34
  284.0 2.5 copy-start.36
  284.0 2.5 copy-start.38
  284.0 2.5 copy-start.40
Sparse Core Ops, SparseCore 0:
  12.8 50.4 all-gather.1
  257.1 19.7 reduce-scatter.4
  279.2 43.7 reduce-scatter.2
where the time goes:
time: 385 us; the launch traced here: 381 us
  waiting for transfers between devices  163 us (42%)
  other arithmetic  69.5 us (18%)
  blocking collectives  60.5 us (16%)
  matrix products  27.2 us (7%)
  starting transfers between devices  26.7 us (7%)
  local copies, waits for them, and re-layouts  19.4 us (5%)
  between operations  14.5 us (4%)
    ppermute x8, waiting for transfers between devices, shifted(): lax.ppermute(value, axis, [(source, source + steps) for source in range(f...  130 us
    psum x1, blocking collectives, body(): sum_w, sum_k = lax.psum((shard_w, shard_k), 'space')  49.8 us
    ppermute x8, starting transfers between devices, shifted(): lax.ppermute(value, axis, [(source, source + steps) for source in range(f...  26.3 us
    convert_element_type x2, other arithmetic, body(): dconv = dsum.astype(jnp.bfloat16)  23.6 us
    reduce_sum x1, other arithmetic, body(): tap_rows.append(jnp.sum(source * gd_wide, axis=(0, 1, 2)))  19.3 us
    reduce_scatter x1, waiting for transfers between devices, body(): lax.psum_scatter(part_w.astype(jnp.bfloat16), 'dp', scatter_dimension=1,...  18.4 us
    convert_element_type x1, other arithmetic, body(): grad_total.astype(jnp.bfloat16)  18.1 us
    another operation x20, local copies, waits for them, and re-layouts, body(): k_parts.append(jnp.stack(tap_rows))  16.5 us
  transfers between devices with their start and end apart: 11, of which 4 were waited for; matrix products, arithmetic and copies ran while one was open for 30% of the time, Pallas kernels for 0%

commit v1 on v0

v1 whole, which is shorter than its diff:
```python
import functools
import math

import jax
import jax.numpy as jnp
from jax import lax
from jax.experimental import pallas as pl
from jax.experimental.pallas import tpu as pltpu
from jax.sharding import PartitionSpec as P

RATES = (12, 24)
SIDES = (-1, 0, 1)
F32 = jnp.float32
BF16 = jnp.bfloat16
TAP_ROWS = 32


def shift(value, axis, steps):
    count = lax.axis_size(axis)
    first, last = max(0, -steps), min(count, count - steps)
    return lax.ppermute(value, axis, [(i, i + steps) for i in range(first, last)])


def cycle(value, axis, steps):
    count = lax.axis_size(axis)
    return lax.ppermute(value, axis, [(i, (i + steps) % count) for i in range(count)])


def swap(value, axis, mask):
    count = lax.axis_size(axis)
    return lax.ppermute(value, axis, [(i, i ^ mask) for i in range(count)])


def to_slabs(field, grain):
    n, rows, width, ch = field.shape
    parts = field.reshape(n, rows, width // grain, grain, ch)
    return parts.transpose(2, 0, 1, 3, 4).reshape(-1, ch)


def from_slabs(flat, shape, grain):
    n, rows, width, ch = shape
    parts = flat.reshape(width // grain, n, rows, grain, ch)
    return parts.transpose(1, 2, 0, 3, 4).reshape(shape)


def span(slabs, move):
    return max(0, -move), min(slabs, slabs - move)


def forward_kernel(terms, centre, slabs, idx_ref, x_ref, k_ref, w_ref, *refs):
    outs, acc = refs[: len(terms)], refs[len(terms)]
    step = pl.program_id(0)
    size = x_ref.shape[0] // slabs

    @pl.when(step == 0)
    def _():
        acc[...] = jnp.zeros_like(acc)

    for t, (branch, _, reach) in enumerate(terms):
        taps = [k_ref[0, 3 * t + i : 3 * t + i + 1, :] for i in range(3)]
        weight = w_ref[0, branch]
        pieces = []
        for q in range(slabs):
            total = None
            for i, side in enumerate(SIDES):
                src = q + side * reach
                if 0 <= src < slabs:
                    term = x_ref[src * size : (src + 1) * size, :].astype(F32) * taps[i]
                    total = term if total is None else total + term
            pieces.append(total.astype(BF16))
        field = jnp.concatenate(pieces, axis=0)
        acc[t] += jnp.dot(field, weight, preferred_element_type=F32)

    @pl.when(step == pl.num_programs(0) - 1)
    def _():
        for t in range(len(terms)):
            outs[t][...] = acc[t].astype(outs[t].dtype)


def forward(terms, slabs, idx, x, k, w):
    cells, channels = x.shape
    blocks, _, own, co = w.shape
    dtypes = [F32 if u == 0 else BF16 for _, u, _ in terms]
    return pl.pallas_call(
        functools.partial(forward_kernel, terms, None, slabs),
        grid_spec=pltpu.PrefetchScalarGridSpec(
            num_scalar_prefetch=1,
            grid=(blocks,),
            in_specs=[
                pl.BlockSpec((cells, own), lambda d, s: (0, s[3 + d])),
                pl.BlockSpec((1, k.shape[1], own), lambda d, s: (d, 0, 0)),
                pl.BlockSpec((1, 2, own, co), lambda d, s: (d, 0, 0, 0)),
            ],
            out_specs=[pl.BlockSpec((cells, co), lambda d, s: (0, 0)) for _ in terms],
            scratch_shapes=[pltpu.VMEM((len(terms), cells, co), F32)],
        ),
        out_shape=[jax.ShapeDtypeStruct((cells, co), dt) for dt in dtypes],
        compiler_params=pltpu.CompilerParams(vmem_limit_bytes=60 << 20),
        cost_estimate=pl.CostEstimate(
            flops=2 * len(terms) * cells * channels * co,
            bytes_accessed=2 * cells * channels + 2 * 2 * channels * co,
            transcendentals=0,
        ),
        name="forward_terms",
    )(idx, x, k, w)


def columns_of(terms, slabs, size, g_refs, gi):
    co = g_refs[0].shape[1]
    cells = slabs * size
    for t, (_, _, reach) in enumerate(terms):
        for i, side in enumerate(SIDES):
            lanes = slice((3 * t + i) * co, (3 * t + i + 1) * co)
            lo, hi = span(slabs, -side * reach)
            if lo > 0:
                gi[0 : lo * size, lanes] = jnp.zeros((lo * size, co), BF16)
            if hi * size < gi.shape[0]:
                gi[hi * size :, lanes] = jnp.zeros((gi.shape[0] - hi * size, co), BF16)
            a = lo - side * reach
            gi[lo * size : hi * size, lanes] = g_refs[t][a * size : (a + hi - lo) * size, :]
    del cells


def weight_kernel(terms, slabs, size, halves, quarters, last, idx_ref, xt_ref, kc_ref, w_ref, *refs):
    n = len(terms)
    g_refs = refs[:n]
    refs = refs[n:]
    if last:
        before_w, before_k, out_ref, gi, wacc, kacc = refs
    else:
        out_w, out_k, gi, wacc, kacc = refs
    own, co = w_ref.shape[2], w_ref.shape[3]

    @pl.when(pl.program_id(0) == 0)
    def _():
        columns_of(terms, slabs, size, g_refs, gi)

    if last:
        wacc[...] = before_w[0]
        kacc[...] = before_k[0]
    else:
        wacc[...] = jnp.zeros_like(wacc)
        kacc[...] = jnp.zeros_like(kacc)
    upper = idx_ref[2] > 0
    for t, (branch, u, _) in enumerate(terms):
        for i in range(3):
            col = 3 * t + i
            part = jnp.dot(
                xt_ref[...], gi[:, col * co : (col + 1) * co], preferred_element_type=F32
            )
            wacc[branch] += part * kc_ref[0, :, col : col + 1]
            total = jnp.sum(part * w_ref[0, branch].astype(F32), axis=1, keepdims=True)
            row = branch * 9 + i
            if u is None:
                kacc[:, row : row + 1] = jnp.where(upper, 0.0, total)
                kacc[:, row + 6 : row + 7] = jnp.where(upper, total, 0.0)
            else:
                at = row + 3 * (u + 1)
                kacc[:, at : at + 1] = total
    if not last:
        out_w[0] = wacc[...]
        out_k[0] = kacc[...]
        return
    taps = kacc[...].T
    part_c = own // halves
    piece = part_c // quarters
    rows = TAP_ROWS // quarters
    for h in range(halves):
        for q in range(quarters):
            at_h = h ^ idx_ref[0] if halves > 1 else 0
            at_q = q ^ idx_ref[1] if quarters > 1 else 0
            base = h * part_c + q * piece
            for branch in range(2):
                out_ref[0, at_h, at_q, branch * piece : (branch + 1) * piece, :] = wacc[
                    branch, base : base + piece, :
                ].astype(BF16)
            block = taps[q * rows : (q + 1) * rows, h * part_c : (h + 1) * part_c]
            if part_c < co:
                block = jnp.concatenate([block, jnp.zeros((rows, co - part_c), F32)], axis=1)
            out_ref[0, at_h, at_q, 2 * piece :, :] = block.astype(BF16)


def weight_grads(terms, slabs, size, halves, quarters, idx, xt, kc, w, gs, before=None):
    blocks, _, own, co = w.shape
    padded = xt.shape[1]
    last = before is not None
    in_specs = [
        pl.BlockSpec((own, padded), lambda d, s: (s[3 + d], 0)),
        pl.BlockSpec((1,) + kc.shape[1:], lambda d, s: (d, 0, 0)),
        pl.BlockSpec((1, 2, own, co), lambda d, s: (d, 0, 0, 0)),
    ] + [pl.BlockSpec(g.shape, lambda d, s: (0, 0)) for g in gs]
    args = [xt, kc, w, *gs]
    wide = [
        pl.BlockSpec((1, 2, own, co), lambda d, s: (d, 0, 0, 0)),
        pl.BlockSpec((1, own, 128), lambda d, s: (d, 0, 0)),
    ]
    if last:
        rows = (2 * (own // halves) + TAP_ROWS) // quarters
        in_specs += wide
        args += list(before)
        out_specs = pl.BlockSpec((1, halves, quarters, rows, co), lambda d, s: (d, 0, 0, 0, 0))
        out_shape = jax.ShapeDtypeStruct((blocks, halves, quarters, rows, co), BF16)
    else:
        out_specs = wide
        out_shape = [
            jax.ShapeDtypeStruct((blocks, 2, own, co), F32),
            jax.ShapeDtypeStruct((blocks, own, 128), F32),
        ]
    return pl.pallas_call(
        functools.partial(weight_kernel, terms, slabs, size, halves, quarters, last),
        grid_spec=pltpu.PrefetchScalarGridSpec(
            num_scalar_prefetch=1,
            grid=(blocks,),
            in_specs=in_specs,
            out_specs=out_specs,
            scratch_shapes=[
                pltpu.VMEM((padded, 3 * len(terms) * co), BF16),
                pltpu.VMEM((2, own, co), F32),
                pltpu.VMEM((own, 128), F32),
            ],
        ),
        out_shape=out_shape,
        compiler_params=pltpu.CompilerParams(vmem_limit_bytes=60 << 20),
        cost_estimate=pl.CostEstimate(
            flops=6 * len(terms) * padded * own * blocks * co,
            bytes_accessed=2 * own * blocks * padded + 8 * own * blocks * co,
            transcendentals=0,
        ),
        name="weight_terms_last" if last else "weight_terms",
    )(idx, *args)


def feature_kernel(terms, slabs, size, last, idx_ref, k_ref, wt_ref, *refs):
    n = len(terms)
    g_refs = refs[:n]
    refs = refs[n:]
    if last:
        before, out_ref, gi, kw = refs
    else:
        out_ref, gi, kw = refs
    co = wt_ref.shape[2]

    @pl.when(pl.program_id(0) == 0)
    def _():
        columns_of(terms, slabs, size, g_refs, gi)

    for t, (branch, _, _) in enumerate(terms):
        weight = wt_ref[0, branch].astype(F32)
        for i in range(3):
            col = 3 * t + i
            kw[col * co : (col + 1) * co, :] = (weight * k_ref[0, col : col + 1, :]).astype(BF16)

    def chunk(q, carry):
        rows = pl.ds(q * size, size)
        part = jnp.dot(gi[rows, :], kw[...], preferred_element_type=F32)
        if last:
            part = part + before[rows, :]
        out_ref[rows, :] = part.astype(out_ref.dtype)
        return carry

    lax.fori_loop(0, slabs, chunk, 0)


def feature_grads(terms, slabs, size, idx, k, wt, gs, before=None):
    blocks, _, co, own = wt.shape
    cells = slabs * size
    last = before is not None
    block = pl.BlockSpec((cells, own), lambda d, s: (0, s[3 + d]))
    in_specs = [
        pl.BlockSpec((1,) + k.shape[1:], lambda d, s: (d, 0, 0)),
        pl.BlockSpec((1, 2, co, own), lambda d, s: (d, 0, 0, 0)),
    ] + [pl.BlockSpec(g.shape, lambda d, s: (0, 0)) for g in gs]
    args = [k, wt, *gs]
    if last:
        in_specs.append(block)
        args.append(before)
    return pl.pallas_call(
        functools.partial(feature_kernel, terms, slabs, size, last),
        grid_spec=pltpu.PrefetchScalarGridSpec(
            num_scalar_prefetch=1,
            grid=(blocks,),
            in_specs=in_specs,
            out_specs=block,
            scratch_shapes=[
                pltpu.VMEM((cells, 3 * len(terms) * co), BF16),
                pltpu.VMEM((3 * len(terms) * co, own), BF16),
            ],
        ),
        out_shape=jax.ShapeDtypeStruct((cells, own * blocks), BF16 if last else F32),
        compiler_params=pltpu.CompilerParams(vmem_limit_bytes=60 << 20),
        cost_estimate=pl.CostEstimate(
            flops=6 * len(terms) * cells * own * blocks * co,
            bytes_accessed=6 * own * blocks * cells,
            transcendentals=0,
        ),
        name="feature_terms_last" if last else "feature_terms",
    )(idx, *args)


def finish_kernel(factor, idx_ref, in_ref, w_ref, k_ref):
    piece = w_ref.shape[3]
    for branch in range(2):
        rows = in_ref[0, 0, branch * piece : (branch + 1) * piece, :]
        w_ref[branch, 0, 0] = rows.astype(F32) * factor
    k_ref[...] = in_ref[0, 0, 2 * piece :, : k_ref.shape[1]].astype(F32) * factor


def finish(idx, pieces, own, factor):
    halves, quarters, rows, co = pieces.shape
    part_c = own // halves
    piece = part_c // quarters

    def place(h, q, s):
        return (h ^ s[0] if halves > 1 else h, q ^ s[1] if quarters > 1 else q, 0, 0)

    w, k = pl.pallas_call(
        functools.partial(finish_kernel, factor),
        grid_spec=pltpu.PrefetchScalarGridSpec(
            num_scalar_prefetch=1,
            grid=(halves, quarters),
            in_specs=[pl.BlockSpec((1, 1, rows, co), place)],
            out_specs=[
                pl.BlockSpec((2, 1, 1, piece, co), lambda h, q, s: (0, h, q, 0, 0)),
                pl.BlockSpec((TAP_ROWS // quarters, part_c), lambda h, q, s: (q, h)),
            ],
        ),
        out_shape=[
            jax.ShapeDtypeStruct((2, halves, quarters, piece, co), F32),
            jax.ShapeDtypeStruct((TAP_ROWS, own), F32),
        ],
        name="finish_grads",
    )(idx, pieces)
    return w.reshape(2, own, co), k[:18].reshape(2, 9, own)


def body(features, pointwise, depthwise, cotangent):
    n, rows, width, channels = features.shape
    own, co = pointwise.shape[1:]
    space, dp = lax.axis_size("space"), lax.axis_size("dp")
    me, row = lax.axis_index("space"), lax.axis_index("dp")
    chips = space // 2
    halves = 2 if space % 2 == 0 and own % 256 == 0 else 1
    part_c = own // halves
    even = chips & (chips - 1) == 0 and TAP_ROWS % (8 * chips) == 0 and part_c % (16 * chips) == 0
    quarters = chips if halves == 2 and even else 1
    core, chip = me % 2, me // 2

    grain = math.gcd(*RATES)
    slabs, size = width // grain, n * rows * grain
    cells = slabs * size

    terms, moves = [], []
    for branch, rate in enumerate(RATES):
        offset, reach = rate // rows, rate // grain
        terms.append((branch, 0, reach))
        moves.append(0)
        if 2 * offset == space:
            terms.append((branch, None, reach))
            moves.append(offset)
        elif offset < space:
            for u in (-1, 1):
                terms.append((branch, u, reach))
                moves.append(u * offset)
    middle = [t for t, m in enumerate(moves) if m == 0]
    outer = [t for t, m in enumerate(moves) if m != 0]
    half_way = next((moves[t] for t in outer if terms[t][1] is None), space)
    upper = (me >= half_way).astype(jnp.int32)

    def send(value, t, direction):
        if terms[t][1] is None:
            return cycle(value, "space", moves[t])
        return shift(value, "space", direction * moves[t])

    idx = jnp.concatenate(
        [
            jnp.stack([core, chip, upper]).astype(jnp.int32),
            (row + dp - jnp.arange(dp)).astype(jnp.int32) % dp,
        ]
    )

    taps = depthwise.reshape(18, own)
    k_all = [taps] + [cycle(taps, "dp", d) for d in range(1, dp)]
    if halves == 2:
        mine = lax.dynamic_slice_in_dim(pointwise, core * part_c, part_c, axis=1)
        mine = jnp.stack([mine] + [cycle(mine, "dp", d) for d in range(1, dp)])
        other = swap(mine, "space", 1)
        low = jnp.where(core == 0, mine, other)
        high = jnp.where(core == 0, other, mine)
        w = jnp.concatenate([low, high], axis=2)
    else:
        w = jnp.stack([pointwise] + [cycle(pointwise, "dp", d) for d in range(1, dp)])
    wt = w.transpose(0, 1, 3, 2)

    k_rows = jnp.stack(k_all).astype(F32)
    k_terms = []
    for branch, u, _ in terms:
        at = branch * 9
        if u is None:
            k_terms.append(
                jnp.where(upper > 0, k_rows[:, at + 6 : at + 9], k_rows[:, at : at + 3])
            )
        else:
            k_terms.append(k_rows[:, at + 3 * (u + 1) : at + 3 * (u + 1) + 3])

    def tap_rows(chosen):
        joined = jnp.concatenate([k_terms[t] for t in chosen], axis=1)
        return jnp.pad(joined, ((0, 0), (0, -joined.shape[1] % 8), (0, 0)))

    k_fwd = tap_rows(range(len(terms)))
    k_mid, k_out = tap_rows(middle), tap_rows(outer)
    kc_mid, kc_out = k_mid.transpose(0, 2, 1), k_out.transpose(0, 2, 1)

    x = to_slabs(features, grain)
    xt = jnp.pad(x.T, ((0, 0), (0, -cells % 128)))
    cot = to_slabs(cotangent, grain)

    parts = forward(terms, slabs, idx, x, k_fwd, w)
    received = {t: send(parts[t], t, -1) for t in outer}

    outputs, gs = [], [None] * len(terms)
    for t in middle:
        branch = terms[t][0]
        pre = parts[t]
        for o in outer:
            if terms[o][0] == branch:
                pre = pre + received[o].astype(F32)
        sig = jax.nn.sigmoid(pre)
        outputs.append((pre * sig).astype(BF16))
        cot_part = cot[:, branch * co : (branch + 1) * co].astype(F32)
        gs[t] = (cot_part * sig * (1.0 + pre * (1.0 - sig))).astype(BF16)
        for o in outer:
            if terms[o][0] == branch:
                gs[o] = send(gs[t], o, 1)
    branches_out = from_slabs(jnp.concatenate(outputs, axis=-1), cotangent.shape, grain)

    pick = lambda values, chosen: [values[t] for t in chosen]
    mid_terms, out_terms = pick(terms, middle), pick(terms, outer)
    first = weight_grads(
        mid_terms, slabs, size, halves, quarters, idx, xt, kc_mid, w, pick(gs, middle)
    )
    f_first = feature_grads(mid_terms, slabs, size, idx, k_mid, wt, pick(gs, middle))
    grads = weight_grads(
        out_terms, slabs, size, halves, quarters, idx, xt, kc_out, w, pick(gs, outer), first
    )
    f_last = feature_grads(out_terms, slabs, size, idx, k_out, wt, pick(gs, outer), f_first)
    feature_grad = from_slabs(f_last, features.shape, grain)

    factor = 1.0 / math.sqrt(dp * n * space * rows * width)
    if halves == 2:
        kept = grads[:, 0].astype(F32) + swap(grads[:, 1], "space", 1).astype(F32)
        kept = kept.astype(BF16)
    else:
        kept = grads[:, 0]
    if quarters > 1:
        total = kept[:, 0].astype(F32)
        for e in range(1, quarters):
            total = total + swap(kept[:, e], "space", 2 * e).astype(F32)
        total = total.astype(BF16)
    else:
        total = kept[:, 0]
    mine = total[0].astype(F32)
    for d in range(1, dp):
        mine = mine + cycle(total[d], "dp", -d).astype(F32)
    if quarters > 1:
        mine = mine.astype(BF16)
        block = jnp.stack([mine] + [swap(mine, "space", 2 * e) for e in range(1, quarters)])
    else:
        peers = [[i for i in range(space) if i % halves == c] for c in range(halves)]
        block = lax.psum(mine, "space", axis_index_groups=peers)[None]
    block = jnp.stack([block, swap(block, "space", 1)]) if halves == 2 else block[None]
    pointwise_grad, depthwise_grad = finish(idx, block, own, factor)
    return branches_out, feature_grad, pointwise_grad, depthwise_grad


def solution(mesh):
    return jax.shard_map(
        body,
        mesh=mesh,
        in_specs=(
            P("dp", "space", None, None),
            P(None, "dp", None),
            P(None, None, "dp"),
            P("dp", "space", None, None),
        ),
        out_specs=(
            P("dp", "space", None, None),
            P("dp", "space", None, None),
            P(None, "dp", None),
            P(None, None, "dp"),
        ),
        check_vma=False,
    )
```

time: 385 us -> 233 us (0.61)
  waiting for transfers between devices: 163 us -> 28.8 us
  Pallas kernels: 0 us -> 77.6 us
  blocking collectives: 60.5 us -> 0 us
  other arithmetic: 69.5 us -> 11.4 us
  local copies, waits for them, and re-layouts: 19.4 us -> 64.3 us
  matrix products: 27.2 us -> 0 us
  starting transfers between devices: 26.7 us -> 46.9 us
  between operations: 14.5 us -> 1.03 us
    ppermute x8 -> x24, waiting for transfers between devices: 130 us -> 28.8 us  [the longest x4 13.5 us: shift(): lax.ppermute(value, axis, [(i, i + steps) for i in range(first, last)])]
    pallas_call x0 -> x6, Pallas kernels: none -> 77.6 us  [the longest x2 31.9 us: feature_grads(): pl.pallas_call(functools.partial(feature_kernel, terms, slabs, size, last...]
    psum x1 -> x0, blocking collectives: 49.8 us -> none  [body(): sum_w, sum_k = lax.psum((shard_w, shard_k), 'space')]
    convert_element_type x4 -> x5, other arithmetic: 42.4 us -> 5.02 us  [the longest x1 3.12 us: body(): gs[t] = (cot_part * sig * (1.0 + pre * (1.0 - sig))).astype(BF16)]
    reduce_scatter x2 -> x0, waiting for transfers between devices: 32.8 us -> none  [the longest x1 18.4 us: body(): lax.psum_scatter(part_w.astype(jnp.bfloat16), 'dp', scatter_dimension=1,...]
    dot_general x10 -> x0, matrix products: 27.2 us -> none  [the longest x6 13.6 us: transposed(): lax.dot_general(left, weight, (((1,), (1,)), ((), ())), preferred_element...]
    ppermute x8 -> x24, starting transfers between devices: 26.3 us -> 46.9 us  [the longest x11 18.9 us: cycle(): lax.ppermute(value, axis, [(i, (i + steps) % count) for i in range(count)])]
    reshape x0 -> x7, local copies, waits for them, and re-layouts: none -> 19.6 us  [the longest x3 12.8 us: to_slabs(): return parts.transpose(2, 0, 1, 3, 4).reshape(-1, ch)]
  transfers between devices with their start and end apart: 11 -> 24, of which waited for: 4 -> 8; matrix products, arithmetic and copies ran while one was open for 30% -> 25% of each run, Pallas kernels for 0% -> 19%
where the time goes in v1:
time: 233 us; the launch traced here: 230 us
  Pallas kernels  77.6 us (33%)
  local copies, waits for them, and re-layouts  64.3 us (28%)
  starting transfers between devices  46.9 us (20%)
  waiting for transfers between devices  28.8 us (12%)
  other arithmetic  11.4 us (5%)
    pallas_call x2, Pallas kernels, feature_grads(): pl.pallas_call(functools.partial(feature_kernel, terms, slabs, size, last...  31.9 us
    pallas_call x2, Pallas kernels, weight_grads(): pl.pallas_call(functools.partial(weight_kernel, terms, slabs, size, halve...  27.8 us
    ppermute x11, starting transfers between devices, cycle(): lax.ppermute(value, axis, [(i, (i + steps) % count) for i in range(count)])  18.9 us
    ppermute x9, starting transfers between devices, swap(): return lax.ppermute(value, axis, [(i, i ^ mask) for i in range(count)])  16.3 us
    unnamed x32, local copies, waits for them, and re-layouts  16.3 us
    ppermute x4, waiting for transfers between devices, shift(): lax.ppermute(value, axis, [(i, i + steps) for i in range(first, last)])  13.5 us
    reshape x3, local copies, waits for them, and re-layouts, to_slabs(): return parts.transpose(2, 0, 1, 3, 4).reshape(-1, ch)  12.8 us
    pallas_call x1, Pallas kernels, forward(): pl.pallas_call(functools.partial(forward_kernel, terms, None, slabs), gri...  12.2 us
  transfers between devices with their start and end apart: 24, of which 8 were waited for; matrix products, arithmetic and copies ran while one was open for 25% of the time, Pallas kernels for 19%

profile of v1, /device:TPU:1, one launch (start us, length us, event | category | flops | bytes accessed | tf_op | source)
XLA Modules:
  0.0 230.2 jit_solution(13658000741362062375)
XLA Ops:
  0.6 0.8 copy.48
  1.4 4.2 %collective-permute-start.2 = (bf16[18,512]{1,0:T(8,128)(2,1)S(1)}, bf16[18,512]{1,0:T(8,128)(2,1)S(1)}, u32[]{:S(2)}, u32[]{:S(2)}) collective-permute-start(bf16[18,512]{1,0:T(8,128)(2,1)S(1)} %reshape.49), channel_id=1, source_target_pairs={{0,3},{1,0},{2,1},{3,2},{4,7},{5,4},{6,5},{7,6},{8,11},{9,8},{10,9... | collective-permute-start | bytes 55304 | tf_op jit(solution)/shard_map/ppermute | solution.py:26
  5.6 0.7 constant_dynamic-slice_fusion
  6.4 2.4 %collective-permute-start.4 = (bf16[2,256,256]{2,1,0:T(8,128)(2,1)}, bf16[2,256,256]{2,1,0:T(8,128)(2,1)S(1)}, u32[]{:S(2)}, u32[]{:S(2)}) collective-permute-start(bf16[2,256,256]{2,1,0:T(8,128)(2,1)} %constant_dynamic-slice_fusion), channel_id=1, source_target_pairs={{0,2},{1,3},{2,0},{3,1},{4,6},{5,7},{6,4},{7,5},{8,10},{9,11},{10,... | collective-permute-start | bytes 786440 | tf_op jit(solution)/shard_map/ppermute | solution.py:26
  8.7 3.3 %collective-permute-start.5 = (bf16[2,256,256]{2,1,0:T(8,128)(2,1)}, bf16[2,256,256]{2,1,0:T(8,128)(2,1)}, u32[]{:S(2)}, u32[]{:S(2)}) collective-permute-start(bf16[2,256,256]{2,1,0:T(8,128)(2,1)} %constant_dynamic-slice_fusion), channel_id=1, source_target_pairs={{0,3},{1,0},{2,1},{3,2},{4,7},{5,4},{6,5},{7,6},{8,11},{9,8},{10,9... | collective-permute-start | bytes 786440 | tf_op jit(solution)/shard_map/ppermute | solution.py:26
  12.1 0.6 pad_add_fusion.idx_ref
  12.8 2.1 copy.57
  15.3 5.6 %copy.46 = bf16[2,6,72,2048]{3,0,2,1:T(2,128)(2,1)S(1)} copy(bf16[2,6,72,2048]{3,2,1,0:T(8,128)(2,1)} %param.4) | data formatting | bytes 7077888 | tf_op args[0]
  21.0 4.0 %copy.47 = bf16[6,2,6,12,2048]{4,3,2,1,0:T(8,128)(2,1)} copy(bf16[6,2,6,12,2048]{4,1,3,0,2:T(2,128)(2,1)S(1)} %bitcast.69) | data formatting | bytes 7077888 | tf_op jit(solution)/shard_map/transpose | solution.py:37
  24.9 6.6 %reshape.48.x_ref = bf16[864,2048]{1,0:T(8,128)(2,1)} reshape(bf16[6,2,6,12,2048]{4,3,2,1,0:T(8,128)(2,1)} %copy.47) | data formatting | bytes 7077888 | tf_op jit(solution)/shard_map/reshape | solution.py:37
  31.5 6.0 %copy.65 = bf16[864,2048]{0,1:T(8,128)(2,1)} copy(bf16[864,2048]{1,0:T(8,128)(2,1)} %reshape.48.x_ref) | data formatting | bytes 7077888 | tf_op jit(solution)/shard_map/reshape | solution.py:37
  37.6 4.2 %pad.19.xt_ref = bf16[2048,896]{1,0:T(8,128)(2,1)} pad(bf16[2048,864]{1,0:T(8,128)(2,1)} %bitcast.67, bf16[]{:T(256)} %constant.57.clone.1), padding=0_0x0_32 | pad | bytes 7208962 | tf_op jit(solution)/shard_map/jit(_pad)/pad | solution.py:414
  42.1 1.1 pad_maximum_fusion.1
  43.2 2.1 collective-permute-start.6
  45.4 0.7 pad.16.k_ref
  46.1 1.5 collective-permute-done.6
  47.6 1.2 broadcast_select_fusion.1
  48.8 2.5 %fusion.9 = (bf16[4,2,256,512]{2,3,1,0:T(8,128)(2,1)}, bf16[4,2,512,256]{3,2,1,0:T(8,128)(2,1)}) fusion(bf16[4,2,256,256]{3,2,1,0:T(8,128)(2,1)S(1)} %get-tuple-element.41, bf16[4,2,256,256]{3,2,1,0:T(8,128)(2,1)S(1)} %get-tuple-element.40), kind=kLoop, calls=%fused_computation.53 | loop fusion | flops 4194304 | bytes 6291456 | tf_op jit(solution)/shard_map/transpose | solution.py:392
  51.3 12.2 %forward_terms.1 = (f32[864,256]{1,0:T(8,128)}, bf16[864,256]{1,0:T(8,128)(2,1)}, bf16[864,256]{1,0:T(8,128)(2,1)}, f32[864,256]{1,0:T(8,128)}, bf16[864,256]{1,0:T(8,128)(2,1)}) custom-call(s32[7]{0:T(128)} %pad_add_fusion.idx_ref, bf16[864,2048]{1,0:T(8,128)(2,1)} %reshape.48.x_ref, f32[4,16,512]{2,1,0:T(8,128)} %pad.16.k_ref, ...), custom_call_target="tpu_custom_call" | custom-call | flops 4529848320 | bytes 5636096 | tf_op jit(solution)/shard_map/forward_terms/pallas_call | solution.py:84
  63.4 3.1 %collective-permute-start.7 = (bf16[864,256]{1,0:T(8,128)(2,1)}, bf16[864,256]{1,0:T(8,128)(2,1)S(1)}, u32[]{:S(2)}, u32[]{:S(2)}) collective-permute-start(bf16[864,256]{1,0:T(8,128)(2,1)} %get-tuple-element.14), channel_id=1, source_target_pairs={{0,8},{4,12},{8,16},{12,20},{16,24},{20,28},{1,9},{5,13},{9,17},{1... | collective-permute-start | bytes 1327112 | tf_op jit(solution)/shard_map/ppermute | solution.py:21
  66.6 1.5 collective-permute-start.8
  68.0 3.1 %collective-permute-start.9 = (bf16[864,256]{1,0:T(8,128)(2,1)}, bf16[864,256]{1,0:T(8,128)(2,1)}, u32[]{:S(2)}, u32[]{:S(2)}) collective-permute-start(bf16[864,256]{1,0:T(8,128)(2,1)} %get-tuple-element.17), channel_id=1, source_target_pairs={{0,16},{4,20},{8,24},{12,28},{16,0},{20,4},{24,8},{28,12},{1,17},{... | collective-permute-start | bytes 1327112 | tf_op jit(solution)/shard_map/ppermute | solution.py:26
  71.9 1.0 pad_bitcast_fusion.1.kc_ref
  72.9 1.0 pad_bitcast_fusion.kc_ref
  74.0 2.0 collective-permute-done.7
  76.0 11.5 %collective-permute-done.8 = bf16[864,256]{1,0:T(8,128)(2,1)} collective-permute-done((bf16[864,256]{1,0:T(8,128)(2,1)}, bf16[864,256]{1,0:T(8,128)(2,1)}, u32[]{:S(2)}, u32[]{:S(2)}) %collective-permute-start.8) | collective-permute-done | bytes 442400 | tf_op jit(solution)/shard_map/ppermute | solution.py:21
  87.5 3.1 %multiply_convert_fusion = (bf16[864,256]{1,0:T(8,128)(2,1)S(1)}, bf16[864,256]{1,0:T(8,128)(2,1)S(1)}, bf16[864,256]{1,0:T(8,128)(2,1)}, bf16[864,256]{1,0:T(8,128)(2,1)}) fusion(f32[864,256]{1,0:T(8,128)S(1)} %copy-done.5, bf16[864,256]{1,0:T(8,128)(2,1)} %collective-permute-done.9, bf16[864,512]{1,0:T(8,128)(2,1)S(1)} %reshape.53, ...), kind=kLoop, calls=%fused_computation.9 | loop fusion | flops 6635520 | bytes 5750784 | tf_op jit(solution)/shard_map/convert_element_type | solution.py:430
  90.6 5.8 %collective-permute-start.11 = (bf16[864,256]{1,0:T(8,128)(2,1)}, bf16[864,256]{1,0:T(8,128)(2,1)S(1)}, u32[]{:S(2)}, u32[]{:S(2)}) collective-permute-start(bf16[864,256]{1,0:T(8,128)(2,1)} %get-tuple-element.50.refs_0_), channel_id=1, source_target_pairs={{0,8},{4,12},{8,16},{12,20},{16,24},{20,28},{1,9},{5,13},{9,17},{1... | collective-permute-start | bytes 1327112 | tf_op jit(solution)/shard_map/ppermute | solution.py:21
  96.4 1.3 collective-permute-start.10
  97.7 1.9 collective-permute-start.12
  99.5 11.6 %weight_terms.1 = (f32[4,2,512,256]{3,2,1,0:T(8,128)}, f32[4,512,128]{2,1,0:T(8,128)}) custom-call(s32[7]{0:T(128)} %pad_add_fusion.idx_ref, bf16[2048,896]{1,0:T(8,128)(2,1)} %pad.19.xt_ref, f32[4,512,8]{2,1,0:T(8,128)} %pad_bitcast_fusion.kc_ref, bf16[4,2,512,256]{3,2,1,0:T(8,128)(2,1)} %get-tuple-element.39.w_ref, ...), custom_call_target="tpu_custom_call" | custom-call | flops 5637144576 | bytes 7864320 | tf_op jit(solution)/shard_map/weight_terms/pallas_call | solution.py:209
  111.1 4.5 %collective-permute-done.12.refs_2_ = bf16[864,256]{1,0:T(8,128)(2,1)} collective-permute-done((bf16[864,256]{1,0:T(8,128)(2,1)S(1)}, bf16[864,256]{1,0:T(8,128)(2,1)}, u32[]{:S(2)}, u32[]{:S(2)}) %collective-permute-start.12) | collective-permute-done | bytes 442400 | tf_op jit(solution)/shard_map/ppermute | solution.py:26
  115.7 0.8 copy-done.8
  116.6 16.2 %weight_terms_last.1 = bf16[4,2,4,136,256]{4,3,2,1,0:T(8,128)(2,1)} custom-call(s32[7]{0:T(128)} %pad_add_fusion.idx_ref, bf16[2048,896]{1,0:T(8,128)(2,1)} %pad.19.xt_ref, f32[4,512,16]{2,1,0:T(8,128)} %pad_bitcast_fusion.1.kc_ref, bf16[4,2,512,256]{3,2,1,0:T(8,128)(2,1)} %get-tuple-element.39.w_ref, bf16[864,256]{1,0:T(8,128)(2,1)} %copy-done.9, ...), custom_call_target="tpu_custom_call" | custom-call | flops 8455716864 | bytes 7864320 | tf_op jit(solution)/shard_map/weight_terms_last/pallas_call | solution.py:209
  132.8 1.7 fusion.10
  134.6 1.4 collective-permute-start.13
  136.1 2.4 %collective-permute-done.13 = bf16[4,4,136,256]{3,2,0,1:T(8,128)(2,1)S(1)} collective-permute-done((bf16[4,4,136,256]{3,2,0,1:T(8,128)(2,1)S(1)}, bf16[4,4,136,256]{3,2,0,1:T(8,128)(2,1)S(1)}, u32[]{:S(2)}, u32[]{:S(2)}) %collective-permute-start.13) | collective-permute-done | bytes 1114144 | tf_op jit(solution)/shard_map/ppermute | solution.py:31
  138.8 1.0 copy-done.2
  139.8 0.8 slice_bitcast_fusion.2
  140.6 5.0 %collective-permute-start.14 = (bf16[4,136,256]{2,1,0:T(8,128)(2,1)}, bf16[4,136,256]{2,1,0:T(8,128)(2,1)}, u32[]{:S(2)}, u32[]{:S(2)}) collective-permute-start(bf16[4,136,256]{2,1,0:T(8,128)(2,1)} %get-tuple-element.46), channel_id=1, source_target_pairs={{0,8},{4,12},{8,0},{12,4},{16,24},{20,28},{24,16},{28,20},{1,9},{5... | collective-permute-start | bytes 835592 | tf_op jit(solution)/shard_map/ppermute | solution.py:31
  145.5 1.2 collective-permute-start.15
  147.4 0.7 pad.17.clone.k_ref
  148.1 0.6 pad.18.clone.k_ref
  148.7 4.1 %copy.63.wt_ref = bf16[4,2,256,512]{3,2,1,0:T(8,128)(2,1)} copy(bf16[4,2,256,512]{2,3,1,0:T(8,128)(2,1)} %get-tuple-element.38) | data formatting | bytes 4194304 | tf_op jit(solution)/shard_map/transpose | solution.py:392
  152.8 4.6 %collective-permute-done.16 = bf16[4,136,256]{2,1,0:T(8,128)(2,1)} collective-permute-done((bf16[4,136,256]{2,1,0:T(8,128)(2,1)S(1)}, bf16[4,136,256]{2,1,0:T(8,128)(2,1)}, u32[]{:S(2)}, u32[]{:S(2)}) %collective-permute-start.16) | collective-permute-done | bytes 278560 | tf_op jit(solution)/shard_map/ppermute | solution.py:31
  157.4 1.8 collective-permute-done.15
  159.2 1.3 fusion.3
  160.5 3.6 %collective-permute-start.17 = (bf16[136,256]{1,0:T(8,128)(2,1)S(1)}, bf16[136,256]{1,0:T(8,128)(2,1)S(1)}, u32[]{:S(2)}, u32[]{:S(2)}) collective-permute-start(bf16[136,256]{1,0:T(8,128)(2,1)S(1)} %get-tuple-element.53), channel_id=1, source_target_pairs={{0,3},{1,0},{2,1},{3,2},{4,7},{5,4},{6,5},{7,6},{8,11},{9,8},{10,9... | collective-permute-start | bytes 208904 | tf_op jit(solution)/shard_map/ppermute | solution.py:26
  164.1 0.6 collective-permute-start.18
  164.7 14.0 %feature_terms.1.refs_3_ = f32[864,2048]{1,0:T(8,128)} custom-call(s32[7]{0:T(128)} %pad_add_fusion.idx_ref, f32[4,8,512]{2,1,0:T(8,128)} %pad.18.clone.k_ref, bf16[4,2,256,512]{3,2,1,0:T(8,128)(2,1)} %copy.63.wt_ref, bf16[864,256]{1,0:T(8,128)(2,1)} %get-tuple-element.50.refs_0_, bf16[864,256]{1,0:T(8,128)(2,1)} %copy-done.6), custom_call_target="tpu_custom_call" | custom-call | flops 5435817984 | bytes 10616832 | tf_op jit(solution)/shard_map/feature_terms/pallas_call | solution.py:277
  178.7 1.5 collective-permute-start.22
  180.2 0.9 collective-permute-start.21
  181.7 0.9 copy.55
  182.7 1.1 copy.68
  183.7 0.6 collective-permute-done.20
  184.4 3.9 %collective-permute-start.23 = (bf16[4,136,256]{2,1,0:T(8,128)(2,1)S(1)}, bf16[4,136,256]{2,1,0:T(8,128)(2,1)S(1)}, u32[]{:S(2)}, u32[]{:S(2)}) collective-permute-start(bf16[4,136,256]{2,1,0:T(8,128)(2,1)S(1)} %get-tuple-element.52), channel_id=1, source_target_pairs={{0,4},{4,0},{8,12},{12,8},{16,20},{20,16},{24,28},{28,24},{1,5},{5... | collective-permute-start | bytes 835592 | tf_op jit(solution)/shard_map/ppermute | solution.py:31
  188.3 17.9 %feature_terms_last.1 = bf16[864,2048]{1,0:T(8,128)(2,1)} custom-call(s32[7]{0:T(128)} %pad_add_fusion.idx_ref, f32[4,16,512]{2,1,0:T(8,128)} %pad.17.clone.k_ref, bf16[4,2,256,512]{3,2,1,0:T(8,128)(2,1)} %copy.63.wt_ref, bf16[864,256]{1,0:T(8,128)(2,1)} %copy-done.9, bf16[864,256]{1,0:T(8,128)(2,1)} %copy-done.8, ...), custom_call_target="tpu_custom_call" | custom-call | flops 8153726976 | bytes 10616832 | tf_op jit(solution)/shard_map/feature_terms_last/pallas_call | solution.py:277
  206.1 6.5 %reshape.54 = bf16[6,2,6,12,2048]{4,3,2,1,0:T(8,128)(2,1)} reshape(bf16[864,2048]{1,0:T(8,128)(2,1)} %feature_terms_last.1) | data formatting | bytes 7077888 | tf_op jit(solution)/shard_map/reshape | solution.py:42
  212.7 6.0 %copy.64 = bf16[2,6,6,12,2048]{4,0,3,2,1:T(2,128)(2,1)S(1)} copy(bf16[2,6,6,12,2048]{4,3,1,0,2:T(8,128)(2,1)} %bitcast.66) | data formatting | bytes 7077888 | tf_op jit(solution)/shard_map/transpose | solution.py:43
  218.7 3.4 %copy.69 = bf16[2,6,72,2048]{3,2,1,0:T(8,128)(2,1)} copy(bf16[2,6,72,2048]{3,0,2,1:T(2,128)(2,1)S(1)} %bitcast.68) | data formatting | bytes 7077888
  222.1 0.9 pad_maximum_fusion.3.in_ref
  222.9 5.8 %finish_grads.1 = (f32[2,2,4,64,256]{4,3,2,1,0:T(8,128)}, f32[32,512]{1,0:T(8,128)}) custom-call(s32[7]{0:T(128)} %pad_add_fusion.idx_ref, bf16[2,4,136,256]{3,2,1,0:T(8,128)(2,1)} %pad_maximum_fusion.3.in_ref), custom_call_target="tpu_custom_call" | custom-call | tf_op jit(solution)/shard_map/finish_grads/pallas_call | solution.py:316
  228.7 0.8 slice.75
  229.5 0.6 copy.70
  (70 shorter events, 3.7 us)
Async XLA Ops:
  0.6 5.0 %copy-start = (bf16[2,512,256]{2,1,0:T(8,128)(2,1)S(1)}, bf16[2,512,256]{2,1,0:T(8,128)(2,1)}, u32[]{:S(2)}) copy-start(bf16[2,512,256]{2,1,0:T(8,128)(2,1)} %param.5) | copy-start | bytes 1572868
  1.4 10.6 %collective-permute-start.2 = (bf16[18,512]{1,0:T(8,128)(2,1)S(1)}, bf16[18,512]{1,0:T(8,128)(2,1)S(1)}, u32[]{:S(2)}, u32[]{:S(2)}) collective-permute-start(bf16[18,512]{1,0:T(8,128)(2,1)S(1)} %reshape.49), channel_id=1, source_target_pairs={{0,3},{1,0},{2,1},{3,2},{4,7},{5,4},{6,5},{7,6},{8,11},{9,8},{10,9... | collective-permute-start | bytes 55304 | tf_op jit(solution)/shard_map/ppermute | solution.py:26
  5.6 36.1 %collective-permute-start.1 = (bf16[18,512]{1,0:T(8,128)(2,1)S(1)}, bf16[18,512]{1,0:T(8,128)(2,1)S(1)}, u32[]{:S(2)}, u32[]{:S(2)}) collective-permute-start(bf16[18,512]{1,0:T(8,128)(2,1)S(1)} %reshape.49), channel_id=1, source_target_pairs={{0,2},{1,3},{2,0},{3,1},{4,6},{5,7},{6,4},{7,5},{8,10},{9,11},{10,... | collective-permute-start | bytes 55304 | tf_op jit(solution)/shard_map/ppermute | solution.py:26
  6.4 35.7 %collective-permute-start.4 = (bf16[2,256,256]{2,1,0:T(8,128)(2,1)}, bf16[2,256,256]{2,1,0:T(8,128)(2,1)S(1)}, u32[]{:S(2)}, u32[]{:S(2)}) collective-permute-start(bf16[2,256,256]{2,1,0:T(8,128)(2,1)} %constant_dynamic-slice_fusion), channel_id=1, source_target_pairs={{0,2},{1,3},{2,0},{3,1},{4,6},{5,7},{6,4},{7,5},{8,10},{9,11},{10,... | collective-permute-start | bytes 786440 | tf_op jit(solution)/shard_map/ppermute | solution.py:26
  8.7 33.3 %collective-permute-start.3 = (bf16[2,256,256]{2,1,0:T(8,128)(2,1)}, bf16[2,256,256]{2,1,0:T(8,128)(2,1)S(1)}, u32[]{:S(2)}, u32[]{:S(2)}) collective-permute-start(bf16[2,256,256]{2,1,0:T(8,128)(2,1)} %constant_dynamic-slice_fusion), channel_id=1, source_target_pairs={{0,1},{1,2},{2,3},{3,0},{4,5},{5,6},{6,7},{7,4},{8,9},{9,10},{10,1... | collective-permute-start | bytes 786440 | tf_op jit(solution)/shard_map/ppermute | solution.py:26
  8.7 33.3 %collective-permute-start.5 = (bf16[2,256,256]{2,1,0:T(8,128)(2,1)}, bf16[2,256,256]{2,1,0:T(8,128)(2,1)}, u32[]{:S(2)}, u32[]{:S(2)}) collective-permute-start(bf16[2,256,256]{2,1,0:T(8,128)(2,1)} %constant_dynamic-slice_fusion), channel_id=1, source_target_pairs={{0,3},{1,0},{2,1},{3,2},{4,7},{5,4},{6,5},{7,6},{8,11},{9,8},{10,9... | collective-permute-start | bytes 786440 | tf_op jit(solution)/shard_map/ppermute | solution.py:26
  12.1 29.7 %collective-permute-start = (bf16[18,512]{1,0:T(8,128)(2,1)S(1)}, bf16[18,512]{1,0:T(8,128)(2,1)S(1)}, u32[]{:S(2)}, u32[]{:S(2)}) collective-permute-start(bf16[18,512]{1,0:T(8,128)(2,1)S(1)} %reshape.49), channel_id=1, source_target_pairs={{0,1},{1,2},{2,3},{3,0},{4,5},{5,6},{6,7},{7,4},{8,9},{9,10},{10,1... | collective-permute-start | bytes 55304 | tf_op jit(solution)/shard_map/ppermute | solution.py:26
  43.2 4.4 %collective-permute-start.6 = (bf16[4,2,256,256]{3,2,1,0:T(8,128)(2,1)S(1)}, bf16[4,2,256,256]{3,2,1,0:T(8,128)(2,1)S(1)}, u32[]{:S(2)}, u32[]{:S(2)}) collective-permute-start(bf16[4,2,256,256]{3,2,1,0:T(8,128)(2,1)S(1)} %pad_maximum_fusion.1), channel_id=1, source_target_pairs={{0,4},{4,0},{8,12},{12,8},{16,20},{20,16},{24,28},{28,24},{1,5},{5... | collective-permute-start | bytes 3145736 | tf_op jit(solution)/shard_map/ppermute | solution.py:31
  63.4 12.6 %collective-permute-start.7 = (bf16[864,256]{1,0:T(8,128)(2,1)}, bf16[864,256]{1,0:T(8,128)(2,1)S(1)}, u32[]{:S(2)}, u32[]{:S(2)}) collective-permute-start(bf16[864,256]{1,0:T(8,128)(2,1)} %get-tuple-element.14), channel_id=1, source_target_pairs={{0,8},{4,12},{8,16},{12,20},{16,24},{20,28},{1,9},{5,13},{9,17},{1... | collective-permute-start | bytes 1327112 | tf_op jit(solution)/shard_map/ppermute | solution.py:21
  66.6 20.9 %collective-permute-start.8 = (bf16[864,256]{1,0:T(8,128)(2,1)}, bf16[864,256]{1,0:T(8,128)(2,1)}, u32[]{:S(2)}, u32[]{:S(2)}) collective-permute-start(bf16[864,256]{1,0:T(8,128)(2,1)} %get-tuple-element.15), channel_id=1, source_target_pairs={{8,0},{12,4},{16,8},{20,12},{24,16},{28,20},{9,1},{13,5},{17,9},{2... | collective-permute-start | bytes 1327112 | tf_op jit(solution)/shard_map/ppermute | solution.py:21
  68.0 19.4 %collective-permute-start.9 = (bf16[864,256]{1,0:T(8,128)(2,1)}, bf16[864,256]{1,0:T(8,128)(2,1)}, u32[]{:S(2)}, u32[]{:S(2)}) collective-permute-start(bf16[864,256]{1,0:T(8,128)(2,1)} %get-tuple-element.17), channel_id=1, source_target_pairs={{0,16},{4,20},{8,24},{12,28},{16,0},{20,4},{24,8},{28,12},{1,17},{... | collective-permute-start | bytes 1327112 | tf_op jit(solution)/shard_map/ppermute | solution.py:26
  71.9 15.6 %copy-start.4 = (f32[864,256]{1,0:T(8,128)S(1)}, f32[864,256]{1,0:T(8,128)}, u32[]{:S(2)}) copy-start(f32[864,256]{1,0:T(8,128)} %get-tuple-element.13) | copy-start | bytes 2654212
  71.9 15.6 %copy-start.5 = (f32[864,256]{1,0:T(8,128)S(1)}, f32[864,256]{1,0:T(8,128)}, u32[]{:S(2)}) copy-start(f32[864,256]{1,0:T(8,128)} %get-tuple-element.16) | copy-start | bytes 2654212
  76.0 11.5 %copy-start.7 = (bf16[864,256]{1,0:T(8,128)(2,1)}, bf16[864,256]{1,0:T(8,128)(2,1)S(1)}, u32[]{:S(2)}) copy-start(bf16[864,256]{1,0:T(8,128)(2,1)S(1)} %collective-permute-done.7) | copy-start | bytes 1327108
  90.6 9.0 %copy-start.6 = (bf16[864,256]{1,0:T(8,128)(2,1)}, bf16[864,256]{1,0:T(8,128)(2,1)S(1)}, u32[]{:S(2)}) copy-start(bf16[864,256]{1,0:T(8,128)(2,1)S(1)} %get-tuple-element.44.refs_1_) | copy-start | bytes 1327108
  90.6 25.1 %collective-permute-start.11 = (bf16[864,256]{1,0:T(8,128)(2,1)}, bf16[864,256]{1,0:T(8,128)(2,1)S(1)}, u32[]{:S(2)}, u32[]{:S(2)}) collective-permute-start(bf16[864,256]{1,0:T(8,128)(2,1)} %get-tuple-element.50.refs_0_), channel_id=1, source_target_pairs={{0,8},{4,12},{8,16},{12,20},{16,24},{20,28},{1,9},{5,13},{9,17},{1... | collective-permute-start | bytes 1327112 | tf_op jit(solution)/shard_map/ppermute | solution.py:21
  96.4 19.3 %collective-permute-start.10 = (bf16[864,256]{1,0:T(8,128)(2,1)}, bf16[864,256]{1,0:T(8,128)(2,1)S(1)}, u32[]{:S(2)}, u32[]{:S(2)}) collective-permute-start(bf16[864,256]{1,0:T(8,128)(2,1)} %get-tuple-element.50.refs_0_), channel_id=1, source_target_pairs={{8,0},{12,4},{16,8},{20,12},{24,16},{28,20},{9,1},{13,5},{17,9},{2... | collective-permute-start | bytes 1327112 | tf_op jit(solution)/shard_map/ppermute | solution.py:21
  97.7 18.0 %collective-permute-start.12 = (bf16[864,256]{1,0:T(8,128)(2,1)S(1)}, bf16[864,256]{1,0:T(8,128)(2,1)}, u32[]{:S(2)}, u32[]{:S(2)}) collective-permute-start(bf16[864,256]{1,0:T(8,128)(2,1)S(1)} %get-tuple-element.44.refs_1_), channel_id=1, source_target_pairs={{0,16},{4,20},{8,24},{12,28},{16,0},{20,4},{24,8},{28,12},{1,17},{... | collective-permute-start | bytes 1327112 | tf_op jit(solution)/shard_map/ppermute | solution.py:26
  115.7 0.8 copy-start.8
  115.7 0.9 copy-start.9
  134.6 3.8 %collective-permute-start.13 = (bf16[4,4,136,256]{3,2,0,1:T(8,128)(2,1)S(1)}, bf16[4,4,136,256]{3,2,0,1:T(8,128)(2,1)S(1)}, u32[]{:S(2)}, u32[]{:S(2)}) collective-permute-start(bf16[4,4,136,256]{3,2,0,1:T(8,128)(2,1)S(1)} %bitcast.73), channel_id=1, source_target_pairs={{0,4},{4,0},{8,12},{12,8},{16,20},{20,16},{24,28},{28,24},{1,5},{5... | collective-permute-start | bytes 3342344 | tf_op jit(solution)/shard_map/ppermute | solution.py:31
  138.8 1.0 copy-start.2
  140.6 12.3 %collective-permute-start.14 = (bf16[4,136,256]{2,1,0:T(8,128)(2,1)}, bf16[4,136,256]{2,1,0:T(8,128)(2,1)}, u32[]{:S(2)}, u32[]{:S(2)}) collective-permute-start(bf16[4,136,256]{2,1,0:T(8,128)(2,1)} %get-tuple-element.46), channel_id=1, source_target_pairs={{0,8},{4,12},{8,0},{12,4},{16,24},{20,28},{24,16},{28,20},{1,9},{5... | collective-permute-start | bytes 835592 | tf_op jit(solution)/shard_map/ppermute | solution.py:31
  145.5 11.9 %collective-permute-start.16 = (bf16[4,136,256]{2,1,0:T(8,128)(2,1)S(1)}, bf16[4,136,256]{2,1,0:T(8,128)(2,1)}, u32[]{:S(2)}, u32[]{:S(2)}) collective-permute-start(bf16[4,136,256]{2,1,0:T(8,128)(2,1)S(1)} %get-tuple-element.47), channel_id=1, source_target_pairs={{0,24},{4,28},{8,16},{12,20},{16,8},{20,12},{24,0},{28,4},{1,25},{... | collective-permute-start | bytes 835592 | tf_op jit(solution)/shard_map/ppermute | solution.py:31
  145.5 13.6 %collective-permute-start.15 = (bf16[4,136,256]{2,1,0:T(8,128)(2,1)S(1)}, bf16[4,136,256]{2,1,0:T(8,128)(2,1)}, u32[]{:S(2)}, u32[]{:S(2)}) collective-permute-start(bf16[4,136,256]{2,1,0:T(8,128)(2,1)S(1)} %get-tuple-element.48), channel_id=1, source_target_pairs={{0,16},{4,20},{8,24},{12,28},{16,0},{20,4},{24,8},{28,12},{1,17},{... | collective-permute-start | bytes 835592 | tf_op jit(solution)/shard_map/ppermute | solution.py:31
  160.5 18.1 %collective-permute-start.17 = (bf16[136,256]{1,0:T(8,128)(2,1)S(1)}, bf16[136,256]{1,0:T(8,128)(2,1)S(1)}, u32[]{:S(2)}, u32[]{:S(2)}) collective-permute-start(bf16[136,256]{1,0:T(8,128)(2,1)S(1)} %get-tuple-element.53), channel_id=1, source_target_pairs={{0,3},{1,0},{2,1},{3,2},{4,7},{5,4},{6,5},{7,6},{8,11},{9,8},{10,9... | collective-permute-start | bytes 208904 | tf_op jit(solution)/shard_map/ppermute | solution.py:26
  164.1 14.6 %collective-permute-start.19 = (bf16[136,256]{1,0:T(8,128)(2,1)S(1)}, bf16[136,256]{1,0:T(8,128)(2,1)S(1)}, u32[]{:S(2)}, u32[]{:S(2)}) collective-permute-start(bf16[136,256]{1,0:T(8,128)(2,1)S(1)} %get-tuple-element.54), channel_id=1, source_target_pairs={{0,1},{1,2},{2,3},{3,0},{4,5},{5,6},{6,7},{7,4},{8,9},{9,10},{10,1... | collective-permute-start | bytes 208904 | tf_op jit(solution)/shard_map/ppermute | solution.py:26
  164.1 17.3 %copy-start.3 = (bf16[864,256]{1,0:T(8,128)(2,1)S(1)}, bf16[864,256]{1,0:T(8,128)(2,1)}, u32[]{:S(2)}) copy-start(bf16[864,256]{1,0:T(8,128)(2,1)} %get-tuple-element.49) | copy-start | bytes 1327108
  164.1 14.6 %collective-permute-start.18 = (bf16[136,256]{1,0:T(8,128)(2,1)S(1)}, bf16[136,256]{1,0:T(8,128)(2,1)S(1)}, u32[]{:S(2)}, u32[]{:S(2)}) collective-permute-start(bf16[136,256]{1,0:T(8,128)(2,1)S(1)} %get-tuple-element.55), channel_id=1, source_target_pairs={{0,2},{1,3},{2,0},{3,1},{4,6},{5,7},{6,4},{7,5},{8,10},{9,11},{10,... | collective-permute-start | bytes 208904 | tf_op jit(solution)/shard_map/ppermute | solution.py:26
  178.7 5.0 %collective-permute-start.22 = (bf16[136,256]{1,0:T(8,128)(2,1)S(1)}, bf16[136,256]{1,0:T(8,128)(2,1)S(1)}, u32[]{:S(2)}, u32[]{:S(2)}) collective-permute-start(bf16[136,256]{1,0:T(8,128)(2,1)S(1)} %fusion.6), channel_id=1, source_target_pairs={{0,24},{4,28},{8,16},{12,20},{16,8},{20,12},{24,0},{28,4},{1,25},{... | collective-permute-start | bytes 208904 | tf_op jit(solution)/shard_map/ppermute | solution.py:31
  180.2 3.5 %collective-permute-start.21 = (bf16[136,256]{1,0:T(8,128)(2,1)S(1)}, bf16[136,256]{1,0:T(8,128)(2,1)S(1)}, u32[]{:S(2)}, u32[]{:S(2)}) collective-permute-start(bf16[136,256]{1,0:T(8,128)(2,1)S(1)} %fusion.6), channel_id=1, source_target_pairs={{0,16},{4,20},{8,24},{12,28},{16,0},{20,4},{24,8},{28,12},{1,17},{... | collective-permute-start | bytes 208904 | tf_op jit(solution)/shard_map/ppermute | solution.py:31
  181.2 3.2 %collective-permute-start.20 = (bf16[136,256]{1,0:T(8,128)(2,1)S(1)}, bf16[136,256]{1,0:T(8,128)(2,1)S(1)}, u32[]{:S(2)}, u32[]{:S(2)}) collective-permute-start(bf16[136,256]{1,0:T(8,128)(2,1)S(1)} %fusion.6), channel_id=1, source_target_pairs={{0,8},{4,12},{8,0},{12,4},{16,24},{20,28},{24,16},{28,20},{1,9},{5... | collective-permute-start | bytes 208904 | tf_op jit(solution)/shard_map/ppermute | solution.py:31
  184.4 37.7 %collective-permute-start.23 = (bf16[4,136,256]{2,1,0:T(8,128)(2,1)S(1)}, bf16[4,136,256]{2,1,0:T(8,128)(2,1)S(1)}, u32[]{:S(2)}, u32[]{:S(2)}) collective-permute-start(bf16[4,136,256]{2,1,0:T(8,128)(2,1)S(1)} %get-tuple-element.52), channel_id=1, source_target_pairs={{0,4},{4,0},{8,12},{12,8},{16,20},{20,16},{24,28},{28,24},{1,5},{5... | collective-permute-start | bytes 835592 | tf_op jit(solution)/shard_map/ppermute | solution.py:31
  218.7 11.5 %copy-start.1 = (bf16[2,512,256]{2,1,0:T(8,128)(2,1)S(1)}, bf16[2,512,256]{2,1,0:T(8,128)(2,1)}, u32[]{:S(2)}) copy-start(bf16[2,512,256]{2,1,0:T(8,128)(2,1)} %param.5) | copy-start | bytes 1572868

commit v2 on v1

v2 whole, which is shorter than its diff:
```python
import functools
import math

import jax
import jax.numpy as jnp
from jax import lax
from jax.experimental import pallas as pl
from jax.experimental.pallas import tpu as pltpu
from jax.sharding import PartitionSpec as P

RATES = (12, 24)
SIDES = (-1, 0, 1)
F32 = jnp.float32
BF16 = jnp.bfloat16
TAP_ROWS = 32


def shift(value, axis, steps):
    count = lax.axis_size(axis)
    first, last = max(0, -steps), min(count, count - steps)
    return lax.ppermute(value, axis, [(i, i + steps) for i in range(first, last)])


def cycle(value, axis, steps):
    count = lax.axis_size(axis)
    return lax.ppermute(value, axis, [(i, (i + steps) % count) for i in range(count)])


def swap(value, axis, mask):
    count = lax.axis_size(axis)
    return lax.ppermute(value, axis, [(i, i ^ mask) for i in range(count)])


def to_slabs(field, grain):
    n, rows, width, ch = field.shape
    parts = field.reshape(n, rows, width // grain, grain, ch)
    return parts.transpose(2, 0, 1, 3, 4).reshape(-1, ch)


def from_slabs(flat, shape, grain):
    n, rows, width, ch = shape
    parts = flat.reshape(width // grain, n, rows, grain, ch)
    return parts.transpose(1, 2, 0, 3, 4).reshape(shape)


def span(slabs, q, side, reach):
    return 0 <= q + side * reach < slabs


def sums_kernel(terms, slabs, grain, x_ref, k_ref, xs_ref, *refs):
    outs, wide = refs[: len(terms)], refs[len(terms)]
    n, rows = x_ref.shape[:2]
    size = n * rows * grain
    for g in range(n * rows):
        line = x_ref[g // rows, g % rows].astype(F32)
        for q in range(slabs):
            at = q * size + g * grain
            wide[at : at + grain, :] = line[q * grain : (q + 1) * grain, :]
    xs_ref[...] = wide[...].astype(BF16)
    for t, (_, _, reach) in enumerate(terms):
        taps = [k_ref[0, 3 * t + i : 3 * t + i + 1, :] for i in range(3)]
        for q in range(slabs):
            total = None
            for i, side in enumerate(SIDES):
                if span(slabs, q, side, reach):
                    src = (q + side * reach) * size
                    term = wide[src : src + size, :] * taps[i]
                    total = term if total is None else total + term
            outs[t][q * size : (q + 1) * size, :] = total.astype(BF16)


def depthwise_sums(terms, slabs, grain, idx, x, k):
    n, rows, width, channels = x.shape
    cells, (blocks, _, own) = n * rows * width, k.shape
    flat = pl.BlockSpec((cells, own), lambda d, s: (0, s[3 + d]))
    kernel = functools.partial(sums_kernel, terms, slabs, grain)
    return pl.pallas_call(
        lambda s, *refs: kernel(*refs),
        grid_spec=pltpu.PrefetchScalarGridSpec(
            num_scalar_prefetch=1,
            grid=(blocks,),
            in_specs=[
                pl.BlockSpec((n, rows, width, own), lambda d, s: (0, 0, 0, s[3 + d])),
                pl.BlockSpec((1, k.shape[1], own), lambda d, s: (d, 0, 0)),
            ],
            out_specs=[flat] * (1 + len(terms)),
            scratch_shapes=[pltpu.VMEM((cells, own), F32)],
        ),
        out_shape=[jax.ShapeDtypeStruct((cells, channels), BF16)] * (1 + len(terms)),
        compiler_params=pltpu.CompilerParams(vmem_limit_bytes=60 << 20),
        cost_estimate=pl.CostEstimate(
            flops=6 * len(terms) * cells * channels,
            bytes_accessed=2 * (2 + len(terms)) * cells * channels,
            transcendentals=0,
        ),
        name="depthwise_sums",
    )(idx, x, k)


def forward_kernel(branches, w_ref, *refs):
    n = len(branches)
    ins, outs, acc = refs[:n], refs[n : 2 * n], refs[2 * n]
    step = pl.program_id(0)

    @pl.when(step == 0)
    def _():
        acc[...] = jnp.zeros_like(acc)

    for t, branch in enumerate(branches):
        acc[t] += jnp.dot(ins[t][...], w_ref[0, branch], preferred_element_type=F32)

    @pl.when(step == pl.num_programs(0) - 1)
    def _():
        for t in range(n):
            outs[t][...] = acc[t].astype(outs[t].dtype)


def forward(branches, dtype, idx, sums, w):
    cells, channels = sums[0].shape
    blocks, _, own, co = w.shape
    n = len(branches)
    kernel = functools.partial(forward_kernel, branches)
    return pl.pallas_call(
        lambda s, *refs: kernel(*refs),
        grid_spec=pltpu.PrefetchScalarGridSpec(
            num_scalar_prefetch=1,
            grid=(blocks,),
            in_specs=[pl.BlockSpec((1, 2, own, co), lambda d, s: (d, 0, 0, 0))]
            + [pl.BlockSpec((cells, own), lambda d, s: (0, s[3 + d]))] * n,
            out_specs=[pl.BlockSpec((cells, co), lambda d, s: (0, 0))] * n,
            scratch_shapes=[pltpu.VMEM((n, cells, co), F32)],
        ),
        out_shape=[jax.ShapeDtypeStruct((cells, co), dtype)] * n,
        compiler_params=pltpu.CompilerParams(vmem_limit_bytes=60 << 20),
        cost_estimate=pl.CostEstimate(
            flops=2 * n * cells * channels * co,
            bytes_accessed=2 * n * cells * channels + 4 * channels * co,
            transcendentals=0,
        ),
        name="forward_terms",
    )(idx, w, *sums)


def backward_kernel(terms, slabs, grain, halves, quarters, last, idx_ref, *refs):
    n = len(terms)
    x_ref, k_ref, w_ref, *refs = refs
    g_refs, d_refs, refs = refs[:n], refs[n : 2 * n], refs[2 * n :]
    if last:
        f_before, w_before, k_before, f_out, out_ref, gt, gd, kacc, wide = refs
    else:
        f_out, w_out, k_out, gt, gd, kacc = refs
    own, co = w_ref.shape[2:]
    cells = g_refs[0].shape[0]
    size = cells // slabs
    lanes = own // halves
    upper = idx_ref[2] > 0

    @pl.when(pl.program_id(0) == 0)
    def _():
        for t in range(n):
            gt[t] = g_refs[t][...].T

    kacc[...] = k_before[0] if last else jnp.zeros_like(kacc)
    for h in range(halves):
        cols = slice(h * lanes, (h + 1) * lanes)
        for t, (branch, _, _) in enumerate(terms):
            gd[h, t] = lax.dot_general(
                g_refs[t][...],
                w_ref[0, branch, cols, :],
                (((1,), (1,)), ((), ())),
                preferred_element_type=F32,
            )
        per = 2 * co // quarters
        seg = min(per, co)
        at_h = h ^ idx_ref[0] if halves > 1 else 0
        for branch in range(2):
            total = w_before[0, branch, :, cols] if last else None
            for t in range(n):
                if terms[t][0] == branch:
                    part = jnp.dot(gt[t], d_refs[t][:, cols], preferred_element_type=F32)
                    total = part if total is None else total + part
            if not last:
                w_out[0, branch, :, cols] = total
                continue
            for j in range(co // seg):
                q, off = divmod(branch * co + j * seg, per)
                at_q = q ^ idx_ref[1] if quarters > 1 else 0
                out_ref[0, at_h, at_q, off : off + seg, :] = total[
                    j * seg : (j + 1) * seg, :
                ].astype(BF16)
        sums = [None] * (3 * n)
        for q in range(slabs):
            here = slice(q * size, (q + 1) * size)
            xq = x_ref[here, cols].astype(F32)
            acc = f_before[here, cols] if last else None
            for t, (_, _, reach) in enumerate(terms):
                for i, side in enumerate(SIDES):
                    if not span(slabs, q, -side, reach):
                        continue
                    col = 3 * t + i
                    src = (q - side * reach) * size
                    part = gd[h, t, src : src + size, :]
                    term = part * k_ref[0, col : col + 1, cols]
                    acc = term if acc is None else acc + term
                    prod = jnp.sum((xq * part).reshape(size // 8, 8, lanes), axis=0)
                    sums[col] = prod if sums[col] is None else sums[col] + prod
            if last:
                rows = f_out.shape[1]
                for g in range(f_out.shape[0] * rows):
                    wide[g, q * grain : (q + 1) * grain, cols] = acc[g * grain : (g + 1) * grain, :]
            else:
                f_out[here, cols] = acc
        for t, (branch, u, _) in enumerate(terms):
            for i in range(3):
                total = jnp.sum(sums[3 * t + i], axis=0, keepdims=True)
                row = branch * 9 + i
                if u is None:
                    kacc[row : row + 1, cols] = jnp.where(upper, 0.0, total)
                    kacc[row + 6 : row + 7, cols] = jnp.where(upper, total, 0.0)
                else:
                    row += 3 * (u + 1)
                    kacc[row : row + 1, cols] = total
        if last:
            taps = TAP_ROWS // quarters
            for q in range(quarters):
                at_q = q ^ idx_ref[1] if quarters > 1 else 0
                out_ref[0, at_h, at_q, per:, :] = kacc[q * taps : (q + 1) * taps, cols].astype(BF16)
    if last:
        for g in range(wide.shape[0]):
            f_out[g // f_out.shape[1], g % f_out.shape[1]] = wide[g].astype(BF16)
    else:
        k_out[0] = kacc[...]


def backward(terms, slabs, grain, halves, quarters, idx, shape, x, k, w, gs, ds, before=None):
    blocks, _, own, co = w.shape
    cells, channels = x.shape
    images, rows, width, _ = shape
    n = len(terms)
    last = before is not None
    flat = pl.BlockSpec((cells, own), lambda d, s: (0, s[3 + d]))
    part_w = pl.BlockSpec((1, 2, co, own), lambda d, s: (d, 0, 0, 0))
    part_k = pl.BlockSpec((1, TAP_ROWS, own), lambda d, s: (d, 0, 0))
    in_specs = [
        flat,
        pl.BlockSpec((1,) + k.shape[1:], lambda d, s: (d, 0, 0)),
        pl.BlockSpec((1, 2, own, co), lambda d, s: (d, 0, 0, 0)),
    ]
    in_specs += [pl.BlockSpec((cells, co), lambda d, s: (0, 0))] * n + [flat] * n
    scratch = [
        pltpu.VMEM((n, co, cells), BF16),
        pltpu.VMEM((halves, n, cells, own // halves), F32),
        pltpu.VMEM((TAP_ROWS, own), F32),
    ]
    if last:
        in_specs += [flat, part_w, part_k]
        piece = (2 * co + TAP_ROWS) // quarters
        packed = (halves, quarters, piece, own // halves)
        out_specs = [
            pl.BlockSpec((images, rows, width, own), lambda d, s: (0, 0, 0, s[3 + d])),
            pl.BlockSpec((1,) + packed, lambda d, s: (d, 0, 0, 0, 0)),
        ]
        out_shape = [
            jax.ShapeDtypeStruct(shape, BF16),
            jax.ShapeDtypeStruct((blocks,) + packed, BF16),
        ]
        scratch.append(pltpu.VMEM((images * rows, width, own), F32))
    else:
        out_specs = [flat, part_w, part_k]
        out_shape = [
            jax.ShapeDtypeStruct((cells, channels), F32),
            jax.ShapeDtypeStruct((blocks, 2, co, own), F32),
            jax.ShapeDtypeStruct((blocks, TAP_ROWS, own), F32),
        ]
    return pl.pallas_call(
        functools.partial(backward_kernel, terms, slabs, grain, halves, quarters, last),
        grid_spec=pltpu.PrefetchScalarGridSpec(
            num_scalar_prefetch=1,
            grid=(blocks,),
            in_specs=in_specs,
            out_specs=out_specs,
            scratch_shapes=scratch,
        ),
        out_shape=out_shape,
        compiler_params=pltpu.CompilerParams(vmem_limit_bytes=60 << 20),
        cost_estimate=pl.CostEstimate(
            flops=4 * n * cells * channels * co,
            bytes_accessed=(2 * n + 6) * cells * channels,
            transcendentals=0,
        ),
        name="backward_outer" if last else "backward_middle",
    )(idx, x, k, w, *gs, *ds, *(before or ()))


def finish_kernel(factor, halves, quarters, idx_ref, in_ref, w_ref, k_ref, wide):
    co = w_ref.shape[2]
    per, taps = 2 * co // quarters, TAP_ROWS // quarters
    lanes = in_ref.shape[3]
    for h in range(halves):
        at_h = h ^ idx_ref[0] if halves > 1 else 0
        for q in range(quarters):
            at_q = q ^ idx_ref[1] if quarters > 1 else 0
            block = in_ref[at_h, at_q].astype(F32) * factor
            cols = slice(h * lanes, (h + 1) * lanes)
            wide[q * per : (q + 1) * per, cols] = block[:per]
            k_ref[q * taps : (q + 1) * taps, cols] = block[per:]
    for branch in range(2):
        w_ref[branch] = wide[branch * co : (branch + 1) * co, :].T


def finish(idx, pieces, own, factor):
    halves, quarters, rows, _ = pieces.shape
    co = (rows * quarters - TAP_ROWS) // 2
    w, k = pl.pallas_call(
        functools.partial(finish_kernel, factor, halves, quarters),
        in_specs=[
            pl.BlockSpec(memory_space=pltpu.SMEM),
            pl.BlockSpec(memory_space=pltpu.VMEM),
        ],
        out_specs=[pl.BlockSpec(memory_space=pltpu.VMEM)] * 2,
        out_shape=[
            jax.ShapeDtypeStruct((2, own, co), F32),
            jax.ShapeDtypeStruct((TAP_ROWS, own), F32),
        ],
        scratch_shapes=[pltpu.VMEM((2 * co, own), F32)],
        name="finish_grads",
    )(idx, pieces)
    return w, k[:18].reshape(2, 9, own)


def body(features, pointwise, depthwise, cotangent):
    n, rows, width, channels = features.shape
    own, co = pointwise.shape[1:]
    space, dp = lax.axis_size("space"), lax.axis_size("dp")
    me, row = lax.axis_index("space"), lax.axis_index("dp")
    chips = space // 2
    halves = 2 if space % 2 == 0 and own % 256 == 0 else 1
    part_c = own // halves
    even = chips & (chips - 1) == 0 and TAP_ROWS % (8 * chips) == 0 and 2 * co % (16 * chips) == 0 and chips <= 2 * co
    quarters = chips if halves == 2 and even else 1
    core, chip = me % 2, me // 2

    grain = math.gcd(*RATES)
    slabs = width // grain

    terms, moves = [], []
    for branch, rate in enumerate(RATES):
        offset, reach = rate // rows, rate // grain
        terms.append((branch, 0, reach))
        moves.append(0)
        if 2 * offset == space:
            terms.append((branch, None, reach))
            moves.append(offset)
        elif offset < space:
            for u in (-1, 1):
                terms.append((branch, u, reach))
                moves.append(u * offset)
    middle = [t for t, m in enumerate(moves) if m == 0]
    outer = [t for t, m in enumerate(moves) if m != 0]
    half_way = next((moves[t] for t in outer if terms[t][1] is None), space)
    upper = (me >= half_way).astype(jnp.int32)

    def send(value, t, direction):
        if terms[t][1] is None:
            return cycle(value, "space", moves[t])
        return shift(value, "space", direction * moves[t])

    idx = jnp.concatenate(
        [
            jnp.stack([core, chip, upper]).astype(jnp.int32),
            (row + dp - jnp.arange(dp)).astype(jnp.int32) % dp,
        ]
    )

    taps = depthwise.reshape(18, own)
    k_all = [taps] + [cycle(taps, "dp", d) for d in range(1, dp)]
    if halves == 2:
        mine = lax.dynamic_slice_in_dim(pointwise, core * part_c, part_c, axis=1)
        mine = jnp.stack([mine] + [cycle(mine, "dp", d) for d in range(1, dp)])
        other = swap(mine, "space", 1)
        low = jnp.where(core == 0, mine, other)
        high = jnp.where(core == 0, other, mine)
        w = jnp.concatenate([low, high], axis=2)
    else:
        w = jnp.stack([pointwise] + [cycle(pointwise, "dp", d) for d in range(1, dp)])

    k_rows = jnp.stack(k_all).astype(F32)
    k_terms = []
    for branch, u, _ in terms:
        at = branch * 9
        if u is None:
            k_terms.append(
                jnp.where(upper > 0, k_rows[:, at + 6 : at + 9], k_rows[:, at : at + 3])
            )
        else:
            k_terms.append(k_rows[:, at + 3 * (u + 1) : at + 3 * (u + 1) + 3])

    def tap_rows(chosen):
        joined = jnp.concatenate([k_terms[t] for t in chosen], axis=1)
        return jnp.pad(joined, ((0, 0), (0, -joined.shape[1] % 8), (0, 0)))

    k_fwd = tap_rows(range(len(terms)))
    k_mid, k_out = tap_rows(middle), tap_rows(outer)
    x, *sums = depthwise_sums(terms, slabs, grain, idx, features, k_fwd)
    cot = to_slabs(cotangent, grain)

    pick = lambda values, chosen: [values[t] for t in chosen]
    parts = [None] * len(terms)
    for chosen, dtype in ((outer, BF16), (middle, F32)):
        branches = [terms[t][0] for t in chosen]
        for t, part in zip(chosen, forward(branches, dtype, idx, pick(sums, chosen), w)):
            parts[t] = part
    received = {t: send(parts[t], t, -1) for t in outer}

    outputs, gs = [], [None] * len(terms)
    for t in middle:
        branch = terms[t][0]
        pre = parts[t]
        for o in outer:
            if terms[o][0] == branch:
                pre = pre + received[o].astype(F32)
        sig = jax.nn.sigmoid(pre)
        outputs.append((pre * sig).astype(BF16))
        cot_part = cot[:, branch * co : (branch + 1) * co].astype(F32)
        gs[t] = (cot_part * sig * (1.0 + pre * (1.0 - sig))).astype(BF16)
        for o in outer:
            if terms[o][0] == branch:
                gs[o] = send(gs[t], o, 1)
    branches_out = from_slabs(jnp.concatenate(outputs, axis=-1), cotangent.shape, grain)

    mid_terms, out_terms = pick(terms, middle), pick(terms, outer)
    common = (slabs, grain, halves, quarters, idx, features.shape, x)
    first = backward(mid_terms, *common, k_mid, w, pick(gs, middle), pick(sums, middle))
    feature_grad, grads = backward(
        out_terms, *common, k_out, w, pick(gs, outer), pick(sums, outer), first
    )

    factor = 1.0 / math.sqrt(dp * n * space * rows * width)
    if halves == 2:
        kept = grads[:, 0].astype(F32) + swap(grads[:, 1], "space", 1).astype(F32)
        kept = kept.astype(BF16)
    else:
        kept = grads[:, 0]
    if quarters > 1:
        total = kept[:, 0].astype(F32)
        for e in range(1, quarters):
            total = total + swap(kept[:, e], "space", 2 * e).astype(F32)
        total = total.astype(BF16)
    else:
        total = kept[:, 0]
    mine = total[0].astype(F32)
    for d in range(1, dp):
        mine = mine + cycle(total[d], "dp", -d).astype(F32)
    if quarters > 1:
        mine = mine.astype(BF16)
        block = jnp.stack([mine] + [swap(mine, "space", 2 * e) for e in range(1, quarters)])
    else:
        peers = [[i for i in range(space) if i % halves == c] for c in range(halves)]
        block = lax.psum(mine, "space", axis_index_groups=peers)[None]
    block = jnp.stack([block, swap(block, "space", 1)]) if halves == 2 else block[None]
    pointwise_grad, depthwise_grad = finish(idx, block, own, factor)
    return branches_out, feature_grad, pointwise_grad, depthwise_grad


def solution(mesh):
    return jax.shard_map(
        body,
        mesh=mesh,
        in_specs=(
            P("dp", "space", None, None),
            P(None, "dp", None),
            P(None, None, "dp"),
            P("dp", "space", None, None),
        ),
        out_specs=(
            P("dp", "space", None, None),
            P("dp", "space", None, None),
            P(None, "dp", None),
            P(None, None, "dp"),
        ),
        check_vma=False,
    )
```

time: 233 us -> 180 us (0.77)
  local copies, waits for them, and re-layouts: 64.3 us -> 9.98 us
  waiting for transfers between devices: 28.8 us -> 49.9 us
  Pallas kernels: 77.6 us -> 64.6 us
  other arithmetic: 11.4 us -> 7.67 us
    ppermute x11, waiting for transfers between devices: 4.55 us -> 26.5 us  [cycle(): lax.ppermute(value, axis, [(i, (i + steps) % count) for i in range(count)])]
    pallas_call x6, Pallas kernels: 77.6 us -> 64.6 us  [the longest x2 32.4 us: backward(): pl.pallas_call(functools.partial(backward_kernel, terms, slabs, grain, ha...]
    reshape x3 -> x1, local copies, waits for them, and re-layouts: 12.8 us -> 0.19 us  [to_slabs(): return parts.transpose(2, 0, 1, 3, 4).reshape(-1, ch)]
    unnamed x32, local copies, waits for them, and re-layouts: 16.3 us -> 5.14 us
    ppermute x4, waiting for transfers between devices: 13.5 us -> 5.91 us  [shift(): lax.ppermute(value, axis, [(i, i + steps) for i in range(first, last)])]
    ppermute x9, waiting for transfers between devices: 10.8 us -> 17.5 us  [swap(): return lax.ppermute(value, axis, [(i, i ^ mask) for i in range(count)])]
    reshape x2 -> x1, local copies, waits for them, and re-layouts: 6.73 us -> 0.19 us  [from_slabs(): parts = flat.reshape(width // grain, n, rows, grain, ch)]
    transpose x3 -> x0, local copies, waits for them, and re-layouts: 6.22 us -> none  [the longest x1 4.14 us: body(): wt = w.transpose(0, 1, 3, 2)]
  transfers between devices with their start and end apart: 24 -> 24, of which waited for: 8 -> 16; matrix products, arithmetic and copies ran while one was open for 25% -> 4% of each run, Pallas kernels for 19% -> 19%
where the time goes in v2:
time: 180 us; the launch traced here: 179 us
  Pallas kernels  64.6 us (36%)
  waiting for transfers between devices  49.9 us (28%)
  starting transfers between devices  46.2 us (26%)
  local copies, waits for them, and re-layouts  9.98 us (6%)
  other arithmetic  7.67 us (4%)
    pallas_call x2, Pallas kernels, backward(): pl.pallas_call(functools.partial(backward_kernel, terms, slabs, grain, ha...  32.4 us
    ppermute x11, waiting for transfers between devices, cycle(): lax.ppermute(value, axis, [(i, (i + steps) % count) for i in range(count)])  26.5 us
    ppermute x11, starting transfers between devices, cycle(): lax.ppermute(value, axis, [(i, (i + steps) % count) for i in range(count)])  21 us
    ppermute x9, waiting for transfers between devices, swap(): return lax.ppermute(value, axis, [(i, i ^ mask) for i in range(count)])  17.5 us
    pallas_call x2, Pallas kernels, forward(): pl.pallas_call(lambda s, *refs: kernel(*refs), grid_spec=pltpu.PrefetchSc...  16.3 us
    ppermute x9, starting transfers between devices, swap(): return lax.ppermute(value, axis, [(i, i ^ mask) for i in range(count)])  14.3 us
    pallas_call x1, Pallas kernels, depthwise_sums(): pl.pallas_call(lambda s, *refs: kernel(*refs), grid_spec=pltpu.PrefetchSc...  13.5 us
    ppermute x4, starting transfers between devices, shift(): lax.ppermute(value, axis, [(i, i + steps) for i in range(first, last)])  10.9 us
  transfers between devices with their start and end apart: 24, of which 16 were waited for; matrix products, arithmetic and copies ran while one was open for 4% of the time, Pallas kernels for 19%

profile of v2, /device:TPU:1, one launch (start us, length us, event | category | flops | bytes accessed | tf_op | source)
XLA Modules:
  0.0 179.3 jit_solution(6902305378507679585)
XLA Ops:
  0.7 1.0 copy-done
  1.7 2.2 %collective-permute-start = (bf16[2,256,256]{2,1,0:T(8,128)(2,1)S(1)}, bf16[2,256,256]{2,1,0:T(8,128)(2,1)S(1)}, u32[]{:S(2)}, u32[]{:S(2)}) collective-permute-start(bf16[2,256,256]{2,1,0:T(8,128)(2,1)S(1)} %constant_dynamic-slice_fusion), channel_id=1, source_target_pairs={{0,1},{1,2},{2,3},{3,0},{4,5},{5,6},{6,7},{7,4},{8,9},{9,10},{10,1... | collective-permute-start | bytes 786440 | tf_op jit(solution)/shard_map/ppermute | solution.py:26
  3.9 2.3 %collective-permute-start.1 = (bf16[2,256,256]{2,1,0:T(8,128)(2,1)S(1)}, bf16[2,256,256]{2,1,0:T(8,128)(2,1)S(1)}, u32[]{:S(2)}, u32[]{:S(2)}) collective-permute-start(bf16[2,256,256]{2,1,0:T(8,128)(2,1)S(1)} %constant_dynamic-slice_fusion), channel_id=1, source_target_pairs={{0,2},{1,3},{2,0},{3,1},{4,6},{5,7},{6,4},{7,5},{8,10},{9,11},{10,... | collective-permute-start | bytes 786440 | tf_op jit(solution)/shard_map/ppermute | solution.py:26
  6.2 1.1 collective-permute-start.2
  7.3 4.7 %collective-permute-done = bf16[2,256,256]{2,1,0:T(8,128)(2,1)S(1)} collective-permute-done((bf16[2,256,256]{2,1,0:T(8,128)(2,1)S(1)}, bf16[2,256,256]{2,1,0:T(8,128)(2,1)S(1)}, u32[]{:S(2)}, u32[]{:S(2)}) %collective-permute-start) | collective-permute-done | bytes 262176 | tf_op jit(solution)/shard_map/ppermute | solution.py:26
  12.0 11.9 %collective-permute-done.1 = bf16[2,256,256]{2,1,0:T(8,128)(2,1)S(1)} collective-permute-done((bf16[2,256,256]{2,1,0:T(8,128)(2,1)S(1)}, bf16[2,256,256]{2,1,0:T(8,128)(2,1)S(1)}, u32[]{:S(2)}, u32[]{:S(2)}) %collective-permute-start.1) | collective-permute-done | bytes 262176 | tf_op jit(solution)/shard_map/ppermute | solution.py:26
  23.9 0.7 copy-done.5
  24.8 0.7 collective-permute-start.3
  25.5 5.9 %collective-permute-start.4 = (bf16[18,512]{1,0:T(8,128)(2,1)S(1)}, bf16[18,512]{1,0:T(8,128)(2,1)S(1)}, u32[]{:S(2)}, u32[]{:S(2)}) collective-permute-start(bf16[18,512]{1,0:T(8,128)(2,1)S(1)} %reshape.32), channel_id=1, source_target_pairs={{0,1},{1,2},{2,3},{3,0},{4,5},{5,6},{6,7},{7,4},{8,9},{9,10},{10,1... | collective-permute-start | bytes 55304 | tf_op jit(solution)/shard_map/ppermute | solution.py:26
  31.3 1.3 collective-permute-start.5
  32.6 0.9 collective-permute-start.6
  33.5 0.6 pad_add_fusion.s.idx_ref
  34.1 1.2 collective-permute-done.5
  35.3 0.3 collective-permute-done.6
  35.7 0.2 concatenate.20
  36.0 0.7 pad.12.refs_1_
  36.6 13.5 %depthwise_sums.1 = (bf16[864,2048]{1,0:T(8,128)(2,1)}, bf16[864,2048]{1,0:T(8,128)(2,1)}, bf16[864,2048]{1,0:T(8,128)(2,1)}, bf16[864,2048]{1,0:T(8,128)(2,1)},...) custom-call(s32[7]{0:T(128)} %pad_add_fusion.s.idx_ref, bf16[2,6,72,2048]{3,2,1,0:T(8,128)(2,1)} %refs_0_.1, ...), custom_call_target="tpu_custom_call" | custom-call | flops 53084160 | bytes 24772608 | tf_op jit(solution)/shard_map/depthwise_sums/pallas_call | solution.py:77
  50.3 1.4 pad_maximum_fusion.refs_0_.refs_2_
  51.8 8.8 %forward_terms.3 = (bf16[864,256]{1,0:T(8,128)(2,1)}, bf16[864,256]{1,0:T(8,128)(2,1)}, bf16[864,256]{1,0:T(8,128)(2,1)}) custom-call(s32[7]{0:T(128)} %pad_add_fusion.s.idx_ref, bf16[4,2,512,256]{3,2,1,0:T(8,128)(2,1)} %pad_maximum_fusion.refs_0_.refs_2_, bf16[864,2048]{1,0:T(8,128)(2,1)} %get-tuple-element.25.refs_1_.refs_6_, ...), custom_call_target="tpu_custom_call" | custom-call | flops 2717908992 | bytes 12713984 | tf_op jit(solution)/shard_map/forward_terms/pallas_call | solution.py:123
  60.6 3.1 %collective-permute-start.7 = (bf16[864,256]{1,0:T(8,128)(2,1)}, bf16[864,256]{1,0:T(8,128)(2,1)S(1)}, u32[]{:S(2)}, u32[]{:S(2)}) collective-permute-start(bf16[864,256]{1,0:T(8,128)(2,1)} %get-tuple-element.28), channel_id=1, source_target_pairs={{0,8},{4,12},{8,16},{12,20},{16,24},{20,28},{1,9},{5,13},{9,17},{1... | collective-permute-start | bytes 1327112 | tf_op jit(solution)/shard_map/ppermute | solution.py:21
  63.8 1.3 collective-permute-start.8
  65.1 3.1 %collective-permute-start.9 = (bf16[864,256]{1,0:T(8,128)(2,1)}, bf16[864,256]{1,0:T(8,128)(2,1)}, u32[]{:S(2)}, u32[]{:S(2)}) collective-permute-start(bf16[864,256]{1,0:T(8,128)(2,1)} %get-tuple-element.31), channel_id=1, source_target_pairs={{0,16},{4,20},{8,24},{12,28},{16,0},{20,4},{24,8},{28,12},{1,17},{... | collective-permute-start | bytes 1327112 | tf_op jit(solution)/shard_map/ppermute | solution.py:26
  68.1 0.9 copy.18
  69.0 0.2 copy.19
  69.3 0.2 reshape.36
  69.5 0.7 select_maximum_fusion.refs_1_
  70.2 7.4 %forward_terms.2 = (f32[864,256]{1,0:T(8,128)}, f32[864,256]{1,0:T(8,128)}) custom-call(s32[7]{0:T(128)} %pad_add_fusion.s.idx_ref, bf16[4,2,512,256]{3,2,1,0:T(8,128)(2,1)} %pad_maximum_fusion.refs_0_.refs_2_, bf16[864,2048]{1,0:T(8,128)(2,1)} %get-tuple-element.22.refs_1_.refs_5_, bf16[864,2048]{1,0:T(8,128)(2,1)} %get-tuple-element.23.refs_2_.refs_6_), custom_call_target="tpu_custom_call" | custom-call | flops 1811939328 | bytes 9175040 | tf_op jit(solution)/shard_map/forward_terms/pallas_call | solution.py:123
  77.6 5.9 %collective-permute-done.8 = bf16[864,256]{1,0:T(8,128)(2,1)S(1)} collective-permute-done((bf16[864,256]{1,0:T(8,128)(2,1)}, bf16[864,256]{1,0:T(8,128)(2,1)S(1)}, u32[]{:S(2)}, u32[]{:S(2)}) %collective-permute-start.8) | collective-permute-done | bytes 442400 | tf_op jit(solution)/shard_map/ppermute | solution.py:21
  83.5 0.8 collective-permute-done.9
  84.4 2.4 %multiply_convert_fusion = (bf16[864,256]{1,0:T(8,128)(2,1)S(1)}, bf16[864,256]{1,0:T(8,128)(2,1)S(1)}, bf16[864,256]{1,0:T(8,128)(2,1)S(1)}, bf16[864,256]{1,0:T(8,128)(2,1)S(1)}) fusion(f32[864,256]{1,0:T(8,128)} %get-tuple-element.30, bf16[864,256]{1,0:T(8,128)(2,1)} %collective-permute-done.9, bf16[864,512]{1,0:T(8,128)(2,1)S(1)} %reshape.36, ...), kind=kLoop, calls=%fused_computation.9 | loop fusion | flops 6635520 | bytes 5750784 | tf_op jit(solution)/shard_map/convert_element_type | solution.py:425
  86.8 1.3 collective-permute-start.10
  88.1 5.2 %collective-permute-start.11 = (bf16[864,256]{1,0:T(8,128)(2,1)S(1)}, bf16[864,256]{1,0:T(8,128)(2,1)S(1)}, u32[]{:S(2)}, u32[]{:S(2)}) collective-permute-start(bf16[864,256]{1,0:T(8,128)(2,1)S(1)} %get-tuple-element.58.refs_3_), channel_id=1, source_target_pairs={{0,8},{4,12},{8,16},{12,20},{16,24},{20,28},{1,9},{5,13},{9,17},{1... | collective-permute-start | bytes 1327112 | tf_op jit(solution)/shard_map/ppermute | solution.py:21
  93.3 1.3 collective-permute-start.12
  94.6 0.6 select_maximum_fusion.2.refs_1_
  95.2 13.7 %backward_middle.1 = (f32[864,2048]{1,0:T(8,128)}, f32[4,2,256,512]{3,2,1,0:T(8,128)}, f32[4,32,512]{2,1,0:T(8,128)}) custom-call(s32[7]{0:T(128)} %pad_add_fusion.s.idx_ref, bf16[864,2048]{1,0:T(8,128)(2,1)} %get-tuple-element.32.refs_0_, f32[4,8,512]{2,1,0:T(8,128)} %select_maximum_fusion.2.refs_1_, ...), custom_call_target="tpu_custom_call" | custom-call | flops 3623878656 | bytes 17694720 | tf_op jit(solution)/shard_map/backward_middle/pallas_call | solution.py:275
  109.0 1.8 %collective-permute-done.12.refs_5_ = bf16[864,256]{1,0:T(8,128)(2,1)S(1)} collective-permute-done((bf16[864,256]{1,0:T(8,128)(2,1)S(1)}, bf16[864,256]{1,0:T(8,128)(2,1)S(1)}, u32[]{:S(2)}, u32[]{:S(2)}) %collective-permute-start.12) | collective-permute-done | bytes 442400 | tf_op jit(solution)/shard_map/ppermute | solution.py:26
  110.8 0.8 copy-done.10
  111.5 18.7 %backward_outer.1 = (bf16[2,6,72,2048]{3,2,1,0:T(8,128)(2,1)}, bf16[4,2,4,136,256]{4,3,2,1,0:T(8,128)(2,1)}) custom-call(s32[7]{0:T(128)} %pad_add_fusion.s.idx_ref, bf16[864,2048]{1,0:T(8,128)(2,1)} %get-tuple-element.32.refs_0_, f32[4,16,512]{2,1,0:T(8,128)} %select_maximum_fusion.refs_1_, bf16[4,2,512,256]{3,2,1,0:T(8,128)(2,1)} %pad_maximum_fusion.refs_0_.refs_2_, ...), custom_call_target="tpu_custom_call" | custom-call | flops 5435817984 | bytes 21233664 | tf_op jit(solution)/shard_map/backward_outer/pallas_call | solution.py:275
  130.3 1.5 slice_bitcast_fusion
  131.8 3.7 %collective-permute-start.13 = (bf16[4,4,136,256]{3,2,0,1:T(8,128)(2,1)S(1)}, bf16[4,4,136,256]{3,2,0,1:T(8,128)(2,1)S(1)}, u32[]{:S(2)}, u32[]{:S(2)}) collective-permute-start(bf16[4,4,136,256]{3,2,0,1:T(8,128)(2,1)S(1)} %slice_bitcast_fusion), channel_id=1, source_target_pairs={{0,4},{4,0},{8,12},{12,8},{16,20},{20,16},{24,28},{28,24},{1,5},{5... | collective-permute-start | bytes 3342344 | tf_op jit(solution)/shard_map/ppermute | solution.py:31
  135.5 2.4 %collective-permute-done.13 = bf16[4,4,136,256]{3,2,0,1:T(8,128)(2,1)S(1)} collective-permute-done((bf16[4,4,136,256]{3,2,0,1:T(8,128)(2,1)S(1)}, bf16[4,4,136,256]{3,2,0,1:T(8,128)(2,1)S(1)}, u32[]{:S(2)}, u32[]{:S(2)}) %collective-permute-start.13) | collective-permute-done | bytes 1114144 | tf_op jit(solution)/shard_map/ppermute | solution.py:31
  137.9 0.3 fusion
  138.3 2.3 %collective-permute-start.15 = (bf16[4,136,256]{2,1,0:T(8,128)(2,1)S(1)}, bf16[4,136,256]{2,1,0:T(8,128)(2,1)S(1)}, u32[]{:S(2)}, u32[]{:S(2)}) collective-permute-start(bf16[4,136,256]{2,1,0:T(8,128)(2,1)S(1)} %get-tuple-element.56), channel_id=1, source_target_pairs={{0,16},{4,20},{8,24},{12,28},{16,0},{20,4},{24,8},{28,12},{1,17},{... | collective-permute-start | bytes 835592 | tf_op jit(solution)/shard_map/ppermute | solution.py:31
  140.6 1.1 collective-permute-start.16
  141.7 4.5 %collective-permute-done.14 = bf16[4,136,256]{2,1,0:T(8,128)(2,1)S(1)} collective-permute-done((bf16[4,136,256]{2,1,0:T(8,128)(2,1)S(1)}, bf16[4,136,256]{2,1,0:T(8,128)(2,1)S(1)}, u32[]{:S(2)}, u32[]{:S(2)}) %collective-permute-start.14) | collective-permute-done | bytes 278560 | tf_op jit(solution)/shard_map/ppermute | solution.py:31
  146.1 1.1 collective-permute-done.15
  147.2 6.8 %collective-permute-done.16 = bf16[4,136,256]{2,1,0:T(8,128)(2,1)S(1)} collective-permute-done((bf16[4,136,256]{2,1,0:T(8,128)(2,1)S(1)}, bf16[4,136,256]{2,1,0:T(8,128)(2,1)S(1)}, u32[]{:S(2)}, u32[]{:S(2)}) %collective-permute-start.16) | collective-permute-done | bytes 278560 | tf_op jit(solution)/shard_map/ppermute | solution.py:31
  154.2 2.8 %collective-permute-start.17 = (bf16[136,256]{1,0:T(8,128)(2,1)S(1)}, bf16[136,256]{1,0:T(8,128)(2,1)S(1)}, u32[]{:S(2)}, u32[]{:S(2)}) collective-permute-start(bf16[136,256]{1,0:T(8,128)(2,1)S(1)} %get-tuple-element.61), channel_id=1, source_target_pairs={{0,3},{1,0},{2,1},{3,2},{4,7},{5,4},{6,5},{7,6},{8,11},{9,8},{10,9... | collective-permute-start | bytes 208904 | tf_op jit(solution)/shard_map/ppermute | solution.py:26
  157.0 0.4 collective-permute-start.19
  157.3 1.0 collective-permute-done.17
  158.4 4.7 %collective-permute-done.18 = bf16[136,256]{1,0:T(8,128)(2,1)S(1)} collective-permute-done((bf16[136,256]{1,0:T(8,128)(2,1)S(1)}, bf16[136,256]{1,0:T(8,128)(2,1)S(1)}, u32[]{:S(2)}, u32[]{:S(2)}) %collective-permute-start.18) | collective-permute-done | bytes 69664 | tf_op jit(solution)/shard_map/ppermute | solution.py:26
  163.1 0.4 collective-permute-start.20
  163.5 0.6 collective-permute-start.21
  164.1 1.7 collective-permute-start.22
  165.8 0.5 collective-permute-done.20
  166.3 0.4 collective-permute-done.21
  166.7 1.9 %collective-permute-done.22 = bf16[136,256]{1,0:T(8,128)(2,1)S(1)} collective-permute-done((bf16[136,256]{1,0:T(8,128)(2,1)S(1)}, bf16[136,256]{1,0:T(8,128)(2,1)S(1)}, u32[]{:S(2)}, u32[]{:S(2)}) %collective-permute-start.22) | collective-permute-done | bytes 69664 | tf_op jit(solution)/shard_map/ppermute | solution.py:31
  168.6 3.7 %collective-permute-start.23 = (bf16[4,136,256]{2,1,0:T(8,128)(2,1)S(1)}, bf16[4,136,256]{2,1,0:T(8,128)(2,1)S(1)}, u32[]{:S(2)}, u32[]{:S(2)}) collective-permute-start(bf16[4,136,256]{2,1,0:T(8,128)(2,1)S(1)} %get-tuple-element.60), channel_id=1, source_target_pairs={{0,4},{4,0},{8,12},{12,8},{16,20},{20,16},{24,28},{28,24},{1,5},{5... | collective-permute-start | bytes 835592 | tf_op jit(solution)/shard_map/ppermute | solution.py:31
  172.6 0.9 copy.17
  173.6 1.1 copy.22
  174.6 0.9 pad_maximum_fusion.3.in_ref
  175.5 2.4 %finish_grads.1 = (f32[2,512,256]{2,1,0:T(8,128)}, f32[32,512]{1,0:T(8,128)}) custom-call(s32[7]{0:T(128)} %pad_add_fusion.s.idx_ref, bf16[2,4,136,256]{3,2,1,0:T(8,128)(2,1)} %pad_maximum_fusion.3.in_ref), custom_call_target="tpu_custom_call" | custom-call | tf_op jit(solution)/shard_map/finish_grads/pallas_call | solution.py:314
  177.9 0.8 slice.75
  178.7 0.6 copy.23
  (53 shorter events, 1.2 us)
Async XLA Ops:
  0.6 1.1 copy-start
  0.6 24.8 %copy-start.13 = (bf16[2,9,512]{2,0,1:T(2,128)(2,1)S(1)}, bf16[2,9,512]{2,0,1:T(2,128)(2,1)}, u32[]{:S(2)}) copy-start(bf16[2,9,512]{2,0,1:T(2,128)(2,1)} %param.6) | copy-start | bytes 55300
  1.7 10.3 %collective-permute-start = (bf16[2,256,256]{2,1,0:T(8,128)(2,1)S(1)}, bf16[2,256,256]{2,1,0:T(8,128)(2,1)S(1)}, u32[]{:S(2)}, u32[]{:S(2)}) collective-permute-start(bf16[2,256,256]{2,1,0:T(8,128)(2,1)S(1)} %constant_dynamic-slice_fusion), channel_id=1, source_target_pairs={{0,1},{1,2},{2,3},{3,0},{4,5},{5,6},{6,7},{7,4},{8,9},{9,10},{10,1... | collective-permute-start | bytes 786440 | tf_op jit(solution)/shard_map/ppermute | solution.py:26
  3.9 20.1 %collective-permute-start.1 = (bf16[2,256,256]{2,1,0:T(8,128)(2,1)S(1)}, bf16[2,256,256]{2,1,0:T(8,128)(2,1)S(1)}, u32[]{:S(2)}, u32[]{:S(2)}) collective-permute-start(bf16[2,256,256]{2,1,0:T(8,128)(2,1)S(1)} %constant_dynamic-slice_fusion), channel_id=1, source_target_pairs={{0,2},{1,3},{2,0},{3,1},{4,6},{5,7},{6,4},{7,5},{8,10},{9,11},{10,... | collective-permute-start | bytes 786440 | tf_op jit(solution)/shard_map/ppermute | solution.py:26
  6.2 17.8 %collective-permute-start.2 = (bf16[2,256,256]{2,1,0:T(8,128)(2,1)S(1)}, bf16[2,256,256]{2,1,0:T(8,128)(2,1)S(1)}, u32[]{:S(2)}, u32[]{:S(2)}) collective-permute-start(bf16[2,256,256]{2,1,0:T(8,128)(2,1)S(1)} %constant_dynamic-slice_fusion), channel_id=1, source_target_pairs={{0,3},{1,0},{2,1},{3,2},{4,7},{5,4},{6,5},{7,6},{8,11},{9,8},{10,9... | collective-permute-start | bytes 786440 | tf_op jit(solution)/shard_map/ppermute | solution.py:26
  23.9 0.7 copy-start.5
  24.8 25.3 %collective-permute-start.3 = (bf16[4,2,256,256]{3,2,1,0:T(8,128)(2,1)S(1)}, bf16[4,2,256,256]{3,2,1,0:T(8,128)(2,1)S(1)}, u32[]{:S(2)}, u32[]{:S(2)}) collective-permute-start(bf16[4,2,256,256]{3,2,1,0:T(8,128)(2,1)S(1)} %pad_maximum_fusion.1), channel_id=1, source_target_pairs={{0,4},{4,0},{8,12},{12,8},{16,20},{20,16},{24,28},{28,24},{1,5},{5... | collective-permute-start | bytes 3145736 | tf_op jit(solution)/shard_map/ppermute | solution.py:31
  25.5 8.7 %collective-permute-start.4 = (bf16[18,512]{1,0:T(8,128)(2,1)S(1)}, bf16[18,512]{1,0:T(8,128)(2,1)S(1)}, u32[]{:S(2)}, u32[]{:S(2)}) collective-permute-start(bf16[18,512]{1,0:T(8,128)(2,1)S(1)} %reshape.32), channel_id=1, source_target_pairs={{0,1},{1,2},{2,3},{3,0},{4,5},{5,6},{6,7},{7,4},{8,9},{9,10},{10,1... | collective-permute-start | bytes 55304 | tf_op jit(solution)/shard_map/ppermute | solution.py:26
  31.3 4.0 %collective-permute-start.5 = (bf16[18,512]{1,0:T(8,128)(2,1)S(1)}, bf16[18,512]{1,0:T(8,128)(2,1)S(1)}, u32[]{:S(2)}, u32[]{:S(2)}) collective-permute-start(bf16[18,512]{1,0:T(8,128)(2,1)S(1)} %reshape.32), channel_id=1, source_target_pairs={{0,2},{1,3},{2,0},{3,1},{4,6},{5,7},{6,4},{7,5},{8,10},{9,11},{10,... | collective-permute-start | bytes 55304 | tf_op jit(solution)/shard_map/ppermute | solution.py:26
  32.6 3.0 %collective-permute-start.6 = (bf16[18,512]{1,0:T(8,128)(2,1)S(1)}, bf16[18,512]{1,0:T(8,128)(2,1)S(1)}, u32[]{:S(2)}, u32[]{:S(2)}) collective-permute-start(bf16[18,512]{1,0:T(8,128)(2,1)S(1)} %reshape.32), channel_id=1, source_target_pairs={{0,3},{1,0},{2,1},{3,2},{4,7},{5,4},{6,5},{7,6},{8,11},{9,8},{10,9... | collective-permute-start | bytes 55304 | tf_op jit(solution)/shard_map/ppermute | solution.py:26
  35.7 14.5 %copy-start.6 = (bf16[2,256,256]{2,1,0:T(8,128)(2,1)S(1)}, bf16[2,256,256]{2,1,0:T(8,128)(2,1)}, u32[]{:S(2)}) copy-start(bf16[2,256,256]{2,1,0:T(8,128)(2,1)} %copy-done.5) | copy-start | bytes 786436
  35.7 14.6 %copy-start.11 = (f32[4,3,512]{2,1,0:T(4,128)}, f32[4,3,512]{2,1,0:T(4,128)S(1)}, u32[]{:S(2)}) copy-start(f32[4,3,512]{2,1,0:T(4,128)S(1)} %get-tuple-element.68) | copy-start | bytes 73732
  51.8 16.3 %copy-start.7 = (bf16[2,6,72,512]{3,2,1,0:T(8,128)(2,1)S(1)}, bf16[2,6,72,512]{3,2,1,0:T(8,128)(2,1)}, u32[]{:S(2)}) copy-start(bf16[2,6,72,512]{3,2,1,0:T(8,128)(2,1)} %param.7) | copy-start | bytes 2654212
  60.6 17.0 %collective-permute-start.7 = (bf16[864,256]{1,0:T(8,128)(2,1)}, bf16[864,256]{1,0:T(8,128)(2,1)S(1)}, u32[]{:S(2)}, u32[]{:S(2)}) collective-permute-start(bf16[864,256]{1,0:T(8,128)(2,1)} %get-tuple-element.28), channel_id=1, source_target_pairs={{0,8},{4,12},{8,16},{12,20},{16,24},{20,28},{1,9},{5,13},{9,17},{1... | collective-permute-start | bytes 1327112 | tf_op jit(solution)/shard_map/ppermute | solution.py:21
  63.8 19.8 %collective-permute-start.8 = (bf16[864,256]{1,0:T(8,128)(2,1)}, bf16[864,256]{1,0:T(8,128)(2,1)S(1)}, u32[]{:S(2)}, u32[]{:S(2)}) collective-permute-start(bf16[864,256]{1,0:T(8,128)(2,1)} %get-tuple-element.29), channel_id=1, source_target_pairs={{8,0},{12,4},{16,8},{20,12},{24,16},{28,20},{9,1},{13,5},{17,9},{2... | collective-permute-start | bytes 1327112 | tf_op jit(solution)/shard_map/ppermute | solution.py:21
  65.1 19.3 %collective-permute-start.9 = (bf16[864,256]{1,0:T(8,128)(2,1)}, bf16[864,256]{1,0:T(8,128)(2,1)}, u32[]{:S(2)}, u32[]{:S(2)}) collective-permute-start(bf16[864,256]{1,0:T(8,128)(2,1)} %get-tuple-element.31), channel_id=1, source_target_pairs={{0,16},{4,20},{8,24},{12,28},{16,0},{20,4},{24,8},{28,12},{1,17},{... | collective-permute-start | bytes 1327112 | tf_op jit(solution)/shard_map/ppermute | solution.py:26
  84.3 10.2 %copy-start.12 = (f32[4,3,512]{2,1,0:T(4,128)S(1)}, f32[4,3,512]{2,1,0:T(4,128)}, u32[]{:S(2)}) copy-start(f32[4,3,512]{2,1,0:T(4,128)} %copy-done.11) | copy-start | bytes 73732
  86.8 8.4 %copy-start.3 = (bf16[864,256]{1,0:T(8,128)(2,1)}, bf16[864,256]{1,0:T(8,128)(2,1)S(1)}, u32[]{:S(2)}) copy-start(bf16[864,256]{1,0:T(8,128)(2,1)S(1)} %get-tuple-element.52.refs_4_) | copy-start | bytes 1327108
  86.8 8.4 %copy-start.4 = (bf16[864,256]{1,0:T(8,128)(2,1)}, bf16[864,256]{1,0:T(8,128)(2,1)S(1)}, u32[]{:S(2)}) copy-start(bf16[864,256]{1,0:T(8,128)(2,1)S(1)} %get-tuple-element.58.refs_3_) | copy-start | bytes 1327108
  86.8 22.1 %collective-permute-start.10 = (bf16[864,256]{1,0:T(8,128)(2,1)S(1)}, bf16[864,256]{1,0:T(8,128)(2,1)S(1)}, u32[]{:S(2)}, u32[]{:S(2)}) collective-permute-start(bf16[864,256]{1,0:T(8,128)(2,1)S(1)} %get-tuple-element.58.refs_3_), channel_id=1, source_target_pairs={{8,0},{12,4},{16,8},{20,12},{24,16},{28,20},{9,1},{13,5},{17,9},{2... | collective-permute-start | bytes 1327112 | tf_op jit(solution)/shard_map/ppermute | solution.py:21
  88.1 20.8 %collective-permute-start.11 = (bf16[864,256]{1,0:T(8,128)(2,1)S(1)}, bf16[864,256]{1,0:T(8,128)(2,1)S(1)}, u32[]{:S(2)}, u32[]{:S(2)}) collective-permute-start(bf16[864,256]{1,0:T(8,128)(2,1)S(1)} %get-tuple-element.58.refs_3_), channel_id=1, source_target_pairs={{0,8},{4,12},{8,16},{12,20},{16,24},{20,28},{1,9},{5,13},{9,17},{1... | collective-permute-start | bytes 1327112 | tf_op jit(solution)/shard_map/ppermute | solution.py:21
  93.3 17.5 %collective-permute-start.12 = (bf16[864,256]{1,0:T(8,128)(2,1)S(1)}, bf16[864,256]{1,0:T(8,128)(2,1)S(1)}, u32[]{:S(2)}, u32[]{:S(2)}) collective-permute-start(bf16[864,256]{1,0:T(8,128)(2,1)S(1)} %get-tuple-element.52.refs_4_), channel_id=1, source_target_pairs={{0,16},{4,20},{8,24},{12,28},{16,0},{20,4},{24,8},{28,12},{1,17},{... | collective-permute-start | bytes 1327112 | tf_op jit(solution)/shard_map/ppermute | solution.py:26
  108.9 1.9 %copy-start.8 = (bf16[864,256]{1,0:T(8,128)(2,1)}, bf16[864,256]{1,0:T(8,128)(2,1)S(1)}, u32[]{:S(2)}) copy-start(bf16[864,256]{1,0:T(8,128)(2,1)S(1)} %collective-permute-done.10.refs_3_) | copy-start | bytes 1327108
  108.9 1.8 %copy-start.9 = (bf16[864,256]{1,0:T(8,128)(2,1)}, bf16[864,256]{1,0:T(8,128)(2,1)S(1)}, u32[]{:S(2)}) copy-start(bf16[864,256]{1,0:T(8,128)(2,1)S(1)} %collective-permute-done.11.refs_4_) | copy-start | bytes 1327108
  110.8 0.8 copy-start.10
  130.3 7.6 %copy-start.2 = (bf16[4,2,4,136,256]{4,3,2,1,0:T(8,128)(2,1)S(1)}, bf16[4,2,4,136,256]{4,3,2,1,0:T(8,128)(2,1)}, u32[]{:S(2)}) copy-start(bf16[4,2,4,136,256]{4,3,2,1,0:T(8,128)(2,1)} %get-tuple-element.37) | copy-start | bytes 6684676
  131.8 6.1 %collective-permute-start.13 = (bf16[4,4,136,256]{3,2,0,1:T(8,128)(2,1)S(1)}, bf16[4,4,136,256]{3,2,0,1:T(8,128)(2,1)S(1)}, u32[]{:S(2)}, u32[]{:S(2)}) collective-permute-start(bf16[4,4,136,256]{3,2,0,1:T(8,128)(2,1)S(1)} %slice_bitcast_fusion), channel_id=1, source_target_pairs={{0,4},{4,0},{8,12},{12,8},{16,20},{20,16},{24,28},{28,24},{1,5},{5... | collective-permute-start | bytes 3342344 | tf_op jit(solution)/shard_map/ppermute | solution.py:31
  138.2 7.9 %collective-permute-start.14 = (bf16[4,136,256]{2,1,0:T(8,128)(2,1)S(1)}, bf16[4,136,256]{2,1,0:T(8,128)(2,1)S(1)}, u32[]{:S(2)}, u32[]{:S(2)}) collective-permute-start(bf16[4,136,256]{2,1,0:T(8,128)(2,1)S(1)} %get-tuple-element.54), channel_id=1, source_target_pairs={{0,8},{4,12},{8,0},{12,4},{16,24},{20,28},{24,16},{28,20},{1,9},{5... | collective-permute-start | bytes 835592 | tf_op jit(solution)/shard_map/ppermute | solution.py:31
  138.3 8.9 %collective-permute-start.15 = (bf16[4,136,256]{2,1,0:T(8,128)(2,1)S(1)}, bf16[4,136,256]{2,1,0:T(8,128)(2,1)S(1)}, u32[]{:S(2)}, u32[]{:S(2)}) collective-permute-start(bf16[4,136,256]{2,1,0:T(8,128)(2,1)S(1)} %get-tuple-element.56), channel_id=1, source_target_pairs={{0,16},{4,20},{8,24},{12,28},{16,0},{20,4},{24,8},{28,12},{1,17},{... | collective-permute-start | bytes 835592 | tf_op jit(solution)/shard_map/ppermute | solution.py:31
  140.6 13.4 %collective-permute-start.16 = (bf16[4,136,256]{2,1,0:T(8,128)(2,1)S(1)}, bf16[4,136,256]{2,1,0:T(8,128)(2,1)S(1)}, u32[]{:S(2)}, u32[]{:S(2)}) collective-permute-start(bf16[4,136,256]{2,1,0:T(8,128)(2,1)S(1)} %get-tuple-element.55), channel_id=1, source_target_pairs={{0,24},{4,28},{8,16},{12,20},{16,8},{20,12},{24,0},{28,4},{1,25},{... | collective-permute-start | bytes 835592 | tf_op jit(solution)/shard_map/ppermute | solution.py:31
  154.2 4.1 %collective-permute-start.17 = (bf16[136,256]{1,0:T(8,128)(2,1)S(1)}, bf16[136,256]{1,0:T(8,128)(2,1)S(1)}, u32[]{:S(2)}, u32[]{:S(2)}) collective-permute-start(bf16[136,256]{1,0:T(8,128)(2,1)S(1)} %get-tuple-element.61), channel_id=1, source_target_pairs={{0,3},{1,0},{2,1},{3,2},{4,7},{5,4},{6,5},{7,6},{8,11},{9,8},{10,9... | collective-permute-start | bytes 208904 | tf_op jit(solution)/shard_map/ppermute | solution.py:26
  157.0 6.1 %collective-permute-start.18 = (bf16[136,256]{1,0:T(8,128)(2,1)S(1)}, bf16[136,256]{1,0:T(8,128)(2,1)S(1)}, u32[]{:S(2)}, u32[]{:S(2)}) collective-permute-start(bf16[136,256]{1,0:T(8,128)(2,1)S(1)} %get-tuple-element.63), channel_id=1, source_target_pairs={{0,2},{1,3},{2,0},{3,1},{4,6},{5,7},{6,4},{7,5},{8,10},{9,11},{10,... | collective-permute-start | bytes 208904 | tf_op jit(solution)/shard_map/ppermute | solution.py:26
  157.0 6.1 %collective-permute-start.19 = (bf16[136,256]{1,0:T(8,128)(2,1)S(1)}, bf16[136,256]{1,0:T(8,128)(2,1)S(1)}, u32[]{:S(2)}, u32[]{:S(2)}) collective-permute-start(bf16[136,256]{1,0:T(8,128)(2,1)S(1)} %get-tuple-element.62), channel_id=1, source_target_pairs={{0,1},{1,2},{2,3},{3,0},{4,5},{5,6},{6,7},{7,4},{8,9},{9,10},{10,1... | collective-permute-start | bytes 208904 | tf_op jit(solution)/shard_map/ppermute | solution.py:26
  163.1 3.2 %collective-permute-start.20 = (bf16[136,256]{1,0:T(8,128)(2,1)S(1)}, bf16[136,256]{1,0:T(8,128)(2,1)S(1)}, u32[]{:S(2)}, u32[]{:S(2)}) collective-permute-start(bf16[136,256]{1,0:T(8,128)(2,1)S(1)} %fusion.6), channel_id=1, source_target_pairs={{0,8},{4,12},{8,0},{12,4},{16,24},{20,28},{24,16},{28,20},{1,9},{5... | collective-permute-start | bytes 208904 | tf_op jit(solution)/shard_map/ppermute | solution.py:31
  163.5 3.2 %collective-permute-start.21 = (bf16[136,256]{1,0:T(8,128)(2,1)S(1)}, bf16[136,256]{1,0:T(8,128)(2,1)S(1)}, u32[]{:S(2)}, u32[]{:S(2)}) collective-permute-start(bf16[136,256]{1,0:T(8,128)(2,1)S(1)} %fusion.6), channel_id=1, source_target_pairs={{0,16},{4,20},{8,24},{12,28},{16,0},{20,4},{24,8},{28,12},{1,17},{... | collective-permute-start | bytes 208904 | tf_op jit(solution)/shard_map/ppermute | solution.py:31
  164.1 4.4 %collective-permute-start.22 = (bf16[136,256]{1,0:T(8,128)(2,1)S(1)}, bf16[136,256]{1,0:T(8,128)(2,1)S(1)}, u32[]{:S(2)}, u32[]{:S(2)}) collective-permute-start(bf16[136,256]{1,0:T(8,128)(2,1)S(1)} %fusion.6), channel_id=1, source_target_pairs={{0,24},{4,28},{8,16},{12,20},{16,8},{20,12},{24,0},{28,4},{1,25},{... | collective-permute-start | bytes 208904 | tf_op jit(solution)/shard_map/ppermute | solution.py:31
  168.6 6.0 %collective-permute-start.23 = (bf16[4,136,256]{2,1,0:T(8,128)(2,1)S(1)}, bf16[4,136,256]{2,1,0:T(8,128)(2,1)S(1)}, u32[]{:S(2)}, u32[]{:S(2)}) collective-permute-start(bf16[4,136,256]{2,1,0:T(8,128)(2,1)S(1)} %get-tuple-element.60), channel_id=1, source_target_pairs={{0,4},{4,0},{8,12},{12,8},{16,20},{20,16},{24,28},{28,24},{1,5},{5... | collective-permute-start | bytes 835592 | tf_op jit(solution)/shard_map/ppermute | solution.py:31
  172.6 6.7 %copy-start.1 = (bf16[2,512,256]{2,1,0:T(8,128)(2,1)S(1)}, bf16[2,512,256]{2,1,0:T(8,128)(2,1)}, u32[]{:S(2)}) copy-start(bf16[2,512,256]{2,1,0:T(8,128)(2,1)} %param.5) | copy-start | bytes 1572868

commit v3 on v2

--- a/solution.py
+++ b/solution.py
@@ -72,7 +72,7 @@
 def depthwise_sums(terms, slabs, grain, idx, x, k):
     n, rows, width, channels = x.shape
     cells, (blocks, _, own) = n * rows * width, k.shape
-    flat = pl.BlockSpec((cells, own), lambda d, s: (0, s[3 + d]))
+    flat = pl.BlockSpec((cells, own), lambda d, s: (0, d))
     kernel = functools.partial(sums_kernel, terms, slabs, grain)
     return pl.pallas_call(
         lambda s, *refs: kernel(*refs),
@@ -99,37 +99,23 @@
 
 def forward_kernel(branches, w_ref, *refs):
     n = len(branches)
-    ins, outs, acc = refs[:n], refs[n : 2 * n], refs[2 * n]
-    step = pl.program_id(0)
-
-    @pl.when(step == 0)
-    def _():
-        acc[...] = jnp.zeros_like(acc)
-
     for t, branch in enumerate(branches):
-        acc[t] += jnp.dot(ins[t][...], w_ref[0, branch], preferred_element_type=F32)
-
-    @pl.when(step == pl.num_programs(0) - 1)
-    def _():
-        for t in range(n):
-            outs[t][...] = acc[t].astype(outs[t].dtype)
-
-
-def forward(branches, dtype, idx, sums, w):
+        part = jnp.dot(refs[t][...], w_ref[branch], preferred_element_type=F32)
+        refs[n + t][...] = part.astype(refs[n + t].dtype)
+
+
+def forward(branches, dtype, sums, w):
     cells, channels = sums[0].shape
-    blocks, _, own, co = w.shape
+    co = w.shape[2]
     n = len(branches)
-    kernel = functools.partial(forward_kernel, branches)
+    steps = 2 if cells % 32 == 0 else 1
+    rows = cells // steps
     return pl.pallas_call(
-        lambda s, *refs: kernel(*refs),
-        grid_spec=pltpu.PrefetchScalarGridSpec(
-            num_scalar_prefetch=1,
-            grid=(blocks,),
-            in_specs=[pl.BlockSpec((1, 2, own, co), lambda d, s: (d, 0, 0, 0))]
-            + [pl.BlockSpec((cells, own), lambda d, s: (0, s[3 + d]))] * n,
-            out_specs=[pl.BlockSpec((cells, co), lambda d, s: (0, 0))] * n,
-            scratch_shapes=[pltpu.VMEM((n, cells, co), F32)],
-        ),
+        functools.partial(forward_kernel, branches),
+        grid=(steps,),
+        in_specs=[pl.BlockSpec(w.shape, lambda i: (0, 0, 0))]
+        + [pl.BlockSpec((rows, channels), lambda i: (i, 0))] * n,
+        out_specs=[pl.BlockSpec((rows, co), lambda i: (i, 0))] * n,
         out_shape=[jax.ShapeDtypeStruct((cells, co), dtype)] * n,
         compiler_params=pltpu.CompilerParams(vmem_limit_bytes=60 << 20),
         cost_estimate=pl.CostEstimate(
@@ -138,7 +124,7 @@
             transcendentals=0,
         ),
         name="forward_terms",
-    )(idx, w, *sums)
+    )(w, *sums)
 
 
 def backward_kernel(terms, slabs, grain, halves, quarters, last, idx_ref, *refs):
@@ -146,14 +132,30 @@
     x_ref, k_ref, w_ref, *refs = refs
     g_refs, d_refs, refs = refs[:n], refs[n : 2 * n], refs[2 * n :]
     if last:
-        f_before, w_before, k_before, f_out, out_ref, gt, gd, kacc, wide = refs
+        f_before, w_before, k_before, f_out, *outs, gt, gd, kacc, wide = refs
     else:
         f_out, w_out, k_out, gt, gd, kacc = refs
-    own, co = w_ref.shape[2:]
+    own, co = w_ref.shape[1:]
     cells = g_refs[0].shape[0]
     size = cells // slabs
     lanes = own // halves
     upper = idx_ref[2] > 0
+    per, seg = 2 * co // quarters, min(2 * co // quarters, co)
+
+    def packed(h, q, rows, value):
+        at_q = q ^ idx_ref[1] if quarters > 1 else 0
+        if halves == 1:
+            outs[0][at_q, 0, rows, :] = value.astype(BF16)
+            return
+        keep = idx_ref[0] == h
+
+        @pl.when(keep)
+        def _():
+            outs[0][at_q, 0, rows, :] = value.astype(BF16)
+
+        @pl.when(jnp.logical_not(keep))
+        def _():
+            outs[1][at_q, 0, rows, :] = value.astype(BF16)
 
     @pl.when(pl.program_id(0) == 0)
     def _():
@@ -161,33 +163,26 @@
             gt[t] = g_refs[t][...].T
 
     kacc[...] = k_before[0] if last else jnp.zeros_like(kacc)
+    for t, (branch, _, _) in enumerate(terms):
+        gd[t] = lax.dot_general(
+            g_refs[t][...], w_ref[branch], (((1,), (1,)), ((), ())), preferred_element_type=F32
+        )
+    for branch in range(2):
+        total = w_before[0, branch] if last else None
+        for t in range(n):
+            if terms[t][0] == branch:
+                part = jnp.dot(gt[t], d_refs[t][...], preferred_element_type=F32)
+                total = part if total is None else total + part
+        if not last:
+            w_out[0, branch] = total
+            continue
+        for j in range(co // seg):
+            q, off = divmod(branch * co + j * seg, per)
+            for h in range(halves):
+                block = total[j * seg : (j + 1) * seg, h * lanes : (h + 1) * lanes]
+                packed(h, q, slice(off, off + seg), block)
     for h in range(halves):
         cols = slice(h * lanes, (h + 1) * lanes)
-        for t, (branch, _, _) in enumerate(terms):
-            gd[h, t] = lax.dot_general(
-                g_refs[t][...],
-                w_ref[0, branch, cols, :],
-                (((1,), (1,)), ((), ())),
-                preferred_element_type=F32,
-            )
-        per = 2 * co // quarters
-        seg = min(per, co)
-        at_h = h ^ idx_ref[0] if halves > 1 else 0
-        for branch in range(2):
-            total = w_before[0, branch, :, cols] if last else None
-            for t in range(n):
-                if terms[t][0] == branch:
-                    part = jnp.dot(gt[t], d_refs[t][:, cols], preferred_element_type=F32)
-                    total = part if total is None else total + part
-            if not last:
-                w_out[0, branch, :, cols] = total
-                continue
-            for j in range(co // seg):
-                q, off = divmod(branch * co + j * seg, per)
-                at_q = q ^ idx_ref[1] if quarters > 1 else 0
-                out_ref[0, at_h, at_q, off : off + seg, :] = total[
-                    j * seg : (j + 1) * seg, :
-                ].astype(BF16)
         sums = [None] * (3 * n)
         for q in range(slabs):
             here = slice(q * size, (q + 1) * size)
@@ -199,7 +194,7 @@
                         continue
                     col = 3 * t + i
                     src = (q - side * reach) * size
-                    part = gd[h, t, src : src + size, :]
+                    part = gd[t, src : src + size, cols]
                     term = part * k_ref[0, col : col + 1, cols]
                     acc = term if acc is None else acc + term
                     prod = jnp.sum((xq * part).reshape(size // 8, 8, lanes), axis=0)
@@ -223,8 +218,7 @@
         if last:
             taps = TAP_ROWS // quarters
             for q in range(quarters):
-                at_q = q ^ idx_ref[1] if quarters > 1 else 0
-                out_ref[0, at_h, at_q, per:, :] = kacc[q * taps : (q + 1) * taps, cols].astype(BF16)
+                packed(h, q, slice(per, None), kacc[q * taps : (q + 1) * taps, cols])
     if last:
         for g in range(wide.shape[0]):
             f_out[g // f_out.shape[1], g % f_out.shape[1]] = wide[g].astype(BF16)
@@ -233,37 +227,39 @@
 
 
 def backward(terms, slabs, grain, halves, quarters, idx, shape, x, k, w, gs, ds, before=None):
-    blocks, _, own, co = w.shape
+    blocks, _, own = k.shape
+    co = w.shape[2]
     cells, channels = x.shape
     images, rows, width, _ = shape
     n = len(terms)
     last = before is not None
-    flat = pl.BlockSpec((cells, own), lambda d, s: (0, s[3 + d]))
+    flat = pl.BlockSpec((cells, own), lambda d, s: (0, d))
     part_w = pl.BlockSpec((1, 2, co, own), lambda d, s: (d, 0, 0, 0))
     part_k = pl.BlockSpec((1, TAP_ROWS, own), lambda d, s: (d, 0, 0))
     in_specs = [
         flat,
         pl.BlockSpec((1,) + k.shape[1:], lambda d, s: (d, 0, 0)),
-        pl.BlockSpec((1, 2, own, co), lambda d, s: (d, 0, 0, 0)),
+        pl.BlockSpec((2, own, co), lambda d, s: (0, d, 0)),
     ]
     in_specs += [pl.BlockSpec((cells, co), lambda d, s: (0, 0))] * n + [flat] * n
     scratch = [
         pltpu.VMEM((n, co, cells), BF16),
-        pltpu.VMEM((halves, n, cells, own // halves), F32),
+        pltpu.VMEM((n, cells, own), F32),
         pltpu.VMEM((TAP_ROWS, own), F32),
     ]
     if last:
         in_specs += [flat, part_w, part_k]
         piece = (2 * co + TAP_ROWS) // quarters
-        packed = (halves, quarters, piece, own // halves)
+        packed = (quarters, blocks, piece, own // halves)
         out_specs = [
             pl.BlockSpec((images, rows, width, own), lambda d, s: (0, 0, 0, s[3 + d])),
-            pl.BlockSpec((1,) + packed, lambda d, s: (d, 0, 0, 0, 0)),
         ]
+        out_specs += [
+            pl.BlockSpec((quarters, 1) + packed[2:], lambda d, s: (0, d, 0, 0))
+        ] * halves
         out_shape = [
             jax.ShapeDtypeStruct(shape, BF16),
-            jax.ShapeDtypeStruct((blocks,) + packed, BF16),
-        ]
+        ] + [jax.ShapeDtypeStruct(packed, BF16)] * halves
         scratch.append(pltpu.VMEM((images * rows, width, own), F32))
     else:
         out_specs = [flat, part_w, part_k]
@@ -374,15 +370,10 @@
 
     taps = depthwise.reshape(18, own)
     k_all = [taps] + [cycle(taps, "dp", d) for d in range(1, dp)]
+    mine = pointwise
     if halves == 2:
         mine = lax.dynamic_slice_in_dim(pointwise, core * part_c, part_c, axis=1)
-        mine = jnp.stack([mine] + [cycle(mine, "dp", d) for d in range(1, dp)])
-        other = swap(mine, "space", 1)
-        low = jnp.where(core == 0, mine, other)
-        high = jnp.where(core == 0, other, mine)
-        w = jnp.concatenate([low, high], axis=2)
-    else:
-        w = jnp.stack([pointwise] + [cycle(pointwise, "dp", d) for d in range(1, dp)])
+    mine = [mine] + [cycle(mine, "dp", d) for d in range(1, dp)]
 
     k_rows = jnp.stack(k_all).astype(F32)
     k_terms = []
@@ -402,13 +393,22 @@
     k_fwd = tap_rows(range(len(terms)))
     k_mid, k_out = tap_rows(middle), tap_rows(outer)
     x, *sums = depthwise_sums(terms, slabs, grain, idx, features, k_fwd)
+    x, sums, mine = lax.optimization_barrier((x, sums, mine))
+    if halves == 2:
+        mine = jnp.stack(mine, axis=1)
+        other = swap(mine, "space", 1)
+        low = jnp.where(core == 0, mine, other)
+        high = jnp.where(core == 0, other, mine)
+        w = jnp.concatenate([low, high], axis=2).reshape(2, channels, co)
+    else:
+        w = jnp.concatenate(mine, axis=1)
     cot = to_slabs(cotangent, grain)
 
     pick = lambda values, chosen: [values[t] for t in chosen]
     parts = [None] * len(terms)
     for chosen, dtype in ((outer, BF16), (middle, F32)):
         branches = [terms[t][0] for t in chosen]
-        for t, part in zip(chosen, forward(branches, dtype, idx, pick(sums, chosen), w)):
+        for t, part in zip(chosen, forward(branches, dtype, pick(sums, chosen), w)):
             parts[t] = part
     received = {t: send(parts[t], t, -1) for t in outer}
 
@@ -431,23 +431,20 @@
     mid_terms, out_terms = pick(terms, middle), pick(terms, outer)
     common = (slabs, grain, halves, quarters, idx, features.shape, x)
     first = backward(mid_terms, *common, k_mid, w, pick(gs, middle), pick(sums, middle))
-    feature_grad, grads = backward(
+    feature_grad, *grads = backward(
         out_terms, *common, k_out, w, pick(gs, outer), pick(sums, outer), first
     )
 
     factor = 1.0 / math.sqrt(dp * n * space * rows * width)
+    kept = grads[0]
     if halves == 2:
-        kept = grads[:, 0].astype(F32) + swap(grads[:, 1], "space", 1).astype(F32)
-        kept = kept.astype(BF16)
-    else:
-        kept = grads[:, 0]
+        kept = (kept.astype(F32) + swap(grads[1], "space", 1).astype(F32)).astype(BF16)
+    total = kept[0]
     if quarters > 1:
-        total = kept[:, 0].astype(F32)
+        total = total.astype(F32)
         for e in range(1, quarters):
-            total = total + swap(kept[:, e], "space", 2 * e).astype(F32)
+            total = total + swap(kept[e], "space", 2 * e).astype(F32)
         total = total.astype(BF16)
-    else:
-        total = kept[:, 0]
     mine = total[0].astype(F32)
     for d in range(1, dp):
         mine = mine + cycle(total[d], "dp", -d).astype(F32)

time: 180 us -> 174 us (0.967)
  waiting for transfers between devices: 49.9 us -> 40.2 us
  Pallas kernels: 64.6 us -> 69.8 us
    ppermute x11, waiting for transfers between devices: 26.5 us -> 11.4 us  [cycle(): lax.ppermute(value, axis, [(i, (i + steps) % count) for i in range(count)])]
    pallas_call x2, Pallas kernels: 32.4 us -> 40.7 us  [backward(): pl.pallas_call(functools.partial(backward_kernel, terms, slabs, grain, ha...]
    pallas_call x2, Pallas kernels: 16.3 us -> 13.4 us  [forward(): pl.pallas_call(functools.partial(forward_kernel, branches), grid=(steps,)...]
    ppermute x4, waiting for transfers between devices: 5.91 us -> 8.62 us  [shift(): lax.ppermute(value, axis, [(i, i + steps) for i in range(first, last)])]
    ppermute x9, waiting for transfers between devices: 17.5 us -> 20.1 us  [swap(): return lax.ppermute(value, axis, [(i, i ^ mask) for i in range(count)])]
    unnamed x32 -> x20, local copies, waits for them, and re-layouts: 5.14 us -> 4.2 us
  transfers between devices with their start and end apart: 24 -> 24, of which waited for: 16 -> 13; matrix products, arithmetic and copies ran while one was open for 4% -> 4% of each run, Pallas kernels for 19% -> 18%
where the time goes in v3:
time: 174 us
  Pallas kernels  69.8 us (40%)
  starting transfers between devices  46.3 us (27%)
  waiting for transfers between devices  40.2 us (23%)
  local copies, waits for them, and re-layouts  9.04 us (5%)
  other arithmetic  7.6 us (4%)
    pallas_call x2, Pallas kernels, backward(): pl.pallas_call(functools.partial(backward_kernel, terms, slabs, grain, ha...  40.7 us
    ppermute x9, waiting for transfers between devices, swap(): return lax.ppermute(value, axis, [(i, i ^ mask) for i in range(count)])  20.1 us
    ppermute x11, starting transfers between devices, cycle(): lax.ppermute(value, axis, [(i, (i + steps) % count) for i in range(count)])  19.7 us
    ppermute x9, starting transfers between devices, swap(): return lax.ppermute(value, axis, [(i, i ^ mask) for i in range(count)])  14.9 us
    pallas_call x2, Pallas kernels, forward(): pl.pallas_call(functools.partial(forward_kernel, branches), grid=(steps,)...  13.4 us
    pallas_call x1, Pallas kernels, depthwise_sums(): pl.pallas_call(lambda s, *refs: kernel(*refs), grid_spec=pltpu.PrefetchSc...  13.3 us
    ppermute x4, starting transfers between devices, shift(): lax.ppermute(value, axis, [(i, i + steps) for i in range(first, last)])  11.7 us
    ppermute x11, waiting for transfers between devices, cycle(): lax.ppermute(value, axis, [(i, (i + steps) % count) for i in range(count)])  11.4 us
  transfers between devices with their start and end apart: 24, of which 13 were waited for; matrix products, arithmetic and copies ran while one was open for 4% of the time, Pallas kernels for 18%

profile of v3, /device:TPU:1, one launch (start us, length us, event | category | flops | bytes accessed | tf_op | source)
XLA Modules:
  0.0 173.8 jit_solution(3208122967967509160)
XLA Ops:
  0.6 0.8 copy.14
  1.4 2.2 %collective-permute-start = (bf16[18,512]{1,0:T(8,128)(2,1)S(1)}, bf16[18,512]{1,0:T(8,128)(2,1)S(1)}, u32[]{:S(2)}, u32[]{:S(2)}) collective-permute-start(bf16[18,512]{1,0:T(8,128)(2,1)S(1)} %reshape.33), channel_id=1, source_target_pairs={{0,1},{1,2},{2,3},{3,0},{4,5},{5,6},{6,7},{7,4},{8,9},{9,10},{10,1... | collective-permute-start | bytes 55304 | tf_op jit(solution)/shard_map/ppermute | solution.py:26
  3.6 2.3 %collective-permute-start.1 = (bf16[18,512]{1,0:T(8,128)(2,1)S(1)}, bf16[18,512]{1,0:T(8,128)(2,1)S(1)}, u32[]{:S(2)}, u32[]{:S(2)}) collective-permute-start(bf16[18,512]{1,0:T(8,128)(2,1)S(1)} %reshape.33), channel_id=1, source_target_pairs={{0,2},{1,3},{2,0},{3,1},{4,6},{5,7},{6,4},{7,5},{8,10},{9,11},{10,... | collective-permute-start | bytes 55304 | tf_op jit(solution)/shard_map/ppermute | solution.py:26
  5.9 1.1 collective-permute-start.2
  7.0 0.5 collective-permute-start.3
  7.5 0.6 pad_add_fusion.s.idx_ref
  8.2 2.9 %collective-permute-start.5 = (bf16[2,256,256]{2,1,0:T(8,128)(2,1)S(1)}, bf16[2,256,256]{2,1,0:T(8,128)(2,1)S(1)}, u32[]{:S(2)}, u32[]{:S(2)}) collective-permute-start(bf16[2,256,256]{2,1,0:T(8,128)(2,1)S(1)} %constant_dynamic-slice_fusion), channel_id=1, source_target_pairs={{0,3},{1,0},{2,1},{3,2},{4,7},{5,4},{6,5},{7,6},{8,11},{9,8},{10,9... | collective-permute-start | bytes 786440 | tf_op jit(solution)/shard_map/ppermute | solution.py:26
  11.1 0.2 concatenate.19
  11.3 0.7 pad.12.refs_1_
  12.0 13.3 %depthwise_sums.1 = (bf16[864,2048]{1,0:T(8,128)(2,1)}, bf16[864,2048]{1,0:T(8,128)(2,1)}, bf16[864,2048]{1,0:T(8,128)(2,1)}, bf16[864,2048]{1,0:T(8,128)(2,1)},...) custom-call(s32[7]{0:T(128)} %pad_add_fusion.s.idx_ref, bf16[2,6,72,2048]{3,2,1,0:T(8,128)(2,1)} %refs_0_.1, ...), custom_call_target="tpu_custom_call" | custom-call | flops 53084160 | bytes 24772608 | tf_op jit(solution)/shard_map/depthwise_sums/pallas_call | solution.py:77
  25.3 2.1 %collective-permute-done.4 = bf16[2,256,256]{2,1,0:T(8,128)(2,1)S(1)} collective-permute-done((bf16[2,256,256]{2,1,0:T(8,128)(2,1)S(1)}, bf16[2,256,256]{2,1,0:T(8,128)(2,1)S(1)}, u32[]{:S(2)}, u32[]{:S(2)}) %collective-permute-start.4) | collective-permute-done | bytes 262176 | tf_op jit(solution)/shard_map/ppermute | solution.py:26
  27.4 0.1 pad_maximum_fusion.1
  27.5 1.7 collective-permute-start.6
  29.2 2.3 %collective-permute-done.6 = bf16[2,4,256,256]{3,2,0,1:T(8,128)(2,1)S(1)} collective-permute-done((bf16[2,4,256,256]{3,2,0,1:T(8,128)(2,1)S(1)}, bf16[2,4,256,256]{3,2,0,1:T(8,128)(2,1)S(1)}, u32[]{:S(2)}, u32[]{:S(2)}) %collective-permute-start.6) | collective-permute-done | bytes 1048608 | tf_op jit(solution)/shard_map/ppermute | solution.py:31
  31.5 0.2 broadcast_select_fusion.1
  31.6 0.1 pad_maximum_fusion
  31.8 1.5 copy.16
  33.3 7.6 %forward_terms.3 = (bf16[864,256]{1,0:T(8,128)(2,1)}, bf16[864,256]{1,0:T(8,128)(2,1)}, bf16[864,256]{1,0:T(8,128)(2,1)}) custom-call(bf16[2,2048,256]{2,1,0:T(8,128)(2,1)} %bitcast.45, bf16[864,2048]{1,0:T(8,128)(2,1)} %get-tuple-element.46.refs_0_.refs_6_, bf16[864,2048]{1,0:T(8,128)(2,1)} %get-tuple-element.47.refs_1_.refs_7_, ...), custom_call_target="tpu_custom_call" | custom-call | flops 2717908992 | bytes 12713984 | tf_op jit(solution)/shard_map/forward_terms/pallas_call | solution.py:113
  40.9 3.1 %collective-permute-start.7 = (bf16[864,256]{1,0:T(8,128)(2,1)}, bf16[864,256]{1,0:T(8,128)(2,1)S(1)}, u32[]{:S(2)}, u32[]{:S(2)}) collective-permute-start(bf16[864,256]{1,0:T(8,128)(2,1)} %get-tuple-element.49), channel_id=1, source_target_pairs={{0,8},{4,12},{8,16},{12,20},{16,24},{20,28},{1,9},{5,13},{9,17},{1... | collective-permute-start | bytes 1327112 | tf_op jit(solution)/shard_map/ppermute | solution.py:21
  44.1 1.3 collective-permute-start.8
  45.4 3.1 %collective-permute-start.9 = (bf16[864,256]{1,0:T(8,128)(2,1)}, bf16[864,256]{1,0:T(8,128)(2,1)}, u32[]{:S(2)}, u32[]{:S(2)}) collective-permute-start(bf16[864,256]{1,0:T(8,128)(2,1)} %get-tuple-element.52), channel_id=1, source_target_pairs={{0,16},{4,20},{8,24},{12,28},{16,0},{20,4},{24,8},{28,12},{1,17},{... | collective-permute-start | bytes 1327112 | tf_op jit(solution)/shard_map/ppermute | solution.py:26
  48.4 0.9 copy.18
  49.3 0.2 copy.19
  49.6 0.2 reshape.38
  49.8 0.7 select_maximum_fusion.refs_1_
  50.5 5.8 %forward_terms.2 = (f32[864,256]{1,0:T(8,128)}, f32[864,256]{1,0:T(8,128)}) custom-call(bf16[2,2048,256]{2,1,0:T(8,128)(2,1)} %bitcast.46, bf16[864,2048]{1,0:T(8,128)(2,1)} %get-tuple-element.43.refs_0_.refs_5_, bf16[864,2048]{1,0:T(8,128)(2,1)} %get-tuple-element.44.refs_1_.refs_6_), custom_call_target="tpu_custom_call" | custom-call | flops 1811939328 | bytes 9175040 | tf_op jit(solution)/shard_map/forward_terms/pallas_call | solution.py:113
  56.2 8.6 %collective-permute-done.8 = bf16[864,256]{1,0:T(8,128)(2,1)S(1)} collective-permute-done((bf16[864,256]{1,0:T(8,128)(2,1)}, bf16[864,256]{1,0:T(8,128)(2,1)S(1)}, u32[]{:S(2)}, u32[]{:S(2)}) %collective-permute-start.8) | collective-permute-done | bytes 442400 | tf_op jit(solution)/shard_map/ppermute | solution.py:21
  64.9 2.4 %multiply_convert_fusion = (bf16[864,256]{1,0:T(8,128)(2,1)S(1)}, bf16[864,256]{1,0:T(8,128)(2,1)S(1)}, bf16[864,256]{1,0:T(8,128)(2,1)S(1)}, bf16[864,256]{1,0:T(8,128)(2,1)S(1)}) fusion(f32[864,256]{1,0:T(8,128)} %get-tuple-element.51, bf16[864,256]{1,0:T(8,128)(2,1)} %collective-permute-done.9, bf16[864,512]{1,0:T(8,128)(2,1)S(1)} %reshape.38, ...), kind=kLoop, calls=%fused_computation.6 | loop fusion | flops 6635520 | bytes 5750784 | tf_op jit(solution)/shard_map/convert_element_type | solution.py:425
  67.3 1.3 collective-permute-start.10
  68.6 6.0 %collective-permute-start.11 = (bf16[864,256]{1,0:T(8,128)(2,1)S(1)}, bf16[864,256]{1,0:T(8,128)(2,1)S(1)}, u32[]{:S(2)}, u32[]{:S(2)}) collective-permute-start(bf16[864,256]{1,0:T(8,128)(2,1)S(1)} %get-tuple-element.80.refs_3_), channel_id=1, source_target_pairs={{0,8},{4,12},{8,16},{12,20},{16,24},{20,28},{1,9},{5,13},{9,17},{1... | collective-permute-start | bytes 1327112 | tf_op jit(solution)/shard_map/ppermute | solution.py:21
  74.6 1.2 collective-permute-start.12
  75.8 0.6 select_maximum_fusion.2.refs_1_
  76.5 12.7 %backward_middle.1 = (f32[864,2048]{1,0:T(8,128)}, f32[4,2,256,512]{3,2,1,0:T(8,128)}, f32[4,32,512]{2,1,0:T(8,128)}) custom-call(s32[7]{0:T(128)} %pad_add_fusion.s.idx_ref, bf16[864,2048]{1,0:T(8,128)(2,1)} %get-tuple-element.53.refs_0_, f32[4,8,512]{2,1,0:T(8,128)} %select_maximum_fusion.2.refs_1_, bf16[2,2048,256]{2,1,0:T(8,128)(2,1)} %bitcast.47, ...), custom_call_target="tpu_custom_call" | custom-call | flops 3623878656 | bytes 17694720 | tf_op jit(solution)/shard_map/backward_middle/pallas_call | solution.py:271
  89.3 3.5 %collective-permute-done.12.refs_5_ = bf16[864,256]{1,0:T(8,128)(2,1)S(1)} collective-permute-done((bf16[864,256]{1,0:T(8,128)(2,1)S(1)}, bf16[864,256]{1,0:T(8,128)(2,1)S(1)}, u32[]{:S(2)}, u32[]{:S(2)}) %collective-permute-start.12) | collective-permute-done | bytes 442400 | tf_op jit(solution)/shard_map/ppermute | solution.py:26
  92.8 0.8 copy-done.7
  93.5 28.0 %backward_outer.1 = (bf16[2,6,72,2048]{3,2,1,0:T(8,128)(2,1)}, bf16[4,4,136,256]{3,2,1,0:T(8,128)(2,1)}, bf16[4,4,136,256]{3,2,1,0:T(8,128)(2,1)}) custom-call(s32[7]{0:T(128)} %pad_add_fusion.s.idx_ref, bf16[864,2048]{1,0:T(8,128)(2,1)} %get-tuple-element.53.refs_0_, f32[4,16,512]{2,1,0:T(8,128)} %select_maximum_fusion.refs_1_, ...), custom_call_target="tpu_custom_call" | custom-call | flops 5435817984 | bytes 21233664 | tf_op jit(solution)/shard_map/backward_outer/pallas_call | solution.py:271
  121.5 3.0 %collective-permute-start.13 = (bf16[4,4,136,256]{3,2,1,0:T(8,128)(2,1)}, bf16[4,4,136,256]{3,2,1,0:T(8,128)(2,1)S(1)}, u32[]{:S(2)}, u32[]{:S(2)}) collective-permute-start(bf16[4,4,136,256]{3,2,1,0:T(8,128)(2,1)} %get-tuple-element.59), channel_id=1, source_target_pairs={{0,4},{4,0},{8,12},{12,8},{16,20},{20,16},{24,28},{28,24},{1,5},{5... | collective-permute-start | bytes 3342344 | tf_op jit(solution)/shard_map/ppermute | solution.py:31
  124.5 2.6 %collective-permute-done.13 = bf16[4,4,136,256]{3,2,1,0:T(8,128)(2,1)S(1)} collective-permute-done((bf16[4,4,136,256]{3,2,1,0:T(8,128)(2,1)}, bf16[4,4,136,256]{3,2,1,0:T(8,128)(2,1)S(1)}, u32[]{:S(2)}, u32[]{:S(2)}) %collective-permute-start.13) | collective-permute-done | bytes 1114144 | tf_op jit(solution)/shard_map/ppermute | solution.py:31
  127.1 1.6 add_convert_fusion
  128.7 0.1 collective-permute-start.14
  128.8 2.3 %collective-permute-start.15 = (bf16[4,136,256]{2,1,0:T(8,128)(2,1)S(1)}, bf16[4,136,256]{2,1,0:T(8,128)(2,1)S(1)}, u32[]{:S(2)}, u32[]{:S(2)}) collective-permute-start(bf16[4,136,256]{2,1,0:T(8,128)(2,1)S(1)} %get-tuple-element.78), channel_id=1, source_target_pairs={{0,16},{4,20},{8,24},{12,28},{16,0},{20,4},{24,8},{28,12},{1,17},{... | collective-permute-start | bytes 835592 | tf_op jit(solution)/shard_map/ppermute | solution.py:31
  131.1 1.1 collective-permute-start.16
  132.2 4.5 %collective-permute-done.14 = bf16[4,136,256]{2,1,0:T(8,128)(2,1)S(1)} collective-permute-done((bf16[4,136,256]{2,1,0:T(8,128)(2,1)S(1)}, bf16[4,136,256]{2,1,0:T(8,128)(2,1)S(1)}, u32[]{:S(2)}, u32[]{:S(2)}) %collective-permute-start.14) | collective-permute-done | bytes 278560 | tf_op jit(solution)/shard_map/ppermute | solution.py:31
  136.6 1.1 collective-permute-done.15
  137.7 6.8 %collective-permute-done.16 = bf16[4,136,256]{2,1,0:T(8,128)(2,1)S(1)} collective-permute-done((bf16[4,136,256]{2,1,0:T(8,128)(2,1)S(1)}, bf16[4,136,256]{2,1,0:T(8,128)(2,1)S(1)}, u32[]{:S(2)}, u32[]{:S(2)}) %collective-permute-start.16) | collective-permute-done | bytes 278560 | tf_op jit(solution)/shard_map/ppermute | solution.py:31
  144.5 0.1 fusion.2
  144.7 5.7 %collective-permute-start.17 = (bf16[136,256]{1,0:T(8,128)(2,1)S(1)}, bf16[136,256]{1,0:T(8,128)(2,1)S(1)}, u32[]{:S(2)}, u32[]{:S(2)}) collective-permute-start(bf16[136,256]{1,0:T(8,128)(2,1)S(1)} %get-tuple-element.83), channel_id=1, source_target_pairs={{0,3},{1,0},{2,1},{3,2},{4,7},{5,4},{6,5},{7,6},{8,11},{9,8},{10,9... | collective-permute-start | bytes 208904 | tf_op jit(solution)/shard_map/ppermute | solution.py:26
  150.4 0.8 collective-permute-start.18
  151.2 0.5 collective-permute-done.17
  151.8 5.3 %collective-permute-done.18 = bf16[136,256]{1,0:T(8,128)(2,1)S(1)} collective-permute-done((bf16[136,256]{1,0:T(8,128)(2,1)S(1)}, bf16[136,256]{1,0:T(8,128)(2,1)S(1)}, u32[]{:S(2)}, u32[]{:S(2)}) %collective-permute-start.18) | collective-permute-done | bytes 69664 | tf_op jit(solution)/shard_map/ppermute | solution.py:26
  157.1 0.4 collective-permute-start.20
  157.5 1.0 collective-permute-start.21
  158.5 1.3 collective-permute-start.22
  159.8 0.5 collective-permute-done.20
  160.4 0.3 collective-permute-done.21
  160.7 2.0 %collective-permute-done.22 = bf16[136,256]{1,0:T(8,128)(2,1)S(1)} collective-permute-done((bf16[136,256]{1,0:T(8,128)(2,1)S(1)}, bf16[136,256]{1,0:T(8,128)(2,1)S(1)}, u32[]{:S(2)}, u32[]{:S(2)}) %collective-permute-start.22) | collective-permute-done | bytes 69664 | tf_op jit(solution)/shard_map/ppermute | solution.py:31
  162.8 4.1 %collective-permute-start.23 = (bf16[4,136,256]{2,1,0:T(8,128)(2,1)S(1)}, bf16[4,136,256]{2,1,0:T(8,128)(2,1)S(1)}, u32[]{:S(2)}, u32[]{:S(2)}) collective-permute-start(bf16[4,136,256]{2,1,0:T(8,128)(2,1)S(1)} %get-tuple-element.82), channel_id=1, source_target_pairs={{0,4},{4,0},{8,12},{12,8},{16,20},{20,16},{24,28},{28,24},{1,5},{5... | collective-permute-start | bytes 835592 | tf_op jit(solution)/shard_map/ppermute | solution.py:31
  166.9 0.2 reshape.35
  167.2 0.9 copy.17
  168.1 1.1 copy.20
  169.1 0.8 pad_maximum_fusion.3.in_ref
  170.0 2.4 %finish_grads.1 = (f32[2,512,256]{2,1,0:T(8,128)}, f32[32,512]{1,0:T(8,128)}) custom-call(s32[7]{0:T(128)} %pad_add_fusion.s.idx_ref, bf16[2,4,136,256]{3,2,1,0:T(8,128)(2,1)} %pad_maximum_fusion.3.in_ref), custom_call_target="tpu_custom_call" | custom-call | tf_op jit(solution)/shard_map/finish_grads/pallas_call | solution.py:310
  172.4 0.8 slice.67
  173.2 0.6 copy.21
  (40 shorter events, 0.5 us)
Async XLA Ops:
  0.6 6.4 %copy-start = (bf16[2,512,256]{2,1,0:T(8,128)(2,1)S(1)}, bf16[2,512,256]{2,1,0:T(8,128)(2,1)}, u32[]{:S(2)}) copy-start(bf16[2,512,256]{2,1,0:T(8,128)(2,1)} %param.5) | copy-start | bytes 1572868
  1.4 6.7 %collective-permute-start = (bf16[18,512]{1,0:T(8,128)(2,1)S(1)}, bf16[18,512]{1,0:T(8,128)(2,1)S(1)}, u32[]{:S(2)}, u32[]{:S(2)}) collective-permute-start(bf16[18,512]{1,0:T(8,128)(2,1)S(1)} %reshape.33), channel_id=1, source_target_pairs={{0,1},{1,2},{2,3},{3,0},{4,5},{5,6},{6,7},{7,4},{8,9},{9,10},{10,1... | collective-permute-start | bytes 55304 | tf_op jit(solution)/shard_map/ppermute | solution.py:26
  3.6 7.4 %collective-permute-start.1 = (bf16[18,512]{1,0:T(8,128)(2,1)S(1)}, bf16[18,512]{1,0:T(8,128)(2,1)S(1)}, u32[]{:S(2)}, u32[]{:S(2)}) collective-permute-start(bf16[18,512]{1,0:T(8,128)(2,1)S(1)} %reshape.33), channel_id=1, source_target_pairs={{0,2},{1,3},{2,0},{3,1},{4,6},{5,7},{6,4},{7,5},{8,10},{9,11},{10,... | collective-permute-start | bytes 55304 | tf_op jit(solution)/shard_map/ppermute | solution.py:26
  5.9 5.1 %collective-permute-start.2 = (bf16[18,512]{1,0:T(8,128)(2,1)S(1)}, bf16[18,512]{1,0:T(8,128)(2,1)S(1)}, u32[]{:S(2)}, u32[]{:S(2)}) collective-permute-start(bf16[18,512]{1,0:T(8,128)(2,1)S(1)} %reshape.33), channel_id=1, source_target_pairs={{0,3},{1,0},{2,1},{3,2},{4,7},{5,4},{6,5},{7,6},{8,11},{9,8},{10,9... | collective-permute-start | bytes 55304 | tf_op jit(solution)/shard_map/ppermute | solution.py:26
  7.0 18.3 %collective-permute-start.3 = (bf16[2,256,256]{2,1,0:T(8,128)(2,1)S(1)}, bf16[2,256,256]{2,1,0:T(8,128)(2,1)S(1)}, u32[]{:S(2)}, u32[]{:S(2)}) collective-permute-start(bf16[2,256,256]{2,1,0:T(8,128)(2,1)S(1)} %constant_dynamic-slice_fusion), channel_id=1, source_target_pairs={{0,1},{1,2},{2,3},{3,0},{4,5},{5,6},{6,7},{7,4},{8,9},{9,10},{10,1... | collective-permute-start | bytes 786440 | tf_op jit(solution)/shard_map/ppermute | solution.py:26
  7.5 19.9 %collective-permute-start.4 = (bf16[2,256,256]{2,1,0:T(8,128)(2,1)S(1)}, bf16[2,256,256]{2,1,0:T(8,128)(2,1)S(1)}, u32[]{:S(2)}, u32[]{:S(2)}) collective-permute-start(bf16[2,256,256]{2,1,0:T(8,128)(2,1)S(1)} %constant_dynamic-slice_fusion), channel_id=1, source_target_pairs={{0,2},{1,3},{2,0},{3,1},{4,6},{5,7},{6,4},{7,5},{8,10},{9,11},{10,... | collective-permute-start | bytes 786440 | tf_op jit(solution)/shard_map/ppermute | solution.py:26
  8.2 19.2 %collective-permute-start.5 = (bf16[2,256,256]{2,1,0:T(8,128)(2,1)S(1)}, bf16[2,256,256]{2,1,0:T(8,128)(2,1)S(1)}, u32[]{:S(2)}, u32[]{:S(2)}) collective-permute-start(bf16[2,256,256]{2,1,0:T(8,128)(2,1)S(1)} %constant_dynamic-slice_fusion), channel_id=1, source_target_pairs={{0,3},{1,0},{2,1},{3,2},{4,7},{5,4},{6,5},{7,6},{8,11},{9,8},{10,9... | collective-permute-start | bytes 786440 | tf_op jit(solution)/shard_map/ppermute | solution.py:26
  27.5 3.9 %collective-permute-start.6 = (bf16[2,4,256,256]{3,2,0,1:T(8,128)(2,1)S(1)}, bf16[2,4,256,256]{3,2,0,1:T(8,128)(2,1)S(1)}, u32[]{:S(2)}, u32[]{:S(2)}) collective-permute-start(bf16[2,4,256,256]{3,2,0,1:T(8,128)(2,1)S(1)} %pad_maximum_fusion.1), channel_id=1, source_target_pairs={{0,4},{4,0},{8,12},{12,8},{16,20},{20,16},{24,28},{28,24},{1,5},{5... | collective-permute-start | bytes 3145736 | tf_op jit(solution)/shard_map/ppermute | solution.py:31
  33.3 15.1 %copy-start.4 = (bf16[2,6,72,512]{3,2,1,0:T(8,128)(2,1)S(1)}, bf16[2,6,72,512]{3,2,1,0:T(8,128)(2,1)}, u32[]{:S(2)}) copy-start(bf16[2,6,72,512]{3,2,1,0:T(8,128)(2,1)} %param.7) | copy-start | bytes 2654212
  40.9 15.3 %collective-permute-start.7 = (bf16[864,256]{1,0:T(8,128)(2,1)}, bf16[864,256]{1,0:T(8,128)(2,1)S(1)}, u32[]{:S(2)}, u32[]{:S(2)}) collective-permute-start(bf16[864,256]{1,0:T(8,128)(2,1)} %get-tuple-element.49), channel_id=1, source_target_pairs={{0,8},{4,12},{8,16},{12,20},{16,24},{20,28},{1,9},{5,13},{9,17},{1... | collective-permute-start | bytes 1327112 | tf_op jit(solution)/shard_map/ppermute | solution.py:21
  44.1 20.8 %collective-permute-start.8 = (bf16[864,256]{1,0:T(8,128)(2,1)}, bf16[864,256]{1,0:T(8,128)(2,1)S(1)}, u32[]{:S(2)}, u32[]{:S(2)}) collective-permute-start(bf16[864,256]{1,0:T(8,128)(2,1)} %get-tuple-element.50), channel_id=1, source_target_pairs={{8,0},{12,4},{16,8},{20,12},{24,16},{28,20},{9,1},{13,5},{17,9},{2... | collective-permute-start | bytes 1327112 | tf_op jit(solution)/shard_map/ppermute | solution.py:21
  45.4 19.5 %collective-permute-start.9 = (bf16[864,256]{1,0:T(8,128)(2,1)}, bf16[864,256]{1,0:T(8,128)(2,1)}, u32[]{:S(2)}, u32[]{:S(2)}) collective-permute-start(bf16[864,256]{1,0:T(8,128)(2,1)} %get-tuple-element.52), channel_id=1, source_target_pairs={{0,16},{4,20},{8,24},{12,28},{16,0},{20,4},{24,8},{28,12},{1,17},{... | collective-permute-start | bytes 1327112 | tf_op jit(solution)/shard_map/ppermute | solution.py:26
  67.3 9.2 %copy-start.2 = (bf16[864,256]{1,0:T(8,128)(2,1)}, bf16[864,256]{1,0:T(8,128)(2,1)S(1)}, u32[]{:S(2)}) copy-start(bf16[864,256]{1,0:T(8,128)(2,1)S(1)} %get-tuple-element.74.refs_4_) | copy-start | bytes 1327108
  67.3 9.2 %copy-start.3 = (bf16[864,256]{1,0:T(8,128)(2,1)}, bf16[864,256]{1,0:T(8,128)(2,1)S(1)}, u32[]{:S(2)}) copy-start(bf16[864,256]{1,0:T(8,128)(2,1)S(1)} %get-tuple-element.80.refs_3_) | copy-start | bytes 1327108
  67.3 21.9 %collective-permute-start.10 = (bf16[864,256]{1,0:T(8,128)(2,1)S(1)}, bf16[864,256]{1,0:T(8,128)(2,1)S(1)}, u32[]{:S(2)}, u32[]{:S(2)}) collective-permute-start(bf16[864,256]{1,0:T(8,128)(2,1)S(1)} %get-tuple-element.80.refs_3_), channel_id=1, source_target_pairs={{8,0},{12,4},{16,8},{20,12},{24,16},{28,20},{9,1},{13,5},{17,9},{2... | collective-permute-start | bytes 1327112 | tf_op jit(solution)/shard_map/ppermute | solution.py:21
  68.6 20.6 %collective-permute-start.11 = (bf16[864,256]{1,0:T(8,128)(2,1)S(1)}, bf16[864,256]{1,0:T(8,128)(2,1)S(1)}, u32[]{:S(2)}, u32[]{:S(2)}) collective-permute-start(bf16[864,256]{1,0:T(8,128)(2,1)S(1)} %get-tuple-element.80.refs_3_), channel_id=1, source_target_pairs={{0,8},{4,12},{8,16},{12,20},{16,24},{20,28},{1,9},{5,13},{9,17},{1... | collective-permute-start | bytes 1327112 | tf_op jit(solution)/shard_map/ppermute | solution.py:21
  74.6 18.2 %collective-permute-start.12 = (bf16[864,256]{1,0:T(8,128)(2,1)S(1)}, bf16[864,256]{1,0:T(8,128)(2,1)S(1)}, u32[]{:S(2)}, u32[]{:S(2)}) collective-permute-start(bf16[864,256]{1,0:T(8,128)(2,1)S(1)} %get-tuple-element.74.refs_4_), channel_id=1, source_target_pairs={{0,16},{4,20},{8,24},{12,28},{16,0},{20,4},{24,8},{28,12},{1,17},{... | collective-permute-start | bytes 1327112 | tf_op jit(solution)/shard_map/ppermute | solution.py:26
  89.2 3.5 %copy-start.5 = (bf16[864,256]{1,0:T(8,128)(2,1)}, bf16[864,256]{1,0:T(8,128)(2,1)S(1)}, u32[]{:S(2)}) copy-start(bf16[864,256]{1,0:T(8,128)(2,1)S(1)} %collective-permute-done.10.refs_3_) | copy-start | bytes 1327108
  89.2 3.5 %copy-start.6 = (bf16[864,256]{1,0:T(8,128)(2,1)}, bf16[864,256]{1,0:T(8,128)(2,1)S(1)}, u32[]{:S(2)}) copy-start(bf16[864,256]{1,0:T(8,128)(2,1)S(1)} %collective-permute-done.11.refs_4_) | copy-start | bytes 1327108
  92.8 0.8 copy-start.7
  121.5 5.6 %collective-permute-start.13 = (bf16[4,4,136,256]{3,2,1,0:T(8,128)(2,1)}, bf16[4,4,136,256]{3,2,1,0:T(8,128)(2,1)S(1)}, u32[]{:S(2)}, u32[]{:S(2)}) collective-permute-start(bf16[4,4,136,256]{3,2,1,0:T(8,128)(2,1)} %get-tuple-element.59), channel_id=1, source_target_pairs={{0,4},{4,0},{8,12},{12,8},{16,20},{20,16},{24,28},{28,24},{1,5},{5... | collective-permute-start | bytes 3342344 | tf_op jit(solution)/shard_map/ppermute | solution.py:31
  128.7 7.9 %collective-permute-start.14 = (bf16[4,136,256]{2,1,0:T(8,128)(2,1)S(1)}, bf16[4,136,256]{2,1,0:T(8,128)(2,1)S(1)}, u32[]{:S(2)}, u32[]{:S(2)}) collective-permute-start(bf16[4,136,256]{2,1,0:T(8,128)(2,1)S(1)} %get-tuple-element.76), channel_id=1, source_target_pairs={{0,8},{4,12},{8,0},{12,4},{16,24},{20,28},{24,16},{28,20},{1,9},{5... | collective-permute-start | bytes 835592 | tf_op jit(solution)/shard_map/ppermute | solution.py:31
  128.8 8.9 %collective-permute-start.15 = (bf16[4,136,256]{2,1,0:T(8,128)(2,1)S(1)}, bf16[4,136,256]{2,1,0:T(8,128)(2,1)S(1)}, u32[]{:S(2)}, u32[]{:S(2)}) collective-permute-start(bf16[4,136,256]{2,1,0:T(8,128)(2,1)S(1)} %get-tuple-element.78), channel_id=1, source_target_pairs={{0,16},{4,20},{8,24},{12,28},{16,0},{20,4},{24,8},{28,12},{1,17},{... | collective-permute-start | bytes 835592 | tf_op jit(solution)/shard_map/ppermute | solution.py:31
  131.1 13.4 %collective-permute-start.16 = (bf16[4,136,256]{2,1,0:T(8,128)(2,1)S(1)}, bf16[4,136,256]{2,1,0:T(8,128)(2,1)S(1)}, u32[]{:S(2)}, u32[]{:S(2)}) collective-permute-start(bf16[4,136,256]{2,1,0:T(8,128)(2,1)S(1)} %get-tuple-element.77), channel_id=1, source_target_pairs={{0,24},{4,28},{8,16},{12,20},{16,8},{20,12},{24,0},{28,4},{1,25},{... | collective-permute-start | bytes 835592 | tf_op jit(solution)/shard_map/ppermute | solution.py:31
  144.7 7.1 %collective-permute-start.17 = (bf16[136,256]{1,0:T(8,128)(2,1)S(1)}, bf16[136,256]{1,0:T(8,128)(2,1)S(1)}, u32[]{:S(2)}, u32[]{:S(2)}) collective-permute-start(bf16[136,256]{1,0:T(8,128)(2,1)S(1)} %get-tuple-element.83), channel_id=1, source_target_pairs={{0,3},{1,0},{2,1},{3,2},{4,7},{5,4},{6,5},{7,6},{8,11},{9,8},{10,9... | collective-permute-start | bytes 208904 | tf_op jit(solution)/shard_map/ppermute | solution.py:26
  150.4 6.7 %collective-permute-start.18 = (bf16[136,256]{1,0:T(8,128)(2,1)S(1)}, bf16[136,256]{1,0:T(8,128)(2,1)S(1)}, u32[]{:S(2)}, u32[]{:S(2)}) collective-permute-start(bf16[136,256]{1,0:T(8,128)(2,1)S(1)} %get-tuple-element.85), channel_id=1, source_target_pairs={{0,2},{1,3},{2,0},{3,1},{4,6},{5,7},{6,4},{7,5},{8,10},{9,11},{10,... | collective-permute-start | bytes 208904 | tf_op jit(solution)/shard_map/ppermute | solution.py:26
  151.2 5.9 %collective-permute-start.19 = (bf16[136,256]{1,0:T(8,128)(2,1)S(1)}, bf16[136,256]{1,0:T(8,128)(2,1)S(1)}, u32[]{:S(2)}, u32[]{:S(2)}) collective-permute-start(bf16[136,256]{1,0:T(8,128)(2,1)S(1)} %get-tuple-element.84), channel_id=1, source_target_pairs={{0,1},{1,2},{2,3},{3,0},{4,5},{5,6},{6,7},{7,4},{8,9},{9,10},{10,1... | collective-permute-start | bytes 208904 | tf_op jit(solution)/shard_map/ppermute | solution.py:26
  157.1 3.2 %collective-permute-start.20 = (bf16[136,256]{1,0:T(8,128)(2,1)S(1)}, bf16[136,256]{1,0:T(8,128)(2,1)S(1)}, u32[]{:S(2)}, u32[]{:S(2)}) collective-permute-start(bf16[136,256]{1,0:T(8,128)(2,1)S(1)} %fusion.5), channel_id=1, source_target_pairs={{0,8},{4,12},{8,0},{12,4},{16,24},{20,28},{24,16},{28,20},{1,9},{5... | collective-permute-start | bytes 208904 | tf_op jit(solution)/shard_map/ppermute | solution.py:31
  157.5 3.2 %collective-permute-start.21 = (bf16[136,256]{1,0:T(8,128)(2,1)S(1)}, bf16[136,256]{1,0:T(8,128)(2,1)S(1)}, u32[]{:S(2)}, u32[]{:S(2)}) collective-permute-start(bf16[136,256]{1,0:T(8,128)(2,1)S(1)} %fusion.5), channel_id=1, source_target_pairs={{0,16},{4,20},{8,24},{12,28},{16,0},{20,4},{24,8},{28,12},{1,17},{... | collective-permute-start | bytes 208904 | tf_op jit(solution)/shard_map/ppermute | solution.py:31
  158.5 4.2 %collective-permute-start.22 = (bf16[136,256]{1,0:T(8,128)(2,1)S(1)}, bf16[136,256]{1,0:T(8,128)(2,1)S(1)}, u32[]{:S(2)}, u32[]{:S(2)}) collective-permute-start(bf16[136,256]{1,0:T(8,128)(2,1)S(1)} %fusion.5), channel_id=1, source_target_pairs={{0,24},{4,28},{8,16},{12,20},{16,8},{20,12},{24,0},{28,4},{1,25},{... | collective-permute-start | bytes 208904 | tf_op jit(solution)/shard_map/ppermute | solution.py:31
  162.8 6.3 %collective-permute-start.23 = (bf16[4,136,256]{2,1,0:T(8,128)(2,1)S(1)}, bf16[4,136,256]{2,1,0:T(8,128)(2,1)S(1)}, u32[]{:S(2)}, u32[]{:S(2)}) collective-permute-start(bf16[4,136,256]{2,1,0:T(8,128)(2,1)S(1)} %get-tuple-element.82), channel_id=1, source_target_pairs={{0,4},{4,0},{8,12},{12,8},{16,20},{20,16},{24,28},{28,24},{1,5},{5... | collective-permute-start | bytes 835592 | tf_op jit(solution)/shard_map/ppermute | solution.py:31
  167.1 6.7 %copy-start.1 = (bf16[2,512,256]{2,1,0:T(8,128)(2,1)S(1)}, bf16[2,512,256]{2,1,0:T(8,128)(2,1)}, u32[]{:S(2)}) copy-start(bf16[2,512,256]{2,1,0:T(8,128)(2,1)} %param.5) | copy-start | bytes 1572868

commit v4 on v3

v4 whole, which is shorter than its diff:
```python
import functools
import math

import jax
import jax.numpy as jnp
from jax import lax
from jax.experimental import pallas as pl
from jax.experimental.pallas import tpu as pltpu
from jax.sharding import PartitionSpec as P


RATES = (12, 24)
SIDES = (-1, 0, 1)
F32 = jnp.float32
BF16 = jnp.bfloat16
TAP_ROWS = 32


def shift(value, axis, steps):
    count = lax.axis_size(axis)
    first, last = max(0, -steps), min(count, count - steps)
    return lax.ppermute(value, axis, [(i, i + steps) for i in range(first, last)])


def cycle(value, axis, steps):
    count = lax.axis_size(axis)
    return lax.ppermute(value, axis, [(i, (i + steps) % count) for i in range(count)])


def swap(value, axis, mask):
    count = lax.axis_size(axis)
    return lax.ppermute(value, axis, [(i, i ^ mask) for i in range(count)])


def to_slabs(field, grain):
    n, rows, width, ch = field.shape
    parts = field.reshape(n, rows, width // grain, grain, ch)
    return parts.transpose(2, 0, 1, 3, 4).reshape(-1, ch)


def from_slabs(flat, shape, grain):
    n, rows, width, ch = shape
    parts = flat.reshape(width // grain, n, rows, grain, ch)
    return parts.transpose(1, 2, 0, 3, 4).reshape(shape)


def span(slabs, q, side, reach):
    return 0 <= q + side * reach < slabs


def sums_kernel(terms, slabs, grain, x_ref, k_ref, xs_ref, *refs):
    outs, wide = refs[: len(terms)], refs[len(terms)]
    n, rows = x_ref.shape[:2]
    size = n * rows * grain
    for g in range(n * rows):
        line = x_ref[g // rows, g % rows].astype(F32)
        for q in range(slabs):
            at = q * size + g * grain
            wide[at : at + grain, :] = line[q * grain : (q + 1) * grain, :]
    xs_ref[...] = wide[...].astype(BF16)
    for t, (_, _, reach) in enumerate(terms):
        taps = [k_ref[0, 3 * t + i : 3 * t + i + 1, :] for i in range(3)]
        for q in range(slabs):
            total = None
            for i, side in enumerate(SIDES):
                if span(slabs, q, side, reach):
                    src = (q + side * reach) * size
                    term = wide[src : src + size, :] * taps[i]
                    total = term if total is None else total + term
            outs[t][q * size : (q + 1) * size, :] = total.astype(BF16)


def depthwise_sums(terms, slabs, grain, idx, x, k):
    n, rows, width, channels = x.shape
    cells, (blocks, _, own) = n * rows * width, k.shape
    flat = pl.BlockSpec((cells, own), lambda d, s: (0, d))
    kernel = functools.partial(sums_kernel, terms, slabs, grain)
    return pl.pallas_call(
        lambda s, *refs: kernel(*refs),
        grid_spec=pltpu.PrefetchScalarGridSpec(
            num_scalar_prefetch=1,
            grid=(blocks,),
            in_specs=[
                pl.BlockSpec((n, rows, width, own), lambda d, s: (0, 0, 0, s[3 + d])),
                pl.BlockSpec((1, k.shape[1], own), lambda d, s: (d, 0, 0)),
            ],
            out_specs=[flat] * (1 + len(terms)),
            scratch_shapes=[pltpu.VMEM((cells, own), F32)],
        ),
        out_shape=[jax.ShapeDtypeStruct((cells, channels), BF16)] * (1 + len(terms)),
        compiler_params=pltpu.CompilerParams(vmem_limit_bytes=60 << 20),
        cost_estimate=pl.CostEstimate(
            flops=6 * len(terms) * cells * channels,
            bytes_accessed=2 * (2 + len(terms)) * cells * channels,
            transcendentals=0,
        ),
        name="depthwise_sums",
    )(idx, x, k)


def forward_kernel(branches, w_ref, *refs):
    n = len(branches)
    for t, branch in enumerate(branches):
        part = jnp.dot(refs[t][...], w_ref[branch], preferred_element_type=F32)
        refs[n + t][...] = part.astype(refs[n + t].dtype)


def forward(branches, dtypes, sums, w):
    cells, channels = sums[0].shape
    co = w.shape[2]
    n = len(branches)
    steps = 2 if cells % 32 == 0 else 1
    rows = cells // steps
    only = branches[0]
    if set(branches) == {only}:
        w_spec = pl.BlockSpec((1,) + w.shape[1:], lambda i: (only, 0, 0))
        branches = [0] * n
    else:
        w_spec = pl.BlockSpec(w.shape, lambda i: (0, 0, 0))
    return pl.pallas_call(
        functools.partial(forward_kernel, branches),
        grid=(steps,),
        in_specs=[w_spec] + [pl.BlockSpec((rows, channels), lambda i: (i, 0))] * n,
        out_specs=[pl.BlockSpec((rows, co), lambda i: (i, 0))] * n,
        out_shape=[jax.ShapeDtypeStruct((cells, co), dt) for dt in dtypes],
        compiler_params=pltpu.CompilerParams(vmem_limit_bytes=60 << 20),
        cost_estimate=pl.CostEstimate(
            flops=2 * n * cells * channels * co,
            bytes_accessed=2 * n * cells * channels + 2 * channels * co,
            transcendentals=0,
        ),
        name="forward_terms",
    )(w, *sums)


def back(g, weight):
    return lax.dot_general(g, weight, (((1,), (1,)), ((), ())), preferred_element_type=F32)


def weight_kernel(terms, slabs, halves, quarters, last, idx_ref, x_ref, w_ref, *refs):
    n = len(terms)
    g_refs, d_refs, refs = refs[:n], refs[n : 2 * n], refs[2 * n :]
    if last:
        w_before, k_before, *outs, gt, gd, kacc, pieces = refs
    else:
        w_out, k_out, gt, gd, kacc = refs
    own, co = w_ref.shape[1:]
    size = g_refs[0].shape[0] // slabs
    lanes = own // halves

    @pl.when(pl.program_id(0) == 0)
    def _():
        for t in range(n):
            gt[t] = g_refs[t][...].T

    for t in range(n):
        gd[t] = back(g_refs[t][...], w_ref[0])
    total = w_before[0] if last else None
    for t in range(n):
        part = jnp.dot(gt[t], d_refs[t][...], preferred_element_type=F32)
        total = part if total is None else total + part
    per = co // quarters
    if last:
        for h in range(halves):
            for q in range(quarters):
                block = total[q * per : (q + 1) * per, h * lanes : (h + 1) * lanes]
                pieces[h, q, :per, :] = block.astype(BF16)
    else:
        w_out[0] = total
    kacc[...] = k_before[0] if last else jnp.zeros_like(kacc)
    upper = idx_ref[2] > 0
    for h in range(halves):
        cols = slice(h * lanes, (h + 1) * lanes)
        sums = [None] * (3 * n)
        for q in range(slabs):
            xq = x_ref[q * size : (q + 1) * size, cols].astype(F32)
            for t, (_, _, reach) in enumerate(terms):
                for i, side in enumerate(SIDES):
                    if not span(slabs, q, -side, reach):
                        continue
                    src = (q - side * reach) * size
                    part = xq * gd[t, src : src + size, cols]
                    part = jnp.sum(part.reshape(size // 8, 8, lanes), axis=0)
                    at = 3 * t + i
                    sums[at] = part if sums[at] is None else sums[at] + part
        for t, (_, u, _) in enumerate(terms):
            for i in range(3):
                total = jnp.sum(sums[3 * t + i], axis=0, keepdims=True)
                if u is None:
                    kacc[i : i + 1, cols] = jnp.where(upper, 0.0, total)
                    kacc[i + 6 : i + 7, cols] = jnp.where(upper, total, 0.0)
                else:
                    row = 3 * (u + 1) + i
                    kacc[row : row + 1, cols] = total
    if not last:
        k_out[0] = kacc[...]
        return
    taps = TAP_ROWS // quarters
    for h in range(halves):
        for q in range(quarters):
            block = kacc[q * taps : (q + 1) * taps, h * lanes : (h + 1) * lanes]
            pieces[h, q, per:, :] = block.astype(BF16)
    for e in range(quarters):
        at = e ^ idx_ref[1] if quarters > 1 else 0
        if halves == 1:
            outs[0][e, 0] = pieces[0, at]
        else:
            outs[0][e, 0] = pieces[idx_ref[0], at]
            outs[1][e, 0] = pieces[1 - idx_ref[0], at]


def weight_grads(terms, slabs, halves, quarters, blocks, idx, x, w, gs, ds, before=None):
    cells, channels = x.shape
    own, co = channels // blocks, w.shape[2]
    n, branch = len(terms), terms[0][0]
    last = before is not None
    flat = pl.BlockSpec((cells, own), lambda d, s: (0, d))
    part_w = pl.BlockSpec((1, co, own), lambda d, s: (d, 0, 0))
    part_k = pl.BlockSpec((1, TAP_ROWS, own), lambda d, s: (d, 0, 0))
    in_specs = [flat, pl.BlockSpec((1, own, co), lambda d, s: (branch, d, 0))]
    in_specs += [pl.BlockSpec((cells, co), lambda d, s: (0, 0))] * n + [flat] * n
    scratch = [
        pltpu.VMEM((n, co, cells), BF16),
        pltpu.VMEM((n, cells, own), F32),
        pltpu.VMEM((TAP_ROWS, own), F32),
    ]
    if last:
        in_specs += [part_w, part_k]
        piece = ((co + TAP_ROWS) // quarters, own // halves)
        out_specs = [pl.BlockSpec((quarters, 1) + piece, lambda d, s: (0, d, 0, 0))] * halves
        out_shape = [jax.ShapeDtypeStruct((quarters, blocks) + piece, BF16)] * halves
        scratch.append(pltpu.VMEM((halves, quarters) + piece, BF16))
    else:
        out_specs = [part_w, part_k]
        out_shape = [
            jax.ShapeDtypeStruct((blocks, co, own), F32),
            jax.ShapeDtypeStruct((blocks, TAP_ROWS, own), F32),
        ]
    return pl.pallas_call(
        functools.partial(weight_kernel, terms, slabs, halves, quarters, last),
        grid_spec=pltpu.PrefetchScalarGridSpec(
            num_scalar_prefetch=1,
            grid=(blocks,),
            in_specs=in_specs,
            out_specs=out_specs,
            scratch_shapes=scratch,
        ),
        out_shape=out_shape,
        compiler_params=pltpu.CompilerParams(vmem_limit_bytes=60 << 20),
        cost_estimate=pl.CostEstimate(
            flops=4 * n * cells * channels * co,
            bytes_accessed=2 * (n + 1) * cells * channels + 6 * channels * co,
            transcendentals=0,
        ),
        name="weight_outer" if last else "weight_middle",
    )(idx, x, w, *gs, *ds, *(before or ()))


def feature_kernel(terms, slabs, grain, k_ref, w_ref, *refs):
    n = len(terms)
    g_refs, (out_ref, gd, wide) = refs[:n], refs[n:]
    size = g_refs[0].shape[0] // slabs
    own = w_ref.shape[1]
    for t, (branch, _, _) in enumerate(terms):
        gd[t] = back(g_refs[t][...], w_ref[branch])
    lanes = own // 2 if own % 256 == 0 else own
    for h in range(own // lanes):
        cols = slice(h * lanes, (h + 1) * lanes)
        for q in range(slabs):
            acc = None
            for t, (_, _, reach) in enumerate(terms):
                for i, side in enumerate(SIDES):
                    if not span(slabs, q, -side, reach):
                        continue
                    src = (q - side * reach) * size
                    term = gd[t, src : src + size, cols] * k_ref[0, 3 * t + i : 3 * t + i + 1, cols]
                    acc = term if acc is None else acc + term
            for g in range(wide.shape[0]):
                wide[g, q * grain : (q + 1) * grain, cols] = acc[g * grain : (g + 1) * grain, :]
    rows = out_ref.shape[1]
    for g in range(wide.shape[0]):
        out_ref[g // rows, g % rows] = wide[g].astype(BF16)


def feature_grads(terms, slabs, grain, idx, shape, k, w, gs):
    images, rows, width, channels = shape
    blocks, _, own = k.shape
    cells, co = gs[0].shape
    n = len(terms)
    kernel = functools.partial(feature_kernel, terms, slabs, grain)
    return pl.pallas_call(
        lambda s, *refs: kernel(*refs),
        grid_spec=pltpu.PrefetchScalarGridSpec(
            num_scalar_prefetch=1,
            grid=(blocks,),
            in_specs=[
                pl.BlockSpec((1,) + k.shape[1:], lambda d, s: (d, 0, 0)),
                pl.BlockSpec((2, own, co), lambda d, s: (0, d, 0)),
            ]
            + [pl.BlockSpec((cells, co), lambda d, s: (0, 0))] * n,
            out_specs=pl.BlockSpec((images, rows, width, own), lambda d, s: (0, 0, 0, s[3 + d])),
            scratch_shapes=[
                pltpu.VMEM((n, cells, own), F32),
                pltpu.VMEM((images * rows, width, own), F32),
            ],
        ),
        out_shape=jax.ShapeDtypeStruct(shape, BF16),
        compiler_params=pltpu.CompilerParams(vmem_limit_bytes=60 << 20),
        cost_estimate=pl.CostEstimate(
            flops=2 * n * cells * channels * co,
            bytes_accessed=4 * cells * channels,
            transcendentals=0,
        ),
        name="feature_grads",
    )(idx, k, w, *gs)


def finish_kernel(factor, halves, quarters, idx_ref, in_ref, w_ref, k_ref, wide, taps_of):
    co = w_ref.shape[2]
    per, taps = co // quarters, TAP_ROWS // quarters
    lanes = in_ref.shape[4]
    for branch in range(2):
        for h in range(halves):
            at_h = h ^ idx_ref[0] if halves > 1 else 0
            cols = slice(h * lanes, (h + 1) * lanes)
            for q in range(quarters):
                at_q = q ^ idx_ref[1] if quarters > 1 else 0
                block = in_ref[at_h, at_q, branch].astype(F32) * factor
                wide[q * per : (q + 1) * per, cols] = block[:per]
                taps_of[q * taps : (q + 1) * taps, cols] = block[per:]
        w_ref[branch] = wide[...].T
        k_ref[branch] = taps_of[: k_ref.shape[1], :]


def finish(idx, pieces, own, factor):
    halves, quarters, _, rows, _ = pieces.shape
    co = rows * quarters - TAP_ROWS
    return pl.pallas_call(
        functools.partial(finish_kernel, factor, halves, quarters),
        in_specs=[
            pl.BlockSpec(memory_space=pltpu.SMEM),
            pl.BlockSpec(memory_space=pltpu.VMEM),
        ],
        out_specs=[pl.BlockSpec(memory_space=pltpu.VMEM)] * 2,
        out_shape=[
            jax.ShapeDtypeStruct((2, own, co), F32),
            jax.ShapeDtypeStruct((2, 9, own), F32),
        ],
        scratch_shapes=[pltpu.VMEM((co, own), F32), pltpu.VMEM((TAP_ROWS, own), F32)],
        name="finish_grads",
    )(idx, pieces)


def pyramid(features, pointwise, depthwise, cotangent):
    n, rows, width, channels = features.shape
    own, co = pointwise.shape[1:]
    space, dp = lax.axis_size("space"), lax.axis_size("dp")
    me, row = lax.axis_index("space"), lax.axis_index("dp")
    chips = space // 2
    halves = 2 if space % 2 == 0 and own % 256 == 0 else 1
    part_c = own // halves
    even = chips & (chips - 1) == 0 and TAP_ROWS % (8 * chips) == 0 and co % (16 * chips) == 0
    quarters = chips if halves == 2 and even else 1
    core, chip = me % 2, me // 2

    grain = math.gcd(*RATES)
    slabs = width // grain

    terms, moves = [], []
    for branch, rate in enumerate(RATES):
        offset, reach = rate // rows, rate // grain
        terms.append((branch, 0, reach))
        moves.append(0)
        if 2 * offset == space:
            terms.append((branch, None, reach))
            moves.append(offset)
        elif offset < space:
            for u in (-1, 1):
                terms.append((branch, u, reach))
                moves.append(u * offset)
    middle = [t for t, m in enumerate(moves) if m == 0]
    outer = [t for t, m in enumerate(moves) if m != 0]
    half_way = next((moves[t] for t in outer if terms[t][1] is None), space)
    upper = (me >= half_way).astype(jnp.int32)

    def send(value, t, direction):
        if terms[t][1] is None:
            return cycle(value, "space", moves[t])
        return shift(value, "space", direction * moves[t])

    idx = jnp.concatenate(
        [
            jnp.stack([core, chip, upper]).astype(jnp.int32),
            (row + dp - jnp.arange(dp)).astype(jnp.int32) % dp,
        ]
    )

    taps = depthwise.reshape(18, own)
    k_all = [taps] + [cycle(taps, "dp", d) for d in range(1, dp)]
    mine = pointwise
    if halves == 2:
        mine = lax.dynamic_slice_in_dim(pointwise, core * part_c, part_c, axis=1)
    mine = [mine] + [cycle(mine, "dp", d) for d in range(1, dp)]

    k_rows = jnp.stack(k_all).astype(F32)
    k_terms = []
    for branch, u, _ in terms:
        at = branch * 9
        if u is None:
            k_terms.append(
                jnp.where(upper > 0, k_rows[:, at + 6 : at + 9], k_rows[:, at : at + 3])
            )
        else:
            k_terms.append(k_rows[:, at + 3 * (u + 1) : at + 3 * (u + 1) + 3])

    taps_all = jnp.concatenate(k_terms, axis=1)
    taps_all = jnp.pad(taps_all, ((0, 0), (0, -taps_all.shape[1] % 8), (0, 0)))

    x, *sums = depthwise_sums(terms, slabs, grain, idx, features, taps_all)
    x, sums, mine = lax.optimization_barrier((x, sums, mine))
    if halves == 2:
        mine = jnp.stack(mine, axis=1)
        other = swap(mine, "space", 1)
        low = jnp.where(core == 0, mine, other)
        high = jnp.where(core == 0, other, mine)
        w = jnp.concatenate([low, high], axis=2).reshape(2, channels, co)
    else:
        w = jnp.concatenate(mine, axis=1)

    held = lax.optimization_barrier
    pick = lambda values, chosen: [values[t] for t in chosen]
    mid = [[t for t in middle if terms[t][0] == b] for b in range(2)]
    out = [[t for t in outer if terms[t][0] == b] for b in range(2)]
    cot = to_slabs(cotangent, grain)

    order = (1, 0)
    parts, received, outputs, gs = [None] * len(terms), {}, [None] * 2, [None] * len(terms)
    for b in order:
        count = len(out[b])
        for t, part in zip(out[b], forward([b] * count, [BF16] * count, pick(sums, out[b]), w)):
            parts[t] = part
        received[b] = [send(parts[t], t, -1) for t in out[b]]
        if b == order[0]:
            _, sums = held((pick(parts, out[b]), sums))
    chosen = mid[1] + mid[0]
    centre = forward([terms[t][0] for t in chosen], [F32] * 2, pick(sums, chosen), w)
    for t, part in zip(chosen, centre):
        parts[t] = part

    common = (slabs, halves, quarters, dp, idx, x, w)
    first, grads, summed = [None] * 2, [None] * 2, [None] * 2
    for b in order:
        t = mid[b][0]
        if b == order[1]:
            received[b], first[order[0]] = held((received[b], first[order[0]]))
        pre = parts[t]
        for other in received[b]:
            pre = pre + other.astype(F32)
        sig = jax.nn.sigmoid(pre)
        outputs[b] = (pre * sig).astype(BF16)
        cot_part = cot[:, b * co : (b + 1) * co].astype(F32)
        gs[t] = (cot_part * sig * (1.0 + pre * (1.0 - sig))).astype(BF16)
        for o in out[b]:
            gs[o] = send(gs[t], o, 1)
        first[b] = weight_grads(pick(terms, mid[b]), *common, pick(gs, mid[b]), pick(sums, mid[b]))
    last_g = pick(gs, out[order[1]])
    for b in order:
        if b == order[0]:
            grad_g = pick(gs, out[b])
            grad_g, first[order[1]] = held((grad_g, first[order[1]]))
        else:
            grad_g = last_g
        grads[b] = weight_grads(pick(terms, out[b]), *common, grad_g, pick(sums, out[b]), first[b])
        kept = grads[b][0]
        if halves == 2:
            kept = (kept.astype(F32) + swap(grads[b][1], "space", 1).astype(F32)).astype(BF16)
        if b == order[0]:
            last_g, kept = held((last_g, kept))
        else:
            gs, kept = held((gs, kept))
        summed[b] = [kept[0]] + [swap(kept[e], "space", 2 * e) for e in range(1, quarters)]
    feature_grad = feature_grads(terms, slabs, grain, idx, features.shape, taps_all, w, gs)
    branches_out = from_slabs(jnp.concatenate(outputs, axis=-1), cotangent.shape, grain)

    factor = 1.0 / math.sqrt(dp * n * space * rows * width)
    total = jnp.stack([sum(p.astype(F32) for p in pieces) for pieces in summed], axis=1)
    total = total.astype(BF16)
    mine = total[0].astype(F32)
    for d in range(1, dp):
        mine = mine + cycle(total[d], "dp", -d).astype(F32)
    if quarters > 1:
        mine = mine.astype(BF16)
        block = jnp.stack([mine] + [swap(mine, "space", 2 * e) for e in range(1, quarters)])
    else:
        peers = [[i for i in range(space) if i % halves == c] for c in range(halves)]
        block = lax.psum(mine, "space", axis_index_groups=peers)[None]
    block = jnp.stack([block, swap(block, "space", 1)]) if halves == 2 else block[None]
    pointwise_grad, depthwise_grad = finish(idx, block, own, factor)
    return branches_out, feature_grad, pointwise_grad, depthwise_grad


def solution(mesh):
    return jax.shard_map(
        pyramid,
        mesh=mesh,
        in_specs=(
            P("dp", "space", None, None),
            P(None, "dp", None),
            P(None, None, "dp"),
            P("dp", "space", None, None),
        ),
        out_specs=(
            P("dp", "space", None, None),
            P("dp", "space", None, None),
            P(None, "dp", None),
            P(None, None, "dp"),
        ),
        check_vma=False,
    )
```

time: 174 us -> 182 us (1.046)
  waiting for transfers between devices: 40.2 us -> 28.4 us
  Pallas kernels: 69.8 us -> 79 us
  starting transfers between devices: 46.3 us -> 54.1 us
    ppermute x9 -> x13, starting transfers between devices: 14.9 us -> 25.5 us  [swap(): return lax.ppermute(value, axis, [(i, i ^ mask) for i in range(count)])]
    ppermute x9 -> x13, waiting for transfers between devices: 20.1 us -> 10.9 us  [swap(): return lax.ppermute(value, axis, [(i, i ^ mask) for i in range(count)])]
    pallas_call x2 -> x5, Pallas kernels: 40.7 us -> 48.4 us  [the longest x4 35.1 us: weight_grads(): pl.pallas_call(functools.partial(weight_kernel, terms, slabs, halves, qua...]
    ppermute x11, waiting for transfers between devices: 11.4 us -> 8.37 us  [cycle(): lax.ppermute(value, axis, [(i, (i + steps) % count) for i in range(count)])]
    convert_element_type x5 -> x6, other arithmetic: 4.21 us -> 6.29 us  [the longest x2 3.81 us: pyramid(): gs[t] = (cot_part * sig * (1.0 + pre * (1.0 - sig))).astype(BF16)]
    unnamed x20 -> x22, local copies, waits for them, and re-layouts: 4.2 us -> 5.81 us
    pallas_call x2 -> x3, Pallas kernels: 13.4 us -> 14.8 us  [forward(): pl.pallas_call(functools.partial(forward_kernel, branches), grid=(steps,)...]
  transfers between devices with their start and end apart: 24 -> 28, of which waited for: 13 -> 13; matrix products, arithmetic and copies ran while one was open for 4% -> 6% of each run, Pallas kernels for 18% -> 29%
where the time goes in v4:
time: 182 us; the launch traced here: 181 us
  Pallas kernels  79 us (43%)
  starting transfers between devices  54.1 us (30%)
  waiting for transfers between devices  28.4 us (16%)
  local copies, waits for them, and re-layouts  9.81 us (5%)
  other arithmetic  8.62 us (5%)
    pallas_call x4, Pallas kernels, weight_grads(): pl.pallas_call(functools.partial(weight_kernel, terms, slabs, halves, qua...  35.1 us
    ppermute x13, starting transfers between devices, swap(): return lax.ppermute(value, axis, [(i, i ^ mask) for i in range(count)])  25.5 us
    ppermute x11, starting transfers between devices, cycle(): lax.ppermute(value, axis, [(i, (i + steps) % count) for i in range(count)])  18.7 us
    pallas_call x3, Pallas kernels, forward(): pl.pallas_call(functools.partial(forward_kernel, branches), grid=(steps,)...  14.8 us
    pallas_call x1, Pallas kernels, depthwise_sums(): pl.pallas_call(lambda s, *refs: kernel(*refs), grid_spec=pltpu.PrefetchSc...  13.3 us
    pallas_call x1, Pallas kernels, feature_grads(): pl.pallas_call(lambda s, *refs: kernel(*refs), grid_spec=pltpu.PrefetchSc...  13.3 us
    ppermute x13, waiting for transfers between devices, swap(): return lax.ppermute(value, axis, [(i, i ^ mask) for i in range(count)])  10.9 us
    ppermute x4, starting transfers between devices, shift(): lax.ppermute(value, axis, [(i, i + steps) for i in range(first, last)])  9.9 us
  transfers between devices with their start and end apart: 28, of which 13 were waited for; matrix products, arithmetic and copies ran while one was open for 6% of the time, Pallas kernels for 29%

profile of v4, /device:TPU:1, one launch (start us, length us, event | category | flops | bytes accessed | tf_op | source)
XLA Modules:
  0.0 180.8 jit_solution(7984381261864125246)
XLA Ops:
  0.6 0.8 copy.14
  1.4 2.2 %collective-permute-start = (bf16[18,512]{1,0:T(8,128)(2,1)S(1)}, bf16[18,512]{1,0:T(8,128)(2,1)S(1)}, u32[]{:S(2)}, u32[]{:S(2)}) collective-permute-start(bf16[18,512]{1,0:T(8,128)(2,1)S(1)} %reshape.32), channel_id=1, source_target_pairs={{0,1},{1,2},{2,3},{3,0},{4,5},{5,6},{6,7},{7,4},{8,9},{9,10},{10,1... | collective-permute-start | bytes 55304 | tf_op jit(solution)/shard_map/ppermute | solution.py:27
  3.6 2.3 %collective-permute-start.1 = (bf16[18,512]{1,0:T(8,128)(2,1)S(1)}, bf16[18,512]{1,0:T(8,128)(2,1)S(1)}, u32[]{:S(2)}, u32[]{:S(2)}) collective-permute-start(bf16[18,512]{1,0:T(8,128)(2,1)S(1)} %reshape.32), channel_id=1, source_target_pairs={{0,2},{1,3},{2,0},{3,1},{4,6},{5,7},{6,4},{7,5},{8,10},{9,11},{10,... | collective-permute-start | bytes 55304 | tf_op jit(solution)/shard_map/ppermute | solution.py:27
  5.9 1.1 collective-permute-start.2
  7.0 0.5 collective-permute-start.3
  7.5 0.7 pad_add_fusion.s.idx_ref
  8.2 2.9 %collective-permute-start.5 = (bf16[2,256,256]{2,1,0:T(8,128)(2,1)S(1)}, bf16[2,256,256]{2,1,0:T(8,128)(2,1)S(1)}, u32[]{:S(2)}, u32[]{:S(2)}) collective-permute-start(bf16[2,256,256]{2,1,0:T(8,128)(2,1)S(1)} %constant_dynamic-slice_fusion), channel_id=1, source_target_pairs={{0,3},{1,0},{2,1},{3,2},{4,7},{5,4},{6,5},{7,6},{8,11},{9,8},{10,9... | collective-permute-start | bytes 786440 | tf_op jit(solution)/shard_map/ppermute | solution.py:27
  11.2 0.2 concatenate.13
  11.4 0.7 pad.4.refs_1_.refs_0_
  12.1 13.3 %depthwise_sums.1 = (bf16[864,2048]{1,0:T(8,128)(2,1)}, bf16[864,2048]{1,0:T(8,128)(2,1)}, bf16[864,2048]{1,0:T(8,128)(2,1)}, bf16[864,2048]{1,0:T(8,128)(2,1)},...) custom-call(s32[7]{0:T(128)} %pad_add_fusion.s.idx_ref, bf16[2,6,72,2048]{3,2,1,0:T(8,128)(2,1)} %refs_0_.1, ...), custom_call_target="tpu_custom_call" | custom-call | flops 53084160 | bytes 24772608 | tf_op jit(solution)/shard_map/depthwise_sums/pallas_call | solution.py:78
  25.4 2.0 %collective-permute-done.4 = bf16[2,256,256]{2,1,0:T(8,128)(2,1)S(1)} collective-permute-done((bf16[2,256,256]{2,1,0:T(8,128)(2,1)S(1)}, bf16[2,256,256]{2,1,0:T(8,128)(2,1)S(1)}, u32[]{:S(2)}, u32[]{:S(2)}) %collective-permute-start.4) | collective-permute-done | bytes 262176 | tf_op jit(solution)/shard_map/ppermute | solution.py:27
  27.5 1.7 collective-permute-start.6
  29.2 2.3 %collective-permute-done.6 = bf16[2,4,256,256]{3,2,0,1:T(8,128)(2,1)S(1)} collective-permute-done((bf16[2,4,256,256]{3,2,0,1:T(8,128)(2,1)S(1)}, bf16[2,4,256,256]{3,2,0,1:T(8,128)(2,1)S(1)}, u32[]{:S(2)}, u32[]{:S(2)}) %collective-permute-start.6) | collective-permute-done | bytes 1048608 | tf_op jit(solution)/shard_map/ppermute | solution.py:32
  31.8 1.5 copy.16
  33.3 3.8 %forward_terms.3 = bf16[864,256]{1,0:T(8,128)(2,1)} custom-call(bf16[2,2048,256]{2,1,0:T(8,128)(2,1)} %bitcast.56, bf16[864,2048]{1,0:T(8,128)(2,1)} %get-tuple-element.86.refs_0_.refs_1_), custom_call_target="tpu_custom_call" | custom-call | flops 905969664 | bytes 4587520 | tf_op jit(solution)/shard_map/forward_terms/pallas_call | solution.py:120
  37.0 1.2 collective-permute-start.9
  38.3 0.9 copy.17
  39.2 0.2 copy.18
  39.6 5.3 %forward_terms.5 = (bf16[864,256]{1,0:T(8,128)(2,1)}, bf16[864,256]{1,0:T(8,128)(2,1)}) custom-call(bf16[2,2048,256]{2,1,0:T(8,128)(2,1)} %bitcast.57, bf16[864,2048]{1,0:T(8,128)(2,1)} %get-tuple-element.73.refs_0_.refs_2_, bf16[864,2048]{1,0:T(8,128)(2,1)} %get-tuple-element.74.refs_1_.refs_3_), custom_call_target="tpu_custom_call" | custom-call | flops 1811939328 | bytes 8126464 | tf_op jit(solution)/shard_map/forward_terms/pallas_call | solution.py:120
  44.9 3.1 %collective-permute-start.7 = (bf16[864,256]{1,0:T(8,128)(2,1)}, bf16[864,256]{1,0:T(8,128)(2,1)S(1)}, u32[]{:S(2)}, u32[]{:S(2)}) collective-permute-start(bf16[864,256]{1,0:T(8,128)(2,1)} %get-tuple-element.75), channel_id=1, source_target_pairs={{0,8},{4,12},{8,16},{12,20},{16,24},{20,28},{1,9},{5,13},{9,17},{1... | collective-permute-start | bytes 1327112 | tf_op jit(solution)/shard_map/ppermute | solution.py:22
  48.1 1.3 collective-permute-start.8
  49.4 5.8 %forward_terms.4 = (f32[864,256]{1,0:T(8,128)}, f32[864,256]{1,0:T(8,128)}) custom-call(bf16[2,2048,256]{2,1,0:T(8,128)(2,1)} %bitcast.58, bf16[864,2048]{1,0:T(8,128)(2,1)} %get-tuple-element.70.refs_0_.refs_1_, bf16[864,2048]{1,0:T(8,128)(2,1)} %get-tuple-element.71.refs_1_), custom_call_target="tpu_custom_call" | custom-call | flops 1811939328 | bytes 8126464 | tf_op jit(solution)/shard_map/forward_terms/pallas_call | solution.py:120
  55.1 1.6 multiply_convert_fusion.3
  56.7 2.0 %collective-permute-start.12 = (bf16[864,256]{1,0:T(8,128)(2,1)S(1)}, bf16[864,256]{1,0:T(8,128)(2,1)}, u32[]{:S(2)}, u32[]{:S(2)}) collective-permute-start(bf16[864,256]{1,0:T(8,128)(2,1)S(1)} %get-tuple-element.100.refs_0_.refs_5_), channel_id=1, source_target_pairs={{0,16},{4,20},{8,24},{12,28},{16,0},{20,4},{24,8},{28,12},{1,17},{... | collective-permute-start | bytes 1327112 | tf_op jit(solution)/shard_map/ppermute | solution.py:27
  58.8 7.7 %weight_middle.2 = (f32[4,256,512]{2,1,0:T(8,128)}, f32[4,32,512]{2,1,0:T(8,128)}) custom-call(s32[7]{0:T(128)} %pad_add_fusion.s.idx_ref, bf16[864,2048]{1,0:T(8,128)(2,1)} %get-tuple-element.77.x_ref, bf16[2,2048,256]{2,1,0:T(8,128)(2,1)} %bitcast.59, bf16[864,256]{1,0:T(8,128)(2,1)} %copy-done.3, bf16[864,2048]{1,0:T(8,128)(2,1)} %get-tuple-element.70.refs_0_.refs_1_), custom_call_target="tpu_custom_call" | custom-call | flops 1811939328 | bytes 10223616 | tf_op jit(solution)/shard_map/weight_middle/pallas_call | solution.py:239
  66.5 1.1 collective-permute-done.8
  67.6 0.8 copy-done.8
  68.4 2.2 %multiply_convert_fusion = (bf16[864,256]{1,0:T(8,128)(2,1)}, bf16[864,256]{1,0:T(8,128)(2,1)S(1)}) fusion(bf16[864,512]{1,0:T(8,128)(2,1)S(1)} %reshape.35, bf16[864,256]{1,0:T(8,128)(2,1)} %copy-done.8, f32[864,256]{1,0:T(8,128)S(1)} %copy-done.5, bf16[864,256]{1,0:T(8,128)(2,1)S(1)} %collective-permute-done.7), kind=kLoop, calls=%fused_computation.7 | loop fusion | flops 3538944 | bytes 3096576 | tf_op jit(solution)/shard_map/convert_element_type | solution.py:462
  70.6 7.7 %weight_middle.3 = (f32[4,256,512]{2,1,0:T(8,128)}, f32[4,32,512]{2,1,0:T(8,128)}) custom-call(s32[7]{0:T(128)} %pad_add_fusion.s.idx_ref, bf16[864,2048]{1,0:T(8,128)(2,1)} %get-tuple-element.77.x_ref, bf16[2,2048,256]{2,1,0:T(8,128)(2,1)} %bitcast.60, bf16[864,256]{1,0:T(8,128)(2,1)} %get-tuple-element.97.refs_0_.refs_2_, ...), custom_call_target="tpu_custom_call" | custom-call | flops 1811939328 | bytes 10223616 | tf_op jit(solution)/shard_map/weight_middle/pallas_call | solution.py:239
  78.3 8.5 %weight_outer.2 = (bf16[4,4,72,256]{3,2,1,0:T(8,128)(2,1)}, bf16[4,4,72,256]{3,2,1,0:T(8,128)(2,1)}) custom-call(s32[7]{0:T(128)} %pad_add_fusion.s.idx_ref, bf16[864,2048]{1,0:T(8,128)(2,1)} %get-tuple-element.77.x_ref, bf16[2,2048,256]{2,1,0:T(8,128)(2,1)} %bitcast.61, bf16[864,256]{1,0:T(8,128)(2,1)} %collective-permute-done.12.refs_0_.refs_6_, ...), custom_call_target="tpu_custom_call" | custom-call | flops 1811939328 | bytes 10223616 | tf_op jit(solution)/shard_map/weight_outer/pallas_call | solution.py:239
  86.8 1.4 collective-permute-start.13
  88.2 1.3 collective-permute-start.10
  89.5 4.2 %collective-permute-start.11 = (bf16[864,256]{1,0:T(8,128)(2,1)S(1)}, bf16[864,256]{1,0:T(8,128)(2,1)S(1)}, u32[]{:S(2)}, u32[]{:S(2)}) collective-permute-start(bf16[864,256]{1,0:T(8,128)(2,1)S(1)} %copy-done.2), channel_id=1, source_target_pairs={{0,8},{4,12},{8,16},{12,20},{16,24},{20,28},{1,9},{5,13},{9,17},{1... | collective-permute-start | bytes 1327112 | tf_op jit(solution)/shard_map/ppermute | solution.py:22
  93.7 1.2 add_convert_fusion.1
  95.0 6.9 %collective-permute-done.10.refs_0_.refs_3_ = bf16[864,256]{1,0:T(8,128)(2,1)S(1)} collective-permute-done((bf16[864,256]{1,0:T(8,128)(2,1)S(1)}, bf16[864,256]{1,0:T(8,128)(2,1)S(1)}, u32[]{:S(2)}, u32[]{:S(2)}) %collective-permute-start.10) | collective-permute-done | bytes 442400 | tf_op jit(solution)/shard_map/ppermute | solution.py:22
  101.8 1.1 collective-permute-done.11.refs_1_.refs_4_
  102.9 0.8 copy-done.7
  103.7 11.3 %weight_outer.3 = (bf16[4,4,72,256]{3,2,1,0:T(8,128)(2,1)}, bf16[4,4,72,256]{3,2,1,0:T(8,128)(2,1)}) custom-call(s32[7]{0:T(128)} %pad_add_fusion.s.idx_ref, bf16[864,2048]{1,0:T(8,128)(2,1)} %get-tuple-element.77.x_ref, bf16[2,2048,256]{2,1,0:T(8,128)(2,1)} %bitcast.62, bf16[864,256]{1,0:T(8,128)(2,1)} %copy-done.6, bf16[864,256]{1,0:T(8,128)(2,1)} %copy-done.7, ...), custom_call_target="tpu_custom_call" | custom-call | flops 3623878656 | bytes 13762560 | tf_op jit(solution)/shard_map/weight_outer/pallas_call | solution.py:239
  114.9 1.2 collective-permute-start.14
  116.2 7.4 %collective-permute-start.18 = (bf16[4,72,256]{2,1,0:T(8,128)(2,1)S(1)}, bf16[4,72,256]{2,1,0:T(8,128)(2,1)S(1)}, u32[]{:S(2)}, u32[]{:S(2)}) collective-permute-start(bf16[4,72,256]{2,1,0:T(8,128)(2,1)S(1)} %get-tuple-element.123), channel_id=1, source_target_pairs={{0,8},{4,12},{8,0},{12,4},{16,24},{20,28},{24,16},{28,20},{1,9},{5... | collective-permute-start | bytes 442376 | tf_op jit(solution)/shard_map/ppermute | solution.py:32
  123.6 3.2 %collective-permute-start.19 = (bf16[4,72,256]{2,1,0:T(8,128)(2,1)S(1)}, bf16[4,72,256]{2,1,0:T(8,128)(2,1)S(1)}, u32[]{:S(2)}, u32[]{:S(2)}) collective-permute-start(bf16[4,72,256]{2,1,0:T(8,128)(2,1)S(1)} %get-tuple-element.125), channel_id=1, source_target_pairs={{0,16},{4,20},{8,24},{12,28},{16,0},{20,4},{24,8},{28,12},{1,17},{... | collective-permute-start | bytes 442376 | tf_op jit(solution)/shard_map/ppermute | solution.py:32
  126.9 1.2 add_convert_fusion
  128.1 1.2 collective-permute-start.15
  129.4 1.5 collective-permute-start.16
  130.8 1.1 collective-permute-start.17
  132.0 0.8 collective-permute-done.19
  132.8 1.1 collective-permute-done.20
  133.9 1.0 collective-permute-done.15
  134.9 4.4 %collective-permute-done.16 = bf16[4,72,256]{2,1,0:T(8,128)(2,1)S(1)} collective-permute-done((bf16[4,72,256]{2,1,0:T(8,128)(2,1)S(1)}, bf16[4,72,256]{2,1,0:T(8,128)(2,1)S(1)}, u32[]{:S(2)}, u32[]{:S(2)}) %collective-permute-start.16) | collective-permute-done | bytes 147488 | tf_op jit(solution)/shard_map/ppermute | solution.py:32
  139.3 1.0 collective-permute-done.17
  140.3 5.7 %collective-permute-start.21 = (bf16[2,72,256]{2,1,0:T(8,128)(2,1)S(1)}, bf16[2,72,256]{2,1,0:T(8,128)(2,1)S(1)}, u32[]{:S(2)}, u32[]{:S(2)}) collective-permute-start(bf16[2,72,256]{2,1,0:T(8,128)(2,1)S(1)} %get-tuple-element.128), channel_id=1, source_target_pairs={{0,3},{1,0},{2,1},{3,2},{4,7},{5,4},{6,5},{7,6},{8,11},{9,8},{10,9... | collective-permute-start | bytes 221192 | tf_op jit(solution)/shard_map/ppermute | solution.py:27
  146.0 0.8 collective-permute-start.22
  146.9 0.6 collective-permute-done.21
  147.4 5.8 %collective-permute-done.22 = bf16[2,72,256]{2,1,0:T(8,128)(2,1)S(1)} collective-permute-done((bf16[2,72,256]{2,1,0:T(8,128)(2,1)S(1)}, bf16[2,72,256]{2,1,0:T(8,128)(2,1)S(1)}, u32[]{:S(2)}, u32[]{:S(2)}) %collective-permute-start.22) | collective-permute-done | bytes 73760 | tf_op jit(solution)/shard_map/ppermute | solution.py:27
  153.3 1.3 collective-permute-start.24
  154.6 1.4 collective-permute-start.26
  156.3 0.9 copy.19
  157.2 1.1 copy.20
  158.2 0.4 collective-permute-done.26
  158.7 4.0 %collective-permute-start.27 = (bf16[4,2,72,256]{3,2,1,0:T(8,128)(2,1)S(1)}, bf16[4,2,72,256]{3,2,1,0:T(8,128)(2,1)S(1)}, u32[]{:S(2)}, u32[]{:S(2)}) collective-permute-start(bf16[4,2,72,256]{3,2,1,0:T(8,128)(2,1)S(1)} %get-tuple-element.127), channel_id=1, source_target_pairs={{0,4},{4,0},{8,12},{12,8},{16,20},{20,16},{24,28},{28,24},{1,5},{5... | collective-permute-start | bytes 884744 | tf_op jit(solution)/shard_map/ppermute | solution.py:32
  162.7 13.3 %feature_grads.1 = bf16[2,6,72,2048]{3,2,1,0:T(8,128)(2,1)} custom-call(s32[7]{0:T(128)} %pad_add_fusion.s.idx_ref, f32[4,16,512]{2,1,0:T(8,128)} %pad.4.refs_1_.refs_0_, bf16[2,2048,256]{2,1,0:T(8,128)(2,1)} %bitcast.63, bf16[864,256]{1,0:T(8,128)(2,1)} %get-tuple-element.97.refs_0_.refs_2_, bf16[864,256]{1,0:T(8,128)(2,1)} %copy-done.6, ...), custom_call_target="tpu_custom_call" | custom-call | flops 4529848320 | bytes 7077888 | tf_op jit(solution)/shard_map/feature_grads/pallas_call | solution.py:291
  176.0 0.9 pad_maximum_fusion.3.in_ref
  176.9 2.4 %finish_grads.1 = (f32[2,512,256]{2,1,0:T(8,128)}, f32[2,9,512]{2,1,0:T(8,128)}) custom-call(s32[7]{0:T(128)} %pad_add_fusion.s.idx_ref, bf16[2,4,2,72,256]{4,3,2,1,0:T(8,128)(2,1)} %pad_maximum_fusion.3.in_ref), custom_call_target="tpu_custom_call" | custom-call | tf_op jit(solution)/shard_map/finish_grads/pallas_call | solution.py:338
  179.3 1.5 copy.21
  (54 shorter events, 1.5 us)
Async XLA Ops:
  0.6 6.4 %copy-start = (bf16[2,512,256]{2,1,0:T(8,128)(2,1)S(1)}, bf16[2,512,256]{2,1,0:T(8,128)(2,1)}, u32[]{:S(2)}) copy-start(bf16[2,512,256]{2,1,0:T(8,128)(2,1)} %param.5) | copy-start | bytes 1572868
  1.4 6.8 %collective-permute-start = (bf16[18,512]{1,0:T(8,128)(2,1)S(1)}, bf16[18,512]{1,0:T(8,128)(2,1)S(1)}, u32[]{:S(2)}, u32[]{:S(2)}) collective-permute-start(bf16[18,512]{1,0:T(8,128)(2,1)S(1)} %reshape.32), channel_id=1, source_target_pairs={{0,1},{1,2},{2,3},{3,0},{4,5},{5,6},{6,7},{7,4},{8,9},{9,10},{10,1... | collective-permute-start | bytes 55304 | tf_op jit(solution)/shard_map/ppermute | solution.py:27
  3.6 7.5 %collective-permute-start.1 = (bf16[18,512]{1,0:T(8,128)(2,1)S(1)}, bf16[18,512]{1,0:T(8,128)(2,1)S(1)}, u32[]{:S(2)}, u32[]{:S(2)}) collective-permute-start(bf16[18,512]{1,0:T(8,128)(2,1)S(1)} %reshape.32), channel_id=1, source_target_pairs={{0,2},{1,3},{2,0},{3,1},{4,6},{5,7},{6,4},{7,5},{8,10},{9,11},{10,... | collective-permute-start | bytes 55304 | tf_op jit(solution)/shard_map/ppermute | solution.py:27
  5.9 5.2 %collective-permute-start.2 = (bf16[18,512]{1,0:T(8,128)(2,1)S(1)}, bf16[18,512]{1,0:T(8,128)(2,1)S(1)}, u32[]{:S(2)}, u32[]{:S(2)}) collective-permute-start(bf16[18,512]{1,0:T(8,128)(2,1)S(1)} %reshape.32), channel_id=1, source_target_pairs={{0,3},{1,0},{2,1},{3,2},{4,7},{5,4},{6,5},{7,6},{8,11},{9,8},{10,9... | collective-permute-start | bytes 55304 | tf_op jit(solution)/shard_map/ppermute | solution.py:27
  7.0 18.4 %collective-permute-start.3 = (bf16[2,256,256]{2,1,0:T(8,128)(2,1)S(1)}, bf16[2,256,256]{2,1,0:T(8,128)(2,1)S(1)}, u32[]{:S(2)}, u32[]{:S(2)}) collective-permute-start(bf16[2,256,256]{2,1,0:T(8,128)(2,1)S(1)} %constant_dynamic-slice_fusion), channel_id=1, source_target_pairs={{0,1},{1,2},{2,3},{3,0},{4,5},{5,6},{6,7},{7,4},{8,9},{9,10},{10,1... | collective-permute-start | bytes 786440 | tf_op jit(solution)/shard_map/ppermute | solution.py:27
  7.5 19.9 %collective-permute-start.4 = (bf16[2,256,256]{2,1,0:T(8,128)(2,1)S(1)}, bf16[2,256,256]{2,1,0:T(8,128)(2,1)S(1)}, u32[]{:S(2)}, u32[]{:S(2)}) collective-permute-start(bf16[2,256,256]{2,1,0:T(8,128)(2,1)S(1)} %constant_dynamic-slice_fusion), channel_id=1, source_target_pairs={{0,2},{1,3},{2,0},{3,1},{4,6},{5,7},{6,4},{7,5},{8,10},{9,11},{10,... | collective-permute-start | bytes 786440 | tf_op jit(solution)/shard_map/ppermute | solution.py:27
  8.2 19.2 %collective-permute-start.5 = (bf16[2,256,256]{2,1,0:T(8,128)(2,1)S(1)}, bf16[2,256,256]{2,1,0:T(8,128)(2,1)S(1)}, u32[]{:S(2)}, u32[]{:S(2)}) collective-permute-start(bf16[2,256,256]{2,1,0:T(8,128)(2,1)S(1)} %constant_dynamic-slice_fusion), channel_id=1, source_target_pairs={{0,3},{1,0},{2,1},{3,2},{4,7},{5,4},{6,5},{7,6},{8,11},{9,8},{10,9... | collective-permute-start | bytes 786440 | tf_op jit(solution)/shard_map/ppermute | solution.py:27
  27.5 3.9 %collective-permute-start.6 = (bf16[2,4,256,256]{3,2,0,1:T(8,128)(2,1)S(1)}, bf16[2,4,256,256]{3,2,0,1:T(8,128)(2,1)S(1)}, u32[]{:S(2)}, u32[]{:S(2)}) collective-permute-start(bf16[2,4,256,256]{3,2,0,1:T(8,128)(2,1)S(1)} %pad_maximum_fusion.1), channel_id=1, source_target_pairs={{0,4},{4,0},{8,12},{12,8},{16,20},{20,16},{24,28},{28,24},{1,5},{5... | collective-permute-start | bytes 3145736 | tf_op jit(solution)/shard_map/ppermute | solution.py:32
  33.3 5.0 %copy-start.4 = (bf16[2,6,72,512]{3,2,1,0:T(8,128)(2,1)S(1)}, bf16[2,6,72,512]{3,2,1,0:T(8,128)(2,1)}, u32[]{:S(2)}) copy-start(bf16[2,6,72,512]{3,2,1,0:T(8,128)(2,1)} %param.7) | copy-start | bytes 2654212
  37.0 18.1 %collective-permute-start.9 = (bf16[864,256]{1,0:T(8,128)(2,1)}, bf16[864,256]{1,0:T(8,128)(2,1)S(1)}, u32[]{:S(2)}, u32[]{:S(2)}) collective-permute-start(bf16[864,256]{1,0:T(8,128)(2,1)} %forward_terms.3), channel_id=1, source_target_pairs={{0,16},{4,20},{8,24},{12,28},{16,0},{20,4},{24,8},{28,12},{1,17},{... | collective-permute-start | bytes 1327112 | tf_op jit(solution)/shard_map/ppermute | solution.py:27
  44.9 21.5 %collective-permute-start.7 = (bf16[864,256]{1,0:T(8,128)(2,1)}, bf16[864,256]{1,0:T(8,128)(2,1)S(1)}, u32[]{:S(2)}, u32[]{:S(2)}) collective-permute-start(bf16[864,256]{1,0:T(8,128)(2,1)} %get-tuple-element.75), channel_id=1, source_target_pairs={{0,8},{4,12},{8,16},{12,20},{16,24},{20,28},{1,9},{5,13},{9,17},{1... | collective-permute-start | bytes 1327112 | tf_op jit(solution)/shard_map/ppermute | solution.py:22
  48.1 19.6 %collective-permute-start.8 = (bf16[864,256]{1,0:T(8,128)(2,1)}, bf16[864,256]{1,0:T(8,128)(2,1)S(1)}, u32[]{:S(2)}, u32[]{:S(2)}) collective-permute-start(bf16[864,256]{1,0:T(8,128)(2,1)} %get-tuple-element.76), channel_id=1, source_target_pairs={{8,0},{12,4},{16,8},{20,12},{24,16},{28,20},{9,1},{13,5},{17,9},{2... | collective-permute-start | bytes 1327112 | tf_op jit(solution)/shard_map/ppermute | solution.py:22
  56.7 2.1 %copy-start.3 = (bf16[864,256]{1,0:T(8,128)(2,1)}, bf16[864,256]{1,0:T(8,128)(2,1)S(1)}, u32[]{:S(2)}) copy-start(bf16[864,256]{1,0:T(8,128)(2,1)S(1)} %get-tuple-element.100.refs_0_.refs_5_) | copy-start | bytes 1327108
  56.7 11.6 %copy-start.5 = (f32[864,256]{1,0:T(8,128)S(1)}, f32[864,256]{1,0:T(8,128)}, u32[]{:S(2)}) copy-start(f32[864,256]{1,0:T(8,128)} %get-tuple-element.72) | copy-start | bytes 2654212
  56.7 21.6 %collective-permute-start.12 = (bf16[864,256]{1,0:T(8,128)(2,1)S(1)}, bf16[864,256]{1,0:T(8,128)(2,1)}, u32[]{:S(2)}, u32[]{:S(2)}) collective-permute-start(bf16[864,256]{1,0:T(8,128)(2,1)S(1)} %get-tuple-element.100.refs_0_.refs_5_), channel_id=1, source_target_pairs={{0,16},{4,20},{8,24},{12,28},{16,0},{20,4},{24,8},{28,12},{1,17},{... | collective-permute-start | bytes 1327112 | tf_op jit(solution)/shard_map/ppermute | solution.py:27
  67.6 0.8 copy-start.8
  78.3 9.9 %copy-start.2 = (bf16[864,256]{1,0:T(8,128)(2,1)S(1)}, bf16[864,256]{1,0:T(8,128)(2,1)}, u32[]{:S(2)}) copy-start(bf16[864,256]{1,0:T(8,128)(2,1)} %get-tuple-element.97.refs_0_.refs_2_) | copy-start | bytes 1327108
  86.8 6.9 %collective-permute-start.13 = (bf16[4,4,72,256]{3,2,1,0:T(8,128)(2,1)}, bf16[4,4,72,256]{3,2,1,0:T(8,128)(2,1)S(1)}, u32[]{:S(2)}, u32[]{:S(2)}) collective-permute-start(bf16[4,4,72,256]{3,2,1,0:T(8,128)(2,1)} %get-tuple-element.90), channel_id=1, source_target_pairs={{0,4},{4,0},{8,12},{12,8},{16,20},{20,16},{24,28},{28,24},{1,5},{5... | collective-permute-start | bytes 1769480 | tf_op jit(solution)/shard_map/ppermute | solution.py:32
  88.2 13.6 %collective-permute-start.10 = (bf16[864,256]{1,0:T(8,128)(2,1)S(1)}, bf16[864,256]{1,0:T(8,128)(2,1)S(1)}, u32[]{:S(2)}, u32[]{:S(2)}) collective-permute-start(bf16[864,256]{1,0:T(8,128)(2,1)S(1)} %copy-done.2), channel_id=1, source_target_pairs={{8,0},{12,4},{16,8},{20,12},{24,16},{28,20},{9,1},{13,5},{17,9},{2... | collective-permute-start | bytes 1327112 | tf_op jit(solution)/shard_map/ppermute | solution.py:22
  89.5 13.4 %collective-permute-start.11 = (bf16[864,256]{1,0:T(8,128)(2,1)S(1)}, bf16[864,256]{1,0:T(8,128)(2,1)S(1)}, u32[]{:S(2)}, u32[]{:S(2)}) collective-permute-start(bf16[864,256]{1,0:T(8,128)(2,1)S(1)} %copy-done.2), channel_id=1, source_target_pairs={{0,8},{4,12},{8,16},{12,20},{16,24},{20,28},{1,9},{5,13},{9,17},{1... | collective-permute-start | bytes 1327112 | tf_op jit(solution)/shard_map/ppermute | solution.py:22
  101.8 1.1 copy-start.6
  102.9 0.8 copy-start.7
  114.9 11.9 %collective-permute-start.14 = (bf16[4,4,72,256]{3,2,1,0:T(8,128)(2,1)}, bf16[4,4,72,256]{3,2,1,0:T(8,128)(2,1)S(1)}, u32[]{:S(2)}, u32[]{:S(2)}) collective-permute-start(bf16[4,4,72,256]{3,2,1,0:T(8,128)(2,1)} %get-tuple-element.96), channel_id=1, source_target_pairs={{0,4},{4,0},{8,12},{12,8},{16,20},{20,16},{24,28},{28,24},{1,5},{5... | collective-permute-start | bytes 1769480 | tf_op jit(solution)/shard_map/ppermute | solution.py:32
  116.2 14.7 %collective-permute-start.18 = (bf16[4,72,256]{2,1,0:T(8,128)(2,1)S(1)}, bf16[4,72,256]{2,1,0:T(8,128)(2,1)S(1)}, u32[]{:S(2)}, u32[]{:S(2)}) collective-permute-start(bf16[4,72,256]{2,1,0:T(8,128)(2,1)S(1)} %get-tuple-element.123), channel_id=1, source_target_pairs={{0,8},{4,12},{8,0},{12,4},{16,24},{20,28},{24,16},{28,20},{1,9},{5... | collective-permute-start | bytes 442376 | tf_op jit(solution)/shard_map/ppermute | solution.py:32
  123.6 9.2 %collective-permute-start.19 = (bf16[4,72,256]{2,1,0:T(8,128)(2,1)S(1)}, bf16[4,72,256]{2,1,0:T(8,128)(2,1)S(1)}, u32[]{:S(2)}, u32[]{:S(2)}) collective-permute-start(bf16[4,72,256]{2,1,0:T(8,128)(2,1)S(1)} %get-tuple-element.125), channel_id=1, source_target_pairs={{0,16},{4,20},{8,24},{12,28},{16,0},{20,4},{24,8},{28,12},{1,17},{... | collective-permute-start | bytes 442376 | tf_op jit(solution)/shard_map/ppermute | solution.py:32
  126.9 7.0 %collective-permute-start.20 = (bf16[4,72,256]{2,1,0:T(8,128)(2,1)S(1)}, bf16[4,72,256]{2,1,0:T(8,128)(2,1)S(1)}, u32[]{:S(2)}, u32[]{:S(2)}) collective-permute-start(bf16[4,72,256]{2,1,0:T(8,128)(2,1)S(1)} %get-tuple-element.124), channel_id=1, source_target_pairs={{0,24},{4,28},{8,16},{12,20},{16,8},{20,12},{24,0},{28,4},{1,25},{... | collective-permute-start | bytes 442376 | tf_op jit(solution)/shard_map/ppermute | solution.py:32
  128.1 6.8 %collective-permute-start.15 = (bf16[4,72,256]{2,1,0:T(8,128)(2,1)S(1)}, bf16[4,72,256]{2,1,0:T(8,128)(2,1)S(1)}, u32[]{:S(2)}, u32[]{:S(2)}) collective-permute-start(bf16[4,72,256]{2,1,0:T(8,128)(2,1)S(1)} %get-tuple-element.120), channel_id=1, source_target_pairs={{0,8},{4,12},{8,0},{12,4},{16,24},{20,28},{24,16},{28,20},{1,9},{5... | collective-permute-start | bytes 442376 | tf_op jit(solution)/shard_map/ppermute | solution.py:32
  129.4 9.9 %collective-permute-start.16 = (bf16[4,72,256]{2,1,0:T(8,128)(2,1)S(1)}, bf16[4,72,256]{2,1,0:T(8,128)(2,1)S(1)}, u32[]{:S(2)}, u32[]{:S(2)}) collective-permute-start(bf16[4,72,256]{2,1,0:T(8,128)(2,1)S(1)} %get-tuple-element.122), channel_id=1, source_target_pairs={{0,16},{4,20},{8,24},{12,28},{16,0},{20,4},{24,8},{28,12},{1,17},{... | collective-permute-start | bytes 442376 | tf_op jit(solution)/shard_map/ppermute | solution.py:32
  130.8 9.4 %collective-permute-start.17 = (bf16[4,72,256]{2,1,0:T(8,128)(2,1)S(1)}, bf16[4,72,256]{2,1,0:T(8,128)(2,1)S(1)}, u32[]{:S(2)}, u32[]{:S(2)}) collective-permute-start(bf16[4,72,256]{2,1,0:T(8,128)(2,1)S(1)} %get-tuple-element.121), channel_id=1, source_target_pairs={{0,24},{4,28},{8,16},{12,20},{16,8},{20,12},{24,0},{28,4},{1,25},{... | collective-permute-start | bytes 442376 | tf_op jit(solution)/shard_map/ppermute | solution.py:32
  140.3 7.1 %collective-permute-start.21 = (bf16[2,72,256]{2,1,0:T(8,128)(2,1)S(1)}, bf16[2,72,256]{2,1,0:T(8,128)(2,1)S(1)}, u32[]{:S(2)}, u32[]{:S(2)}) collective-permute-start(bf16[2,72,256]{2,1,0:T(8,128)(2,1)S(1)} %get-tuple-element.128), channel_id=1, source_target_pairs={{0,3},{1,0},{2,1},{3,2},{4,7},{5,4},{6,5},{7,6},{8,11},{9,8},{10,9... | collective-permute-start | bytes 221192 | tf_op jit(solution)/shard_map/ppermute | solution.py:27
  146.0 7.2 %collective-permute-start.22 = (bf16[2,72,256]{2,1,0:T(8,128)(2,1)S(1)}, bf16[2,72,256]{2,1,0:T(8,128)(2,1)S(1)}, u32[]{:S(2)}, u32[]{:S(2)}) collective-permute-start(bf16[2,72,256]{2,1,0:T(8,128)(2,1)S(1)} %get-tuple-element.130), channel_id=1, source_target_pairs={{0,2},{1,3},{2,0},{3,1},{4,6},{5,7},{6,4},{7,5},{8,10},{9,11},{10,... | collective-permute-start | bytes 221192 | tf_op jit(solution)/shard_map/ppermute | solution.py:27
  146.9 6.4 %collective-permute-start.23 = (bf16[2,72,256]{2,1,0:T(8,128)(2,1)S(1)}, bf16[2,72,256]{2,1,0:T(8,128)(2,1)S(1)}, u32[]{:S(2)}, u32[]{:S(2)}) collective-permute-start(bf16[2,72,256]{2,1,0:T(8,128)(2,1)S(1)} %get-tuple-element.129), channel_id=1, source_target_pairs={{0,1},{1,2},{2,3},{3,0},{4,5},{5,6},{6,7},{7,4},{8,9},{9,10},{10,1... | collective-permute-start | bytes 221192 | tf_op jit(solution)/shard_map/ppermute | solution.py:27
  153.3 5.0 %collective-permute-start.24 = (bf16[2,72,256]{2,1,0:T(8,128)(2,1)S(1)}, bf16[2,72,256]{2,1,0:T(8,128)(2,1)S(1)}, u32[]{:S(2)}, u32[]{:S(2)}) collective-permute-start(bf16[2,72,256]{2,1,0:T(8,128)(2,1)S(1)} %fusion.10), channel_id=1, source_target_pairs={{0,8},{4,12},{8,0},{12,4},{16,24},{20,28},{24,16},{28,20},{1,9},{5... | collective-permute-start | bytes 221192 | tf_op jit(solution)/shard_map/ppermute | solution.py:32
  154.6 3.7 %collective-permute-start.25 = (bf16[2,72,256]{2,1,0:T(8,128)(2,1)S(1)}, bf16[2,72,256]{2,1,0:T(8,128)(2,1)S(1)}, u32[]{:S(2)}, u32[]{:S(2)}) collective-permute-start(bf16[2,72,256]{2,1,0:T(8,128)(2,1)S(1)} %fusion.10), channel_id=1, source_target_pairs={{0,16},{4,20},{8,24},{12,28},{16,0},{20,4},{24,8},{28,12},{1,17},{... | collective-permute-start | bytes 221192 | tf_op jit(solution)/shard_map/ppermute | solution.py:32
  154.6 4.1 %collective-permute-start.26 = (bf16[2,72,256]{2,1,0:T(8,128)(2,1)S(1)}, bf16[2,72,256]{2,1,0:T(8,128)(2,1)S(1)}, u32[]{:S(2)}, u32[]{:S(2)}) collective-permute-start(bf16[2,72,256]{2,1,0:T(8,128)(2,1)S(1)} %fusion.10), channel_id=1, source_target_pairs={{0,24},{4,28},{8,16},{12,20},{16,8},{20,12},{24,0},{28,4},{1,25},{... | collective-permute-start | bytes 221192 | tf_op jit(solution)/shard_map/ppermute | solution.py:32
  158.7 17.3 %collective-permute-start.27 = (bf16[4,2,72,256]{3,2,1,0:T(8,128)(2,1)S(1)}, bf16[4,2,72,256]{3,2,1,0:T(8,128)(2,1)S(1)}, u32[]{:S(2)}, u32[]{:S(2)}) collective-permute-start(bf16[4,2,72,256]{3,2,1,0:T(8,128)(2,1)S(1)} %get-tuple-element.127), channel_id=1, source_target_pairs={{0,4},{4,0},{8,12},{12,8},{16,20},{20,16},{24,28},{28,24},{1,5},{5... | collective-permute-start | bytes 884744 | tf_op jit(solution)/shard_map/ppermute | solution.py:32
  162.7 18.0 %copy-start.1 = (bf16[2,512,256]{2,1,0:T(8,128)(2,1)S(1)}, bf16[2,512,256]{2,1,0:T(8,128)(2,1)}, u32[]{:S(2)}) copy-start(bf16[2,512,256]{2,1,0:T(8,128)(2,1)} %param.5) | copy-start | bytes 1572868
